TPU v7x, 32 devices: a whole 2x2x4 slice. The times are simulated.
32 devices in a mesh: fsdp: 16 (over z, y, core), tp: 2 (over x).
Axes of the slice: x: 2, y: 2, z: 4, core: 2. Of those that a mesh axis runs over, the one named last changes fastest.
Arguments:
- layer_in: bfloat16 [32, 1024, 1024], P('fsdp', 'tp'), may hold values from -6 to 6
- memory: bfloat16 [32, 1024, 1024], P('fsdp', 'tp'), may hold values from -6 to 6
- out_grad: bfloat16 [32, 1024, 1024], P('fsdp', 'tp'), may hold values from -6 to 6
- w_self_in: bfloat16 [1024, 3, 1024], P('fsdp', None, 'tp'), may hold values from -1 to 1
- w_self_out: bfloat16 [1024, 1024], P('tp', 'fsdp'), may hold values from -1 to 1
- w_cross_in: bfloat16 [1024, 3, 1024], P('fsdp', None, 'tp'), may hold values from -1 to 1
- w_cross_out: bfloat16 [1024, 1024], P('tp', 'fsdp'), may hold values from -1 to 1
- w_up: bfloat16 [1024, 4096], P('fsdp', 'tp'), may hold values from -0.1875 to 0.1875
- w_down: bfloat16 [4096, 1024], P('tp', 'fsdp'), may hold values from -0.125 to 0.125
- head_bias: bfloat16 [4, 1024], P(None, 'tp'), may hold values from -3 to 3
- up_bias: bfloat16 [4096], P('tp'), may hold values from -3 to 3
- norm_gain: bfloat16 [3, 1024], replicated, may hold values from 0.5 to 1.5
- row_bias: bfloat16 [6, 1024], replicated, may hold values from -2 to 2
Outputs:
- mixed: bfloat16 [32, 1024, 1024], P('fsdp', 'tp')
- d_layer_in: bfloat16 [32, 1024, 1024], P('fsdp', 'tp')
- d_memory: bfloat16 [32, 1024, 1024], P('fsdp', 'tp')
- d_self_in: float32 [1024, 3, 1024], P('fsdp', None, 'tp')
- d_self_out: float32 [1024, 1024], P('tp', 'fsdp')
- d_cross_in: float32 [1024, 3, 1024], P('fsdp', None, 'tp')
- d_cross_out: float32 [1024, 1024], P('tp', 'fsdp')
- d_up: float32 [1024, 4096], P('fsdp', 'tp')
- d_down: float32 [4096, 1024], P('tp', 'fsdp')
- d_head_bias: float32 [4, 1024], P(None, 'tp')
- d_up_bias: float32 [4096], P('tp')
- d_norm_gain: float32 [3, 1024], replicated
- d_row_bias: float32 [6, 1024], replicated
All inputs are finite; a program needn't handle non-finite values.
Results may differ from a plain program's by a relative error of at most 0.035.
Values may be sent and summed in bfloat16 or wider, within the bound.
A program may use at most 256 MiB of HBM per device.

v0:
```python
import jax
import jax.numpy as jnp
from jax import lax
from jax.sharding import PartitionSpec as P

HD = 64


NORM_EPS = 1e-05
ATT_SCALE = 0.125


def times_back(left, right):
    return lax.dot_general(
        left, right, (((1,), (1,)), ((), ())), preferred_element_type=jnp.float32
    )


def over_rows(left, right):
    return lax.dot_general(
        left, right, (((0,), (0,)), ((), ())), preferred_element_type=jnp.float32
    )


def whole_rows(piece):
    return lax.all_gather(piece, "tp", axis=1, tiled=True)


def whole_grads(piece):
    return lax.all_gather(piece, "tp", axis=1, tiled=True)


def branch_sum(term):
    return lax.psum_scatter(
        term.astype(jnp.bfloat16), "tp", scatter_dimension=1, tiled=True
    ).astype(jnp.float32)


def piece_sum(term):
    return lax.psum_scatter(
        term.astype(jnp.bfloat16), "tp", scatter_dimension=1, tiled=True
    ).astype(jnp.float32)


def norm_forward(resid, gain, shift):
    center = resid - jnp.mean(resid, -1, keepdims=True)
    spread = jnp.mean(center * center, -1, keepdims=True)
    inv_std = lax.rsqrt(spread + NORM_EPS)
    normed = center * inv_std
    return (normed * gain + shift, normed, inv_std)


def norm_backward(grad_out, normed, inv_std, gain):
    grad_normed = grad_out * gain
    grad_resid = inv_std * (
        grad_normed
        - jnp.mean(grad_normed, -1, keepdims=True)
        - normed * jnp.mean(grad_normed * normed, -1, keepdims=True)
    )
    return (grad_resid, jnp.sum(grad_out * normed, (0, 1)), jnp.sum(grad_out, (0, 1)))


def gelu_exact(pre_act):
    return jax.nn.gelu(pre_act, approximate=False)


def gelu_back(pre_act, grad_act):
    unused_out, pull_back = jax.vjp(gelu_exact, pre_act)
    return pull_back(grad_act)[0]


def masked_scores(query_blk, block_start, keys_seq, causal):
    scores = jnp.einsum("qhc,khc->hqk", query_blk, keys_seq, preferred_element_type=jnp.float32)
    if causal:
        row_pos = block_start + lax.broadcasted_iota(jnp.int32, scores.shape[1:], 0)
        col_pos = lax.broadcasted_iota(jnp.int32, scores.shape[1:], 1)
        scores = jnp.where(row_pos >= col_pos, scores, -1e30)
    return scores


def attend_forward(query, keys, values, causal):
    seq_count, length, heads_dev, depth = query.shape
    block_rows = min(512, length)
    block_count = length // block_rows
    block_starts = jnp.arange(block_count, dtype=jnp.int32) * block_rows

    def one_sequence(seq_item):
        query_seq, keys_seq, values_seq = seq_item

        def one_block(blk_item):
            query_blk, block_start = blk_item
            scores = masked_scores(query_blk, block_start, keys_seq, causal)
            row_max = jnp.max(scores, -1, keepdims=True)
            log_total = row_max + jnp.log(jnp.sum(jnp.exp(scores - row_max), -1, keepdims=True))
            probs = jnp.exp(scores - log_total).astype(jnp.bfloat16)
            block_out = jnp.einsum(
                "hqk,khc->qhc", probs, values_seq, preferred_element_type=jnp.float32
            )
            return (block_out.astype(jnp.bfloat16), log_total)

        block_outs, log_totals = lax.map(
            one_block, (query_seq.reshape(block_count, block_rows, heads_dev, depth), block_starts)
        )
        return (block_outs.reshape(length, heads_dev, depth), log_totals)

    return lax.map(one_sequence, (query, keys, values))


def attend_backward(query, keys, values, log_totals, grad_out, causal):
    seq_count, length, heads_dev, depth = query.shape
    block_rows = min(512, length)
    block_count = length // block_rows
    block_starts = jnp.arange(block_count, dtype=jnp.int32) * block_rows

    def one_sequence(seq_item):
        query_seq, keys_seq, values_seq, total_seq, grad_seq = seq_item

        def one_block(carry, blk_item):
            query_blk, grad_blk, total_blk, block_start = blk_item
            probs = jnp.exp(masked_scores(query_blk, block_start, keys_seq, causal) - total_blk)
            grad_probs = jnp.einsum(
                "qhc,khc->hqk", grad_blk, values_seq, preferred_element_type=jnp.float32
            )
            row_delta = jnp.sum(probs * grad_probs, -1, keepdims=True)
            grad_scores = (probs * (grad_probs - row_delta)).astype(jnp.bfloat16)
            grad_query = jnp.einsum(
                "hqk,khc->qhc", grad_scores, keys_seq, preferred_element_type=jnp.float32
            )
            grad_keys = carry[0] + jnp.einsum(
                "hqk,qhc->khc", grad_scores, query_blk, preferred_element_type=jnp.float32
            )
            grad_values = carry[1] + jnp.einsum(
                "hqk,qhc->khc",
                probs.astype(jnp.bfloat16),
                grad_blk,
                preferred_element_type=jnp.float32,
            )
            return ((grad_keys, grad_values), grad_query)

        zero_keys = jnp.zeros(keys_seq.shape, jnp.float32)
        blk_items = (
            query_seq.reshape(block_count, block_rows, heads_dev, depth),
            grad_seq.reshape(block_count, block_rows, heads_dev, depth),
            total_seq,
            block_starts,
        )
        (grad_keys, grad_values), grad_query = lax.scan(
            one_block, (zero_keys, zero_keys), blk_items
        )
        return (grad_query.reshape(length, heads_dev, depth), grad_keys, grad_values)

    return lax.map(one_sequence, (query, keys, values, log_totals, grad_out))


def on_device(
    layer_in,
    memory,
    out_grad,
    w_self_in,
    w_self_out,
    w_cross_in,
    w_cross_out,
    w_up,
    w_down,
    head_bias,
    up_bias,
    norm_gain,
    row_bias,
):
    seq_count, piece_len, model_width = layer_in.shape
    head_cols = w_self_in.shape[2]
    unit_cols = w_up.shape[1]
    heads_dev = head_cols // HD
    tp_place = lax.axis_index("tp")
    tp_count = lax.axis_size("tp")
    zero_index = jnp.zeros((), jnp.int32)
    gains = norm_gain.astype(jnp.float32)
    shifts = row_bias.astype(jnp.float32)
    col_bias = head_bias.astype(jnp.float32)
    unit_bias = up_bias.astype(jnp.float32)
    self_in, self_out, cross_in, cross_out, up_full, down_full = (
        lax.all_gather(w_self_in, "fsdp", axis=0, tiled=True),
        lax.all_gather(w_self_out, "fsdp", axis=1, tiled=True),
        lax.all_gather(w_cross_in, "fsdp", axis=0, tiled=True),
        lax.all_gather(w_cross_out, "fsdp", axis=1, tiled=True),
        lax.all_gather(w_up, "fsdp", axis=0, tiled=True),
        lax.all_gather(w_down, "fsdp", axis=1, tiled=True),
    )
    layer_whole = whole_rows(layer_in)
    length = layer_whole.shape[1]
    row_count = seq_count * length
    token_rows = layer_whole.reshape(row_count, model_width)
    self_proj = jnp.einsum("rd,dkc->rkc", token_rows, self_in, preferred_element_type=jnp.float32)
    self_query = ((self_proj[:, 0] + col_bias[0]) * ATT_SCALE).astype(jnp.bfloat16)
    self_keys = self_proj[:, 1].astype(jnp.bfloat16)
    self_values = (self_proj[:, 2] + col_bias[1]).astype(jnp.bfloat16)
    head_shape = (seq_count, length, heads_dev, HD)
    self_att, self_totals = attend_forward(
        self_query.reshape(head_shape),
        self_keys.reshape(head_shape),
        self_values.reshape(head_shape),
        True,
    )
    self_rows = self_att.reshape(row_count, head_cols)
    self_term = jnp.dot(self_rows, self_out, preferred_element_type=jnp.float32).reshape(
        seq_count, length, model_width
    )
    resid_one = layer_in.astype(jnp.float32) + branch_sum(self_term) + shifts[0]
    normed_one, unit_one, inv_one = norm_forward(resid_one, gains[0], shifts[3])
    normed_rows = whole_rows(normed_one.astype(jnp.bfloat16)).reshape(row_count, model_width)
    cross_query = (
        (jnp.dot(normed_rows, cross_in[:, 0], preferred_element_type=jnp.float32) + col_bias[2])
        * ATT_SCALE
    ).astype(jnp.bfloat16)
    memory_whole = lax.all_gather(memory, "tp", axis=1, tiled=True)
    source_len = memory_whole.shape[1]
    source_rows = memory_whole.reshape(seq_count * source_len, model_width)
    cross_proj = jnp.einsum(
        "rd,dkc->rkc", source_rows, cross_in[:, 1:], preferred_element_type=jnp.float32
    )
    cross_keys = cross_proj[:, 0].astype(jnp.bfloat16)
    cross_values = (cross_proj[:, 1] + col_bias[3]).astype(jnp.bfloat16)
    source_shape = (seq_count, source_len, heads_dev, HD)
    cross_att, cross_totals = attend_forward(
        cross_query.reshape(head_shape),
        cross_keys.reshape(source_shape),
        cross_values.reshape(source_shape),
        False,
    )
    cross_rows = cross_att.reshape(row_count, head_cols)
    cross_term = jnp.dot(cross_rows, cross_out, preferred_element_type=jnp.float32).reshape(
        seq_count, length, model_width
    )
    resid_two = normed_one + branch_sum(cross_term) + shifts[1]
    normed_two, unit_two, inv_two = norm_forward(resid_two, gains[1], shifts[4])
    normed_two_low = normed_two.astype(jnp.bfloat16)
    ffn_rows = whole_rows(normed_two_low).reshape(row_count, model_width)
    pre_act = jnp.dot(ffn_rows, up_full, preferred_element_type=jnp.float32) + unit_bias
    hidden_act = gelu_exact(pre_act).astype(jnp.bfloat16)
    ffn_term = jnp.dot(hidden_act, down_full, preferred_element_type=jnp.float32).reshape(
        seq_count, length, model_width
    )
    ffn_out = branch_sum(ffn_term)
    resid_three = normed_two + ffn_out + shifts[2]
    mixed, unit_three, inv_three = norm_forward(resid_three, gains[2], shifts[5])
    grad_three, gain_grad_three, shift_grad_three = norm_backward(
        out_grad.astype(jnp.float32), unit_three, inv_three, gains[2]
    )
    bias_grad_three = jnp.sum(grad_three, (0, 1))
    grad_three_low = grad_three.astype(jnp.bfloat16)
    grad_rows = whole_grads(grad_three_low).reshape(row_count, model_width)
    grad_act = times_back(grad_rows, down_full)
    grad_pre = gelu_back(pre_act, grad_act).astype(jnp.bfloat16)
    d_up = over_rows(ffn_rows, grad_pre)
    d_down = over_rows(hidden_act, grad_rows)
    unit_grad = jnp.sum(grad_pre, 0, dtype=jnp.float32)
    grad_two_in = piece_sum(times_back(grad_pre, up_full).reshape(seq_count, length, model_width))
    grad_normed_two = grad_three + grad_two_in
    grad_two, gain_grad_two, shift_grad_two = norm_backward(
        grad_normed_two, unit_two, inv_two, gains[1]
    )
    bias_grad_two = jnp.sum(grad_two, (0, 1))
    grad_two_rows = whole_grads(grad_two.astype(jnp.bfloat16)).reshape(row_count, model_width)
    d_cross_out = over_rows(cross_rows, grad_two_rows)
    grad_cross_att = times_back(grad_two_rows, cross_out).astype(jnp.bfloat16)
    cq_grad, ck_grad, cv_grad = attend_backward(
        cross_query.reshape(head_shape),
        cross_keys.reshape(source_shape),
        cross_values.reshape(source_shape),
        cross_totals,
        grad_cross_att.reshape(head_shape),
        False,
    )
    cq_pre = cq_grad.reshape(row_count, head_cols).astype(jnp.bfloat16) * jnp.asarray(
        ATT_SCALE, jnp.bfloat16
    )
    ckv_low = jnp.stack(
        [
            ck_grad.reshape(seq_count * source_len, head_cols),
            cv_grad.reshape(seq_count * source_len, head_cols),
        ],
        1,
    ).astype(jnp.bfloat16)
    cross_q_grad = over_rows(normed_rows, cq_pre)
    cq_bias_grad = jnp.sum(cq_pre, 0, dtype=jnp.float32)
    normed_part = times_back(cq_pre, cross_in[:, 0]).reshape(seq_count, length, model_width)
    source_part = jnp.einsum(
        "rkc,dkc->rd", ckv_low, cross_in[:, 1:], preferred_element_type=jnp.float32
    ).reshape(seq_count, source_len, model_width)
    grad_one_in, memory_grad = (
        lax.psum_scatter(
            normed_part.astype(jnp.bfloat16), "tp", scatter_dimension=1, tiled=True
        ).astype(jnp.float32),
        lax.psum_scatter(
            source_part.astype(jnp.bfloat16), "tp", scatter_dimension=1, tiled=True
        ).astype(jnp.float32),
    )
    d_memory = memory_grad.astype(jnp.bfloat16)
    cross_kv_grad = jnp.einsum(
        "rd,rkc->dkc", source_rows, ckv_low, preferred_element_type=jnp.float32
    )
    cross_grad_term = jnp.concatenate([cross_q_grad[:, None, :], cross_kv_grad], 1)
    cv_own = jnp.sum(ckv_low[:, 1], 0, dtype=jnp.float32)
    cv_wide = lax.dynamic_update_slice(
        jnp.zeros((head_cols * tp_count,), jnp.float32), cv_own, (tp_place * head_cols,)
    )
    grad_normed_one = grad_two + grad_one_in
    grad_one, gain_grad_one, shift_grad_one = norm_backward(
        grad_normed_one, unit_one, inv_one, gains[0]
    )
    bias_grad_one = jnp.sum(grad_one, (0, 1))
    grad_one_rows = whole_grads(grad_one.astype(jnp.bfloat16)).reshape(row_count, model_width)
    d_self_out = over_rows(self_rows, grad_one_rows)
    grad_self_att = times_back(grad_one_rows, self_out).astype(jnp.bfloat16)
    sq_grad, sk_grad, sv_grad = attend_backward(
        self_query.reshape(head_shape),
        self_keys.reshape(head_shape),
        self_values.reshape(head_shape),
        self_totals,
        grad_self_att.reshape(head_shape),
        True,
    )
    sq_pre = sq_grad.reshape(row_count, head_cols).astype(jnp.bfloat16) * jnp.asarray(
        ATT_SCALE, jnp.bfloat16
    )
    sqkv_low = jnp.stack(
        [
            sq_pre,
            sk_grad.reshape(row_count, head_cols).astype(jnp.bfloat16),
            sv_grad.reshape(row_count, head_cols).astype(jnp.bfloat16),
        ],
        1,
    )
    d_self_in = jnp.einsum("rd,rkc->dkc", token_rows, sqkv_low, preferred_element_type=jnp.float32)
    sq_bias_grad = jnp.sum(sq_pre, 0, dtype=jnp.float32)
    sv_bias_grad = jnp.sum(sqkv_low[:, 2], 0, dtype=jnp.float32)
    layer_part = jnp.einsum(
        "rkc,dkc->rd", sqkv_low, self_in, preferred_element_type=jnp.float32
    ).reshape(seq_count, length, model_width)
    d_layer_in = (grad_one + piece_sum(layer_part)).astype(jnp.bfloat16)
    slot_grad = jnp.stack([sq_bias_grad, sv_bias_grad, cq_bias_grad])
    slot_wide = lax.dynamic_update_slice(
        jnp.zeros((3, head_cols * tp_count), jnp.float32),
        slot_grad,
        (zero_index, tp_place * head_cols),
    )
    head_wide = jnp.concatenate([slot_wide, cv_wide[None, :]], 0)
    unit_wide_grad = lax.dynamic_update_slice(
        jnp.zeros((unit_cols * tp_count,), jnp.float32), unit_grad, (tp_place * unit_cols,)
    )
    gain_grads = jnp.stack([gain_grad_one, gain_grad_two, gain_grad_three])
    shift_grads = jnp.stack(
        [
            bias_grad_one,
            bias_grad_two,
            bias_grad_three,
            shift_grad_one,
            shift_grad_two,
            shift_grad_three,
        ]
    )
    gain_total, shift_total, head_total, unit_total = lax.psum(
        (gain_grads, shift_grads, head_wide, unit_wide_grad), ("fsdp", "tp")
    )
    d_head_bias = lax.dynamic_slice(head_total, (zero_index, tp_place * head_cols), (4, head_cols))
    d_up_bias = lax.dynamic_slice(unit_total, (tp_place * unit_cols,), (unit_cols,))
    g_self_in, g_self_out, g_cross_part, g_cross_out, g_up, g_down = (
        lax.psum_scatter(
            d_self_in.astype(jnp.bfloat16), "fsdp", scatter_dimension=0, tiled=True
        ).astype(jnp.float32),
        lax.psum_scatter(
            d_self_out.astype(jnp.bfloat16), "fsdp", scatter_dimension=1, tiled=True
        ).astype(jnp.float32),
        lax.psum_scatter(
            cross_grad_term.astype(jnp.bfloat16), "fsdp", scatter_dimension=0, tiled=True
        ).astype(jnp.float32),
        lax.psum_scatter(
            d_cross_out.astype(jnp.bfloat16), "fsdp", scatter_dimension=1, tiled=True
        ).astype(jnp.float32),
        lax.psum_scatter(d_up.astype(jnp.bfloat16), "fsdp", scatter_dimension=0, tiled=True).astype(
            jnp.float32
        ),
        lax.psum_scatter(
            d_down.astype(jnp.bfloat16), "fsdp", scatter_dimension=1, tiled=True
        ).astype(jnp.float32),
    )
    return (
        mixed.astype(jnp.bfloat16),
        d_layer_in,
        d_memory,
        g_self_in,
        g_self_out,
        g_cross_part,
        g_cross_out,
        g_up,
        g_down,
        d_head_bias,
        d_up_bias,
        gain_total,
        shift_total,
    )


def solution(mesh):
    return jax.shard_map(
        on_device,
        mesh=mesh,
        in_specs=(
            P("fsdp", "tp", None),
            P("fsdp", "tp", None),
            P("fsdp", "tp", None),
            P("fsdp", None, "tp"),
            P("tp", "fsdp"),
            P("fsdp", None, "tp"),
            P("tp", "fsdp"),
            P("fsdp", "tp"),
            P("tp", "fsdp"),
            P(None, "tp"),
            P("tp"),
            P(),
            P(),
        ),
        out_specs=(
            P("fsdp", "tp", None),
            P("fsdp", "tp", None),
            P("fsdp", "tp", None),
            P("fsdp", None, "tp"),
            P("tp", "fsdp"),
            P("fsdp", None, "tp"),
            P("tp", "fsdp"),
            P("fsdp", "tp"),
            P("tp", "fsdp"),
            P(None, "tp"),
            P("tp"),
            P(),
            P(),
        ),
        check_vma=False,
    )
```

profile of v0, /device:TPU:0, one launch (start us, length us, event | category | flops | bytes accessed | tf_op | source)
XLA Modules:
  0.0 2256.1 jit_solution(16151405634365936579)
XLA Ops:
  10.9 58.1 %all-gather.14.cloned.1.call-done = bf16[2,1024,1024]{2,1,0:T(8,128)(2,1)} async-done(((bf16[2,512,1024]{2,1,0:T(8,128)(2,1)}), bf16[2,1024,1024]{2,1,0:T(8,128)(2,1)}) %all-gather.14.cloned.1.call-update) | async-done | bytes 4194320 | tf_op jit(solution)/shard_map/all_gather | solution.py:26
  69.0 47.7 %all-gather.16.cloned.1.call-done = bf16[1024,3,512]{2,0,1:T(8,128)(2,1)} async-done(((bf16[64,3,512]{2,0,1:T(8,128)(2,1)}), bf16[1024,3,512]{2,0,1:T(8,128)(2,1)}) %all-gather.16.cloned.1.call-update) | async-done | bytes 3145744 | tf_op jit(solution)/shard_map/all_gather | solution.py:182
  116.7 9.4 fusion.110
  178.8 71.9 %while.115 = (s32[]{:T(128)}, bf16[2,1024,8,64]{3,2,1,0:T(8,128)(2,1)}, f32[2,2,8,512,1]{3,2,1,4,0:T(8,128)}, bf16[2,1024,8,64]{1,3,2,0:T(8,128)(2,1)}, bf16[2,1...) while((s32[]{:T(128)}, ...), condition=%wide.region_5.6_spmd.clone, body=%wide.region_0.5_spmd.clone.sunk | while | flops 1108079104 | bytes 79892848 | solution.py:106
  183.2 26.9 %while.120 = (s32[]{:T(128)}, bf16[2,512,8,64]{1,3,2,0:T(8,128)(2,1)}, f32[2,8,512,1]{2,1,3,0:T(8,128)S(1)}, s32[2]{0:T(128)S(1)}, bf16[2,512,8,64]{1,3,2,0:T(8,...) while((s32[]{:T(128)}, ...), condition=%wide.region_4.4_spmd, body=%wide.region_1.3_spmd.sunk | while | flops 1108079104 | bytes 64098480 | solution.py:101
  219.0 26.9 %while.120 = (s32[]{:T(128)}, bf16[2,512,8,64]{1,3,2,0:T(8,128)(2,1)}, f32[2,8,512,1]{2,1,3,0:T(8,128)S(1)}, s32[2]{0:T(128)S(1)}, bf16[2,512,8,64]{1,3,2,0:T(8,...) while((s32[]{:T(128)}, ...), condition=%wide.region_4.4_spmd, body=%wide.region_1.3_spmd.sunk | while | flops 1108079104 | bytes 64098480 | solution.py:101
  263.3 50.6 %reduce-scatter.12.cloned.1.call-done = bf16[2,512,1024]{2,1,0:T(8,128)(2,1)} async-done(((bf16[2,1024,1024]{2,1,0:T(8,128)(2,1)}), bf16[2,512,1024]{2,1,0:T(8,128)(2,1)}) %reduce-scatter.12.cloned.1.call-update) | async-done | bytes 2097168 | tf_op jit(solution)/shard_map/reduce_scatter | solution.py:34
  321.7 50.4 %all-gather.24.cloned.1.call-done = bf16[2,1024,1024]{2,1,0:T(8,128)(2,1)} async-done(((bf16[2,512,1024]{2,1,0:T(8,128)(2,1)}), bf16[2,1024,1024]{2,1,0:T(8,128)(2,1)}) %all-gather.24.cloned.1.call-update) | async-done | bytes 4194320 | tf_op jit(solution)/shard_map/all_gather | solution.py:215
  372.0 47.6 %all-gather.22.cloned.1.call-done = bf16[1024,3,512]{2,0,1:T(8,128)(2,1)} async-done(((bf16[64,3,512]{2,0,1:T(8,128)(2,1)}), bf16[1024,3,512]{2,0,1:T(8,128)(2,1)}) %all-gather.22.cloned.1.call-update) | async-done | bytes 3145744 | tf_op jit(solution)/shard_map/all_gather | solution.py:184
  456.3 20.5 all-gather.20.cloned.1.call-done
  493.9 88.2 %while.111 = (s32[]{:T(128)}, bf16[2,1024,8,64]{3,2,1,0:T(8,128)(2,1)}, f32[2,2,8,512,1]{3,2,1,4,0:T(8,128)}, bf16[2,1024,8,64]{1,3,2,0:T(8,128)(2,1)}, bf16[2,1...) while((s32[]{:T(128)}, ...), condition=%wide.region_14.15_spmd, body=%wide.region_9.14_spmd.sunk | while | flops 1094971392 | bytes 136511792 | solution.py:106
  498.3 35.2 %while.118 = (s32[]{:T(128)}, bf16[2,512,8,64]{1,3,2,0:T(8,128)(2,1)}, f32[2,8,512,1]{2,1,3,0:T(8,128)S(1)}, bf16[2,512,8,64]{1,3,2,0:T(8,128)(2,1)S(1)}, bf16[1...) while((s32[]{:T(128)}, bf16[2,512,8,64]{1,3,2,0:T(8,128)(2,1)}, ...), condition=%wide.region_13.13_spmd, body=%wide.region_10.12_spmd.sunk | while | flops 1094971392 | bytes 120717440 | solution.py:101
  506.5 9.4 fusion.216
  524.1 9.3 fusion.216
  542.4 35.1 %while.118 = (s32[]{:T(128)}, bf16[2,512,8,64]{1,3,2,0:T(8,128)(2,1)}, f32[2,8,512,1]{2,1,3,0:T(8,128)S(1)}, bf16[2,512,8,64]{1,3,2,0:T(8,128)(2,1)S(1)}, bf16[1...) while((s32[]{:T(128)}, bf16[2,512,8,64]{1,3,2,0:T(8,128)(2,1)}, ...), condition=%wide.region_13.13_spmd, body=%wide.region_10.12_spmd.sunk | while | flops 1094971392 | bytes 120717440 | solution.py:101
  550.6 9.3 fusion.216
  568.1 9.3 fusion.216
  593.0 53.9 %reduce-scatter.14.cloned.1.call-done = bf16[2,512,1024]{2,1,0:T(8,128)(2,1)} async-done(((bf16[2,1024,1024]{2,1,0:T(8,128)(2,1)}), bf16[2,512,1024]{2,1,0:T(8,128)(2,1)}) %reduce-scatter.14.cloned.1.call-update) | async-done | bytes 2097168 | tf_op jit(solution)/shard_map/reduce_scatter | solution.py:34
  655.2 44.1 %all-gather.30.cloned.1.call-done = bf16[1024,2048]{1,0:T(8,128)(2,1)} async-done(((bf16[64,2048]{1,0:T(8,128)(2,1)}), bf16[1024,2048]{1,0:T(8,128)(2,1)}) %all-gather.30.cloned.1.call-update) | async-done | bytes 4194320 | tf_op jit(solution)/shard_map/all_gather | solution.py:186
  699.3 57.4 %all-gather.28.cloned.1.call-done = bf16[2,1024,1024]{2,1,0:T(8,128)(2,1)} async-done(((bf16[2,512,1024]{2,1,0:T(8,128)(2,1)}), bf16[2,1024,1024]{2,1,0:T(8,128)(2,1)}) %all-gather.28.cloned.1.call-update) | async-done | bytes 4194320 | tf_op jit(solution)/shard_map/all_gather | solution.py:26
  756.7 49.7 %multiply_convert_fusion.2 = (bf16[2048,2048]{1,0:T(8,128)(2,1)}, f32[2048,2048]{1,0:T(8,128)}, f32[2048,2048]{1,0:T(8,128)}) fusion(f32[2048]{0:T(1024)S(1)} %convert_element_type.278, bf16[2048,1024]{1,0:T(8,128)(2,1)} %bitcast.439, bf16[1024,2048]{1,0:T(8,128)(2,1)} %all-gather.30.cloned.1.call-done), kind=kOutput, calls=%fused_computation.119 | convolution fusion | flops 8866758656 | bytes 50339840 | tf_op jit(solution)/shard_map/dot_general | solution.py:238
  809.2 13.9 convolution_convert_fusion.2
  823.1 53.0 %reduce-scatter.16.cloned.1.call-done = bf16[2,512,1024]{2,1,0:T(8,128)(2,1)} async-done(((bf16[2,1024,1024]{2,1,0:T(8,128)(2,1)}), bf16[2,512,1024]{2,1,0:T(8,128)(2,1)}) %reduce-scatter.16.cloned.1.call-update) | async-done | bytes 2097168 | tf_op jit(solution)/shard_map/reduce_scatter | solution.py:34
  888.7 56.9 %all-gather.34.cloned.1.call-done = bf16[2,1024,1024]{2,1,0:T(8,128)(2,1)} async-done(((bf16[2,512,1024]{2,1,0:T(8,128)(2,1)}), bf16[2,1024,1024]{2,1,0:T(8,128)(2,1)}) %all-gather.34.cloned.1.call-update) | async-done | bytes 4194320 | tf_op jit(solution)/shard_map/all_gather | solution.py:30
  945.5 28.0 %convert_reduce_fusion = (f32[2048]{0:T(1024)}, bf16[2048,2048]{1,0:T(8,128)(2,1)}) fusion(f32[2048,2048]{1,0:T(8,128)} %get-tuple-element.840, bf16[2048,1024]{1,0:T(8,128)(2,1)} %bitcast.445, bf16[2048,1024]{0,1:T(8,128)(2,1)} %all-gather.32.cloned.1.call-done, f32[2048,2048]{1,0:T(8,128)} %get-tuple-element.871, f32[2048]{0:T(1024)S(1)} %convert_element_type.278), kind=kOutput, calls=%fused_computation.117 | convolution fusion | flops 8661235712 | bytes 50348032 | tf_op jit(solution)/shard_map/dot_general | solution.py:14
  973.5 13.8 convolution_convert_fusion.1
  987.5 54.5 %reduce-scatter.18.cloned.1.call-done = bf16[2,512,1024]{2,1,0:T(8,128)(2,1)} async-done(((bf16[2,1024,1024]{2,1,0:T(8,128)(2,1)}), bf16[2,512,1024]{2,1,0:T(8,128)(2,1)}) %reduce-scatter.18.cloned.1.call-update) | async-done | bytes 2097168 | tf_op jit(solution)/shard_map/reduce_scatter | solution.py:40
  1052.6 56.8 %all-gather.36.cloned.1.call-done = bf16[2,1024,1024]{2,1,0:T(8,128)(2,1)} async-done(((bf16[2,512,1024]{2,1,0:T(8,128)(2,1)}), bf16[2,1024,1024]{2,1,0:T(8,128)(2,1)}) %all-gather.36.cloned.1.call-update) | async-done | bytes 4194320 | tf_op jit(solution)/shard_map/all_gather | solution.py:30
  1128.0 206.2 %while.113 = (s32[]{:T(128)}, bf16[2,1024,8,64]{1,3,2,0:T(8,128)(2,1)}, bf16[2,1024,8,64]{1,3,2,0:T(8,128)(2,1)}, bf16[2,1024,8,64]{1,3,2,0:T(8,128)(2,1)}, bf16...) while((s32[]{:T(128)}, ...), condition=%wide.region_30.31_spmd, body=%wide.region_26.30_spmd.sunk | while | flops 2724196352 | bytes 239256080 | solution.py:152
  1142.9 77.5 %while.119 = (s32[]{:T(128)}, f32[1024,8,64]{0,2,1:T(8,128)}, f32[1024,8,64]{0,2,1:T(8,128)}, bf16[2,512,8,64]{1,3,2,0:T(8,128)(2,1)}, bf16[2,512,8,64]{1,3,2,0:...) while((s32[]{:T(128)}, f32[1024,8,64]{0,2,1:T(8,128)}, ...), condition=%wide.region_29.29_spmd.clone, body=%wide.region_27.28_spmd.clone.sunk | while | flops 2724196352 | bytes 190955760 | solution.py:147
  1150.4 9.3 multiply_reduce_fusion.14
  1159.8 10.2 multiply_convert_fusion.8
  1189.8 9.3 multiply_reduce_fusion.14
  1199.1 10.2 multiply_convert_fusion.8
  1246.0 77.5 %while.119 = (s32[]{:T(128)}, f32[1024,8,64]{0,2,1:T(8,128)}, f32[1024,8,64]{0,2,1:T(8,128)}, bf16[2,512,8,64]{1,3,2,0:T(8,128)(2,1)}, bf16[2,512,8,64]{1,3,2,0:...) while((s32[]{:T(128)}, f32[1024,8,64]{0,2,1:T(8,128)}, ...), condition=%wide.region_29.29_spmd.clone, body=%wide.region_27.28_spmd.clone.sunk | while | flops 2724196352 | bytes 190955760 | solution.py:147
  1253.5 9.3 multiply_reduce_fusion.14
  1262.9 10.2 multiply_convert_fusion.8
  1292.9 9.3 multiply_reduce_fusion.14
  1302.2 10.2 multiply_convert_fusion.8
  1343.4 54.5 %reduce-scatter.20.cloned.1.call-done = bf16[2,512,1024]{2,1,0:T(8,128)(2,1)} async-done(((bf16[2,1024,1024]{2,1,0:T(8,128)(2,1)}), bf16[2,512,1024]{2,1,0:T(8,128)(2,1)}) %reduce-scatter.20.cloned.1.call-update) | async-done | bytes 2097168 | tf_op jit(solution)/shard_map/reduce_scatter | solution.py:291
  1409.6 14.0 convolution_convert_fusion.3
  1423.7 14.0 convolution_convert_fusion
  1486.8 8.5 convert_bitcast_fusion.1
  1497.3 7.8 copy.169
  1532.0 220.6 %while.117 = (s32[]{:T(128)}, bf16[2,1024,8,64]{1,3,2,0:T(8,128)(2,1)}, bf16[2,1024,8,64]{1,3,2,0:T(8,128)(2,1)}, bf16[2,1024,8,64]{1,3,2,0:T(8,128)(2,1)}, bf16...) while((s32[]{:T(128)}, ...), condition=%wide.region_38.39_spmd.clone, body=%wide.region_34.38_spmd.clone.sunk | while | flops 2737304064 | bytes 247976656 | solution.py:152
  1542.4 89.7 %while.121 = (s32[]{:T(128)}, f32[1024,8,64]{0,2,1:T(8,128)}, f32[1024,8,64]{0,2,1:T(8,128)}, bf16[2,512,8,64]{1,3,2,0:T(8,128)(2,1)}, bf16[2,512,8,64]{1,3,2,0:...) while((s32[]{:T(128)}, f32[1024,8,64]{0,2,1:T(8,128)}, ...), condition=%wide.region_37.37_spmd.clone, body=%wide.region_35.36_spmd.clone.sunk | while | flops 2737304064 | bytes 199676304 | solution.py:147
  1553.5 11.3 multiply_reduce_fusion.13
  1564.7 10.7 multiply_convert_fusion.7
  1575.4 7.1 fusion.198
  1599.0 11.2 multiply_reduce_fusion.13
  1610.2 10.6 multiply_convert_fusion.7
  1652.6 89.4 %while.121 = (s32[]{:T(128)}, f32[1024,8,64]{0,2,1:T(8,128)}, f32[1024,8,64]{0,2,1:T(8,128)}, bf16[2,512,8,64]{1,3,2,0:T(8,128)(2,1)}, bf16[2,512,8,64]{1,3,2,0:...) while((s32[]{:T(128)}, f32[1024,8,64]{0,2,1:T(8,128)}, ...), condition=%wide.region_37.37_spmd.clone, body=%wide.region_35.36_spmd.clone.sunk | while | flops 2737304064 | bytes 199676304 | solution.py:147
  1663.6 11.2 multiply_reduce_fusion.13
  1674.8 10.5 multiply_convert_fusion.7
  1708.9 11.2 multiply_reduce_fusion.13
  1720.1 10.5 multiply_convert_fusion.7
  1803.8 8.8 convert_bitcast_fusion
  1820.3 11.4 bitcast_convert_fusion.1
  1833.2 8.8 bitcast_convert_fusion
  1849.0 49.1 %all-reduce.7.cloned.1.call-done = (f32[4,1024]{1,0:T(4,128)}, f32[4096]{0:T(1024)}, f32[3,1024]{1,0:T(4,128)}, f32[6,1024]{1,0:T(8,128)}) async-done(((f32[4,1024]{1,0:T(4,128)}, f32[4096]{0:T(1024)}, f32[3,1024]{1,0:T(4,128)}, f32[6,1024]{1,0:T(8,128)}), (f32[4,1024]{1,0:T(4,128)}, f32[4096]{0:T(1024)}, f32[3,1024]{1,0:T(4,128)}, f32[6,1024]{1,0:T(8,128)})) %all-reduce.7.cloned.1.call-update) | async-done | bytes 69648 | tf_op jit(solution)/shard_map/psum | solution.py:362
  1900.7 60.9 %reduce-scatter.26.cloned.1.call-done = bf16[512,64]{0,1:T(8,128)(2,1)} async-done(((bf16[512,1024]{0,1:T(8,128)(2,1)}), bf16[512,64]{0,1:T(8,128)(2,1)}) %reduce-scatter.26.cloned.1.call-update) | async-done | bytes 65552 | tf_op jit(solution)/shard_map/reduce_scatter | solution.py:371
  1963.0 171.4 %all-reduce.9.cloned.1.call-done = (bf16[1024,3,512]{2,1,0:T(4,128)(2,1)}, bf16[1024,3,512]{2,1,0:T(4,128)(2,1)}) async-done(((bf16[1024,3,512]{2,1,0:T(4,128)(2,1)}, bf16[1024,3,512]{2,1,0:T(4,128)(2,1)}), (bf16[1024,3,512]{2,1,0:T(4,128)(2,1)}, bf16[1024,3,512]{2,1,0:T(4,128)(2,1)})) %all-reduce.9.cloned.1.call-update) | async-done | bytes 6291472
  2138.1 52.8 %reduce-scatter.22.cloned.1.call-done = bf16[2,512,1024]{2,1,0:T(8,128)(2,1)} async-done(((bf16[2,1024,1024]{2,1,0:T(8,128)(2,1)}), bf16[2,512,1024]{2,1,0:T(8,128)(2,1)}) %reduce-scatter.22.cloned.1.call-update) | async-done | bytes 2097168 | tf_op jit(solution)/shard_map/reduce_scatter | solution.py:40
  2195.9 52.2 %reduce-scatter.24.cloned.1.call-done = bf16[2,512,1024]{2,1,0:T(8,128)(2,1)} async-done(((bf16[2,1024,1024]{2,1,0:T(8,128)(2,1)}), bf16[2,512,1024]{2,1,0:T(8,128)(2,1)}) %reduce-scatter.24.cloned.1.call-update) | async-done | bytes 2097168 | tf_op jit(solution)/shard_map/reduce_scatter | solution.py:294
  (636 shorter events, 747.9 us)
Async XLA Ops:
  7.2 61.8 %all-gather.14.cloned.1.call-start = ((), (), s32[]{:S(2)}) async-start(), calls=%async_computation.11 | async-start | bytes 6291456 | tf_op jit(solution)/shard_map/all_gather | solution.py:26
  7.9 108.8 %all-gather.16.cloned.1.call-start = ((), (), s32[]{:S(2)}) async-start(), calls=%async_computation.12 | async-start | bytes 3342336 | tf_op jit(solution)/shard_map/all_gather | solution.py:182
  8.7 246.5 %all-gather.18.cloned.1.call-start = ((), (), s32[]{:S(2)}) async-start(), calls=%async_computation.13 | async-start | bytes 1114112 | tf_op jit(solution)/shard_map/all_gather | solution.py:183
  9.4 304.5 %reduce-scatter.12.cloned.1.call-start = ((), (), s32[]{:S(2)}) async-start(), calls=%async_computation.14 | async-start | bytes 6291456 | tf_op jit(solution)/shard_map/reduce_scatter | solution.py:34
  260.8 53.1 %copy-start.14 = (bf16[2,512,1024]{2,1,0:T(8,128)(2,1)S(1)}, bf16[2,512,1024]{2,1,0:T(8,128)(2,1)}, u32[]{:S(2)}) copy-start(bf16[2,512,1024]{2,1,0:T(8,128)(2,1)} %param.29) | copy-start | bytes 6291460
  260.9 111.2 %all-gather.24.cloned.1.call-start = ((), (), s32[]{:S(2)}) async-start(), calls=%async_computation.17 | async-start | bytes 6291456 | tf_op jit(solution)/shard_map/all_gather | solution.py:215
  261.5 158.2 %all-gather.22.cloned.1.call-start = ((), (), s32[]{:S(2)}) async-start(), calls=%async_computation.16 | async-start | bytes 3342336 | tf_op jit(solution)/shard_map/all_gather | solution.py:184
  262.0 214.8 %all-gather.20.cloned.1.call-start = ((), (), s32[]{:S(2)}) async-start(), calls=%async_computation.15 | async-start | bytes 6291456 | tf_op jit(solution)/shard_map/all_gather | solution.py:26
  262.7 54.8 %copy-start.46 = (f32[1,1024]{1,0:T(1,128)}, f32[1,1024]{1,0:T(1,128)S(1)}, u32[]{:S(2)}) copy-start(f32[1,1024]{1,0:T(1,128)S(1)} %get-tuple-element.870) | copy-start | bytes 12292
  263.3 54.2 %copy-start.37 = (f32[1,1024]{1,0:T(1,128)}, f32[1,1024]{1,0:T(1,128)S(1)}, u32[]{:S(2)}) copy-start(f32[1,1024]{1,0:T(1,128)S(1)} %get-tuple-element.866) | copy-start | bytes 12292
  263.3 54.2 %copy-start.52 = (f32[1,1024]{1,0:T(1,128)}, f32[1,1024]{1,0:T(1,128)S(1)}, u32[]{:S(2)}) copy-start(f32[1,1024]{1,0:T(1,128)S(1)} %get-tuple-element.867) | copy-start | bytes 12292
  320.7 265.9 %all-gather.26.cloned.1.call-start = ((), (), s32[]{:S(2)}) async-start(), calls=%async_computation.18 | async-start | bytes 1114112 | tf_op jit(solution)/shard_map/all_gather | solution.py:185
  321.5 325.4 %reduce-scatter.14.cloned.1.call-start = ((), (), s32[]{:S(2)}) async-start(), calls=%async_computation.19 | async-start | bytes 6291456 | tf_op jit(solution)/shard_map/reduce_scatter | solution.py:34
  592.3 54.6 %copy-start.15 = (bf16[2,512,1024]{2,1,0:T(8,128)(2,1)S(1)}, bf16[2,512,1024]{2,1,0:T(8,128)(2,1)}, u32[]{:S(2)}) copy-start(bf16[2,512,1024]{2,1,0:T(8,128)(2,1)} %param.29) | copy-start | bytes 6291460
  592.3 54.6 %copy-start.38 = (f32[1,1024]{1,0:T(1,128)S(1)}, f32[1,1024]{1,0:T(1,128)}, u32[]{:S(2)}) copy-start(f32[1,1024]{1,0:T(1,128)} %copy-done.37) | copy-start | bytes 12292
  592.3 54.6 %copy-start.41 = (f32[2,512]{1,0:T(2,128)S(1)}, f32[2,512]{1,0:T(2,128)}, u32[]{:S(2)}) copy-start(f32[2,512]{1,0:T(2,128)} %copy-done.40) | copy-start | bytes 12292
  592.3 54.6 %copy-start.44 = (f32[2,512]{1,0:T(2,128)S(1)}, f32[2,512]{1,0:T(2,128)}, u32[]{:S(2)}) copy-start(f32[2,512]{1,0:T(2,128)} %copy-done.43) | copy-start | bytes 12292
  592.3 54.6 %copy-start.47 = (f32[1,1024]{1,0:T(1,128)S(1)}, f32[1,1024]{1,0:T(1,128)}, u32[]{:S(2)}) copy-start(f32[1,1024]{1,0:T(1,128)} %copy-done.46) | copy-start | bytes 12292
  592.3 54.6 %copy-start.53 = (f32[1,1024]{1,0:T(1,128)S(1)}, f32[1,1024]{1,0:T(1,128)}, u32[]{:S(2)}) copy-start(f32[1,1024]{1,0:T(1,128)} %copy-done.52) | copy-start | bytes 12292
  592.3 54.6 %copy-start.61 = (f32[1,1024]{1,0:T(1,128)S(1)}, f32[1,1024]{1,0:T(1,128)}, u32[]{:S(2)}) copy-start(f32[1,1024]{1,0:T(1,128)} %get-tuple-element.865) | copy-start | bytes 12292
  592.3 107.0 %all-gather.30.cloned.1.call-start = ((), (), s32[]{:S(2)}) async-start(), calls=%async_computation.21 | async-start | bytes 4456448 | tf_op jit(solution)/shard_map/all_gather | solution.py:186
  592.9 163.8 %all-gather.28.cloned.1.call-start = ((), (), s32[]{:S(2)}) async-start(), calls=%async_computation.20 | async-start | bytes 6291456 | tf_op jit(solution)/shard_map/all_gather | solution.py:26
  654.5 154.6 %all-gather.32.cloned.1.call-start = ((), (), s32[]{:S(2)}) async-start(), calls=%async_computation.22 | async-start | bytes 4456448 | tf_op jit(solution)/shard_map/all_gather | solution.py:187
  655.1 221.0 %reduce-scatter.16.cloned.1.call-start = ((), (), s32[]{:S(2)}) async-start(), calls=%async_computation.23 | async-start | bytes 6291456 | tf_op jit(solution)/shard_map/reduce_scatter | solution.py:34
  823.1 53.1 %copy-start.60 = (f32[1,1024]{1,0:T(1,128)S(1)}, f32[1,1024]{1,0:T(1,128)}, u32[]{:S(2)}) copy-start(f32[1,1024]{1,0:T(1,128)} %get-tuple-element.863) | copy-start | bytes 12292
  823.1 122.5 %all-gather.34.cloned.1.call-start = ((), (), s32[]{:S(2)}) async-start(), calls=%async_computation.24 | async-start | bytes 6291456 | tf_op jit(solution)/shard_map/all_gather | solution.py:30
  888.6 153.3 %reduce-scatter.18.cloned.1.call-start = ((), (), s32[]{:S(2)}) async-start(), calls=%async_computation.25 | async-start | bytes 6291456 | tf_op jit(solution)/shard_map/reduce_scatter | solution.py:40
  987.4 122.0 %all-gather.36.cloned.1.call-start = ((), (), s32[]{:S(2)}) async-start(), calls=%async_computation.26 | async-start | bytes 6291456 | tf_op jit(solution)/shard_map/all_gather | solution.py:30
  1042.0 7.1 copy-start.34
  1049.1 60.3 %copy-start.76 = (bf16[512,1024]{0,1:T(8,128)(2,1)S(1)}, bf16[512,1024]{0,1:T(8,128)(2,1)}, u32[]{:S(2)}) copy-start(bf16[512,1024]{0,1:T(8,128)(2,1)} %all-gather.26.cloned.1.call-done) | copy-start | bytes 3145732
  1052.5 345.3 %reduce-scatter.20.cloned.1.call-start = ((), (), s32[]{:S(2)}) async-start(), calls=%async_computation.27 | async-start | bytes 6291456 | tf_op jit(solution)/shard_map/reduce_scatter | solution.py:291
  1209.3 7.0 copy-start.4
  1220.5 7.3 copy-start.6
  1323.6 7.2 copy-start.6
  1343.3 54.6 %copy-start.16 = (bf16[2,512,1024]{2,1,0:T(8,128)(2,1)S(1)}, bf16[2,512,1024]{2,1,0:T(8,128)(2,1)}, u32[]{:S(2)}) copy-start(bf16[2,512,1024]{2,1,0:T(8,128)(2,1)} %param.29) | copy-start | bytes 6291460
  1343.3 54.6 %copy-start.39 = (f32[1,1024]{1,0:T(1,128)S(1)}, f32[1,1024]{1,0:T(1,128)}, u32[]{:S(2)}) copy-start(f32[1,1024]{1,0:T(1,128)} %copy-done.37) | copy-start | bytes 12292
  1343.3 54.6 %copy-start.42 = (f32[2,512]{1,0:T(2,128)S(1)}, f32[2,512]{1,0:T(2,128)}, u32[]{:S(2)}) copy-start(f32[2,512]{1,0:T(2,128)} %copy-done.40) | copy-start | bytes 12292
  1343.3 54.6 %copy-start.45 = (f32[2,512]{1,0:T(2,128)S(1)}, f32[2,512]{1,0:T(2,128)}, u32[]{:S(2)}) copy-start(f32[2,512]{1,0:T(2,128)} %copy-done.43) | copy-start | bytes 12292
  1343.3 54.6 %copy-start.48 = (f32[1,1024]{1,0:T(1,128)S(1)}, f32[1,1024]{1,0:T(1,128)}, u32[]{:S(2)}) copy-start(f32[1,1024]{1,0:T(1,128)} %copy-done.46) | copy-start | bytes 12292
  1343.3 169.8 %all-gather.38.cloned.1.call-start = ((), (), s32[]{:S(2)}) async-start(), calls=%async_computation.28 | async-start | bytes 6291456 | tf_op jit(solution)/shard_map/all_gather | solution.py:30
  1409.6 434.3 %reduce-scatter.32.cloned.1.call-start = ((), (), s32[]{:S(2)}) async-start(), calls=%async_computation.34 | async-start | bytes 4456448 | tf_op jit(solution)/shard_map/reduce_scatter | solution.py:383
  1423.7 422.1 %reduce-scatter.30.cloned.1.call-start = ((), (), s32[]{:S(2)}) async-start(), calls=%async_computation.33 | async-start | bytes 4456448 | tf_op jit(solution)/shard_map/reduce_scatter | solution.py:380
  1437.8 409.7 %reduce-scatter.28.cloned.1.call-start = ((), (), s32[]{:S(2)}) async-start(), calls=%async_computation.32 | async-start | bytes 1114112 | tf_op jit(solution)/shard_map/reduce_scatter | solution.py:377
  1444.7 7.2 copy-start.69
  1444.7 8.7 copy-start.30
  1505.4 7.0 copy-start.57
  1511.7 386.4 %all-reduce.7.cloned.1.call-start = ((), (), s32[]{:S(2)}) async-start(), calls=%async_computation.35 | async-start | bytes 163840 | tf_op jit(solution)/shard_map/psum | solution.py:362
  1575.4 7.1 copy-start.1
  1575.4 7.1 copy-start.7
  1620.8 7.1 copy-start.1
  1620.8 7.1 copy-start.7
  1632.1 7.2 copy-start.9
  1685.4 7.1 copy-start.1
  1685.4 7.1 copy-start.7
  1730.6 7.1 copy-start.1
  1730.7 7.1 copy-start.7
  1741.9 7.3 copy-start.9
  1761.1 7.3 copy-start.36
  1773.9 187.6 %reduce-scatter.26.cloned.1.call-start = ((), (), s32[]{:S(2)}) async-start(), calls=%async_computation.31 | async-start | bytes 1114112 | tf_op jit(solution)/shard_map/reduce_scatter | solution.py:371
  1799.0 335.4 %all-reduce.9.cloned.1.call-start = ((), (), s32[]{:S(2)}) async-start(), calls=%async_computation.36 | async-start | bytes 16777216
  1818.4 372.5 %reduce-scatter.22.cloned.1.call-start = ((), (), s32[]{:S(2)}) async-start(), calls=%async_computation.29 | async-start | bytes 6291456 | tf_op jit(solution)/shard_map/reduce_scatter | solution.py:40
  1831.7 416.4 %reduce-scatter.24.cloned.1.call-start = ((), (), s32[]{:S(2)}) async-start(), calls=%async_computation.30 | async-start | bytes 6291456 | tf_op jit(solution)/shard_map/reduce_scatter | solution.py:294
  2138.1 110.0 %copy-start.64 = (f32[3,1024]{1,0:T(4,128)S(1)}, f32[3,1024]{1,0:T(4,128)}, u32[]{:S(2)}) copy-start(f32[3,1024]{1,0:T(4,128)} %get-tuple-element.1641) | copy-start | bytes 36868
  2138.1 110.6 %copy-start.55 = (f32[6,1024]{1,0:T(8,128)S(1)}, f32[6,1024]{1,0:T(8,128)}, u32[]{:S(2)}) copy-start(f32[6,1024]{1,0:T(8,128)} %get-tuple-element.1642) | copy-start | bytes 73732
  (86 other events, 311.8 us)
Sparse Core Ops, SparseCore 0:
  9.5 59.4 all-gather.13
  71.2 45.4 all-gather.15
  118.9 36.2 all-gather.17
  261.0 52.8 reduce-scatter.11
  315.3 56.7 all-gather.23
  374.1 45.4 all-gather.21
  421.7 55.0 all-gather.19
  479.0 37.8 all-gather.25
  592.5 54.3 reduce-scatter.13
  648.9 50.3 all-gather.29
  701.4 55.2 all-gather.27
  758.7 50.3 all-gather.31
  823.2 52.8 reduce-scatter.15
  888.8 56.7 all-gather.33
  987.5 54.3 reduce-scatter.17
  1052.7 56.7 all-gather.35
  1343.4 54.3 reduce-scatter.19
  1409.7 56.7 all-gather.37
  1470.3 72.7 reduce-scatter.31
  1546.8 71.8 reduce-scatter.29
  1622.3 56.6 reduce-scatter.27
  1774.0 123.9 all-reduce.6
  1902.3 59.2 reduce-scatter.25
  1965.2 169.1 all-reduce.8
  2136.7 54.1 reduce-scatter.21
  2193.7 54.3 reduce-scatter.23
where the time goes:
time: 2270 us; the launch traced here: 2260 us
  waiting for transfers between devices  1100 us (48%)
  matrix products  542 us (24%)
  local copies, waits for them, and re-layouts  394 us (17%)
  other arithmetic  200 us (9%)
    unnamed x27, waiting for transfers between devices  177 us
    reduce_scatter x3, waiting for transfers between devices, branch_sum(): lax.psum_scatter(term.astype(jnp.bfloat16), 'tp', scatter_dimension=1, ti...  157 us
    all_gather x3, waiting for transfers between devices, whole_rows(): return lax.all_gather(piece, 'tp', axis=1, tiled=True)  136 us
    all_gather x3, waiting for transfers between devices, whole_grads(): return lax.all_gather(piece, 'tp', axis=1, tiled=True)  114 us
    reduce_scatter x2, waiting for transfers between devices, piece_sum(): lax.psum_scatter(term.astype(jnp.bfloat16), 'tp', scatter_dimension=1, ti...  107 us
    convert_element_type x8, other arithmetic, one_block(): grad_scores = (probs * (grad_probs - row_delta)).astype(jnp.bfloat16)  83.1 us
    dot_general x8, matrix products, one_block(): jnp.einsum('qhc,khc->hqk', grad_blk, values_seq, preferred_element_type=j...  82.3 us
    reduce_scatter x1, waiting for transfers between devices, on_device(): lax.psum_scatter(d_self_out.astype(jnp.bfloat16), 'fsdp', scatter_dimensi...  60.9 us
  transfers between devices with their start and end apart: 26, of which 20 were waited for; matrix products, arithmetic and copies ran while one was open for 34% of the time, Pallas kernels for 0%

commit v1 on v0

--- a/solution.py
+++ b/solution.py
@@ -1,11 +1,13 @@
+import functools
+
 import jax
 import jax.numpy as jnp
 from jax import lax
+from jax.experimental import pallas as pl
+from jax.experimental.pallas import tpu as pltpu
 from jax.sharding import PartitionSpec as P
 
 HD = 64
-
-
 NORM_EPS = 1e-05
 ATT_SCALE = 0.125
 
@@ -152,7 +154,7 @@
     return lax.map(one_sequence, (query, keys, values, log_totals, grad_out))
 
 
-def on_device(
+def shared_sequences(
     layer_in,
     memory,
     out_grad,
@@ -399,6 +401,374 @@
         gain_total,
         shift_total,
     )
+
+
+NT=(((1,),(1,)),((),()))
+NN=(((1,),(0,)),((),()))
+f32=jnp.float32
+bf16=jnp.bfloat16
+
+def scores_t(k_h,q,i,bq,causal):
+    s=lax.dot_general(k_h,q,NT,preferred_element_type=f32)
+    return s
+
+def att_fwd_kernel(q_ref,k_ref,v_ref,o_ref,lse_ref,*,bq,causal):
+    n=q_ref.shape[0]; nk=k_ref.shape[0]
+    lane=lax.broadcasted_iota(jnp.int32,(nk,128),1)
+    k=k_ref[...]; v=v_ref[...]
+    zero=jnp.zeros((),bf16)
+    kh=[jnp.where(lane<HD,k,zero),jnp.where(lane>=HD,k,zero)]
+    vt=v.astype(f32).T.astype(bf16)
+    ones=jnp.ones((8,nk),bf16)
+    vh=[jnp.concatenate([vt[h*HD:(h+1)*HD],ones],0) for h in range(2)]
+    for i in range(n//bq):
+        q=q_ref[i*bq:(i+1)*bq,:]
+        L=(i+1)*bq if causal else nk
+        outs=[];lses=[]
+        for h in range(2):
+            s=lax.dot_general(kh[h][:L],q,NT,preferred_element_type=f32)
+            if causal:
+                keep=lax.broadcasted_iota(jnp.int32,(bq,bq),0)<=lax.broadcasted_iota(jnp.int32,(bq,bq),1)
+                sd=jnp.where(keep,s[L-bq:],-1e30)
+                s=jnp.concatenate([s[:L-bq],sd],0) if L>bq else sd
+            m=jnp.max(s,0,keepdims=True)
+            p=jnp.exp(s-m).astype(bf16)
+            ol=lax.dot_general(vh[h][:,:L],p,NN,preferred_element_type=f32)
+            l=ol[HD:HD+1]
+            outs.append(ol[:HD]*(1.0/l))
+            lses.append(m+jnp.log(l))
+        ot=jnp.concatenate(outs,0)
+        o_ref[i*bq:(i+1)*bq,:]=ot.T.astype(bf16)
+        lse_ref[0,:,i*bq:(i+1)*bq]=jnp.concatenate(lses,0)
+
+def att_fwd(q,k,v,causal,bq=256,qo=0,ko=0,vo=0,width=None):
+    n=q.shape[0]; nk=k.shape[0]; width=width or q.shape[1]; np_=width//128
+    spec=lambda rows,off: pl.BlockSpec((rows,128),lambda p: (0,p+off))
+    return pl.pallas_call(
+        functools.partial(att_fwd_kernel,bq=bq,causal=causal),
+        grid=(np_,),
+        in_specs=[spec(n,qo),spec(nk,ko),spec(nk,vo)],
+        out_specs=[spec(n,0),pl.BlockSpec((1,2,n),lambda p:(p,0,0))],
+        out_shape=[jax.ShapeDtypeStruct((n,width),bf16),jax.ShapeDtypeStruct((np_,2,n),f32)],
+        compiler_params=pltpu.CompilerParams(dimension_semantics=("arbitrary",),vmem_limit_bytes=56*2**20),
+    )(q,k,v)
+
+def att_bwd_kernel(q_ref,k_ref,v_ref,o_ref,do_ref,lse_ref,dq_ref,dk_ref,dv_ref,dk_acc,dv_acc,*,bq,causal):
+    n=q_ref.shape[0]; nk=k_ref.shape[0]
+    lane=lax.broadcasted_iota(jnp.int32,(nk,128),1)
+    lq=lax.broadcasted_iota(jnp.int32,(bq,128),1)
+    k=k_ref[...]; v=v_ref[...]
+    zero=jnp.zeros((),bf16)
+    kh=[jnp.where(lane<HD,k,zero),jnp.where(lane>=HD,k,zero)]
+    vh=[jnp.where(lane<HD,v,zero),jnp.where(lane>=HD,v,zero)]
+    kt=k.astype(f32).T.astype(bf16)
+    dk_acc[...]=jnp.zeros_like(dk_acc); dv_acc[...]=jnp.zeros_like(dv_acc)
+    for i in range(n//bq):
+        rows=slice(i*bq,(i+1)*bq)
+        q=q_ref[rows,:]; do=do_ref[rows,:]
+        L=(i+1)*bq if causal else nk
+        dot_=(do.astype(f32)*o_ref[rows,:].astype(f32)).T
+        qm=[jnp.where(lq<HD,q,zero),jnp.where(lq>=HD,q,zero)]
+        dm=[jnp.where(lq<HD,do,zero),jnp.where(lq>=HD,do,zero)]
+        dqs=[]
+        for h in range(2):
+            s=lax.dot_general(kh[h][:L],q,NT,preferred_element_type=f32)
+            dp=lax.dot_general(vh[h][:L],do,NT,preferred_element_type=f32)
+            lse=lse_ref[0,h:h+1,rows]
+            delta=jnp.sum(dot_[h*HD:(h+1)*HD],0,keepdims=True)
+            if causal:
+                keep=lax.broadcasted_iota(jnp.int32,(bq,bq),0)<=lax.broadcasted_iota(jnp.int32,(bq,bq),1)
+                sd=jnp.where(keep,s[L-bq:],-1e30)
+                s=jnp.concatenate([s[:L-bq],sd],0) if L>bq else sd
+            p=jnp.exp(s-lse)
+            ds=(p*(dp-delta)).astype(bf16)
+            pb=p.astype(bf16)
+            dv_acc[:L,:]+=lax.dot_general(pb,dm[h],NN,preferred_element_type=f32)
+            dk_acc[:L,:]+=lax.dot_general(ds,qm[h],NN,preferred_element_type=f32)
+            dqs.append(lax.dot_general(kt[h*HD:(h+1)*HD,:L],ds,NN,preferred_element_type=f32))
+        dq_ref[rows,:]=(jnp.concatenate(dqs,0)*0.125).T.astype(bf16)
+    dk_ref[...]=dk_acc[...].astype(bf16)
+    dv_ref[...]=dv_acc[...].astype(bf16)
+
+def att_bwd(q,k,v,o,do,lse,causal,bq=256,qo=0,ko=0,vo=0):
+    n=q.shape[0]; nk=k.shape[0]; width=o.shape[1]; np_=width//128
+    spec=lambda rows,off: pl.BlockSpec((rows,128),lambda p: (0,p+off))
+    return pl.pallas_call(
+        functools.partial(att_bwd_kernel,bq=bq,causal=causal),
+        grid=(np_,),
+        in_specs=[spec(n,qo),spec(nk,ko),spec(nk,vo),spec(n,0),spec(n,0),pl.BlockSpec((1,2,n),lambda p:(p,0,0))],
+        out_specs=[spec(n,0),spec(nk,0),spec(nk,0)],
+        out_shape=[jax.ShapeDtypeStruct((n,width),bf16),jax.ShapeDtypeStruct((nk,width),bf16),jax.ShapeDtypeStruct((nk,width),bf16)],
+        scratch_shapes=[pltpu.VMEM((nk,128),f32)]*2,
+        compiler_params=pltpu.CompilerParams(dimension_semantics=("arbitrary",),vmem_limit_bytes=56*2**20),
+    )(q,k,v,o,do,lse)
+
+
+ERFC_SLOPE = 0.44
+ERFC_COEFS = (
+    0.12411048270139104,
+    0.12443557227306976,
+    0.1086564621750582,
+    0.10790840846971936,
+    -0.01009671066483208,
+    0.1483525285505606,
+    -0.13897999621011298,
+    0.03561334337852199,
+)
+
+
+def gelu_and_slope(u):
+    a = jnp.abs(u) * 0.7071067811865476
+    t = 1.0 / (1.0 + ERFC_SLOPE * a)
+    q = jnp.full_like(t, ERFC_COEFS[-1])
+    for c in ERFC_COEFS[-2::-1]:
+        q = q * t + c
+    e = jnp.exp(-(a * a))
+    tail = e * (t * q)
+    phi = jnp.where(u < 0, tail, 1.0 - tail)
+    return u * phi, phi + u * (e * 0.3989422804014327)
+
+
+def nn(a, b):
+    return lax.dot_general(a, b, NN, preferred_element_type=f32)
+
+
+def nt(a, b):
+    return lax.dot_general(a, b, NT, preferred_element_type=f32)
+
+
+def tn(a, b):
+    return lax.dot_general(a, b, (((0,), (0,)), ((), ())), preferred_element_type=f32)
+
+
+def norm_rows(r, gain, shift):
+    center = r - jnp.mean(r, -1, keepdims=True)
+    inv = lax.rsqrt(jnp.mean(center * center, -1, keepdims=True) + NORM_EPS)
+    n = center * inv
+    return n * gain + shift, n, inv
+
+
+def norm_rows_back(e, n, inv, gain):
+    eg = e * gain
+    grad = inv * (eg - jnp.mean(eg, -1, keepdims=True) - n * jnp.mean(eg * n, -1, keepdims=True))
+    return grad, jnp.sum(e * n, 0), jnp.sum(e, 0), jnp.sum(grad, 0)
+
+
+def trade(x):
+    return lax.ppermute(x, "tp", [(0, 1), (1, 0)])
+
+
+def in_order(place, own, other, axis=0):
+    return jnp.where(
+        place == 0,
+        jnp.concatenate([own, other], axis),
+        jnp.concatenate([other, own], axis),
+    )
+
+
+def own_sequence(piece, place):
+    own = lax.dynamic_index_in_dim(piece, place, 0, keepdims=False)
+    away = lax.dynamic_index_in_dim(piece, 1 - place, 0, keepdims=False)
+    return in_order(place, own, trade(away))
+
+
+def to_pieces(rows, place):
+    half = rows.shape[0] // 2
+    halves = rows.reshape(2, half, rows.shape[1])
+    own = lax.dynamic_index_in_dim(halves, place, 0, keepdims=True)
+    away = lax.dynamic_index_in_dim(halves, 1 - place, 0, keepdims=True)
+    return in_order(place, own, trade(away))
+
+
+def sum_everywhere(x, fsdp_count):
+    step = 1
+    while step < fsdp_count:
+        x = x + lax.ppermute(x, "fsdp", [(i, i ^ step) for i in range(fsdp_count)])
+        step *= 2
+    return x + trade(x)
+
+
+def whole_sequences(
+    layer_in,
+    memory,
+    out_grad,
+    w_self_in,
+    w_self_out,
+    w_cross_in,
+    w_cross_out,
+    w_up,
+    w_down,
+    head_bias,
+    up_bias,
+    norm_gain,
+    row_bias,
+):
+    place = lax.axis_index("tp")
+    fsdp_count = lax.axis_size("fsdp")
+    width = layer_in.shape[2]
+    cols = w_self_in.shape[2]
+    units = w_up.shape[1]
+    shard = w_self_in.shape[0]
+    gains = norm_gain.astype(f32)
+    shifts = row_bias.astype(f32)
+
+    def gather(*parts):
+        mine = jnp.concatenate(parts, 1) if len(parts) > 1 else parts[0]
+        both = lax.all_gather(mine, ("tp", "fsdp"), axis=0, tiled=True)
+        return both.reshape(2, width, mine.shape[1])
+
+    def scatter(parts):
+        low = jnp.concatenate([p.astype(bf16) for p in parts], 0)
+        return lax.psum_scatter(low, ("tp", "fsdp"), scatter_dimension=0, tiled=True).astype(f32)
+
+    small = jnp.concatenate([head_bias.reshape(-1), up_bias])
+    small = in_order(place, small[None], trade(small)[None])
+    hb = small[:, : 4 * cols].reshape(2, 4, cols).astype(f32)
+    ub = small[:, 4 * cols :].astype(f32)
+
+    g_self = gather(w_self_in.reshape(shard, 3 * cols), w_self_out.T)
+    g_cross = gather(w_cross_in.reshape(shard, 3 * cols), w_cross_out.T)
+    g_ffn = gather(w_up, w_down.T)
+    c3 = 3 * cols
+
+    x = own_sequence(layer_in, place)
+    mem = own_sequence(memory, place)
+    cot = own_sequence(out_grad, place)
+    xf = x.astype(f32)
+    halves = (0, 1)
+    zero = jnp.zeros((cols,), f32)
+    scale3 = jnp.concatenate([zero + ATT_SCALE, zero + 1.0, zero + 1.0])
+    blk = cols // 128
+
+    sy, sa, sl = [], [], []
+    for t in halves:
+        bias = jnp.concatenate([hb[t, 0], zero, hb[t, 1]])
+        y = ((nn(x, g_self[t, :, :c3]) + bias) * scale3).astype(bf16)
+        o, lse = att_fwd(y, y, y, True, 512, 0, blk, 2 * blk, cols)
+        sy.append(y)
+        sa.append(o)
+        sl.append(lse)
+    r1 = xf + (nt(sa[0], g_self[0, :, c3:]) + nt(sa[1], g_self[1, :, c3:])) + shifts[0]
+    h1, n1, i1 = norm_rows(r1, gains[0], shifts[3])
+    h1b = h1.astype(bf16)
+
+    cq, ckv, ca, cl = [], [], [], []
+    for t in halves:
+        kv = (nn(mem, g_cross[t, :, cols:c3]) + jnp.concatenate([zero, hb[t, 3]])).astype(bf16)
+        q = ((nn(h1b, g_cross[t, :, :cols]) + hb[t, 2]) * ATT_SCALE).astype(bf16)
+        o, lse = att_fwd(q, kv, kv, False, 512, 0, 0, blk, cols)
+        cq.append(q)
+        ckv.append(kv)
+        ca.append(o)
+        cl.append(lse)
+    r2 = h1 + (nt(ca[0], g_cross[0, :, c3:]) + nt(ca[1], g_cross[1, :, c3:])) + shifts[1]
+    h2, n2, i2 = norm_rows(r2, gains[1], shifts[4])
+    h2b = h2.astype(bf16)
+
+    act, slope = [], []
+    for t in halves:
+        g, d = gelu_and_slope(nn(h2b, g_ffn[t, :, :units]) + ub[t])
+        act.append(g.astype(bf16))
+        slope.append(d.astype(bf16))
+    r3 = h2 + (nt(act[0], g_ffn[0, :, units:]) + nt(act[1], g_ffn[1, :, units:])) + shifts[2]
+    h3, n3, i3 = norm_rows(r3, gains[2], shifts[5])
+    mixed = to_pieces(h3.astype(bf16), place)
+
+    dr3, gg3, gs3, gb3 = norm_rows_back(cot.astype(f32), n3, i3, gains[2])
+    e3 = dr3.astype(bf16)
+    du = [(nn(e3, g_ffn[t, :, units:]) * slope[t].astype(f32)).astype(bf16) for t in halves]
+    s_ffn = scatter(
+        [jnp.concatenate([tn(h2b, du[t]), tn(e3, act[t])], 1) for t in halves]
+    )
+    gu = jnp.stack([jnp.sum(du[t].astype(f32), 0) for t in halves])
+    dh2 = dr3 + (nt(du[0], g_ffn[0, :, :units]) + nt(du[1], g_ffn[1, :, :units]))
+    dr2, gg2, gs2, gb2 = norm_rows_back(dh2, n2, i2, gains[1])
+    e2 = dr2.astype(bf16)
+
+    dcq, dck, dcv = [], [], []
+    for t in halves:
+        da = nn(e2, g_cross[t, :, c3:]).astype(bf16)
+        a, b, c = att_bwd(cq[t], ckv[t], ckv[t], ca[t], da, cl[t], False, 256, 0, 0, blk)
+        dcq.append(a)
+        dck.append(b)
+        dcv.append(c)
+    grad_cross = [
+        jnp.concatenate(
+            [tn(h1b, dcq[t]), tn(mem, dck[t]), tn(mem, dcv[t]), tn(e2, ca[t])], 1
+        )
+        for t in halves
+    ]
+    dmem = sum(
+        nt(dck[t], g_cross[t, :, cols : 2 * cols]) + nt(dcv[t], g_cross[t, :, 2 * cols : c3])
+        for t in halves
+    )
+    d_memory = to_pieces(dmem.astype(bf16), place)
+    dh1 = dr2 + (nt(dcq[0], g_cross[0, :, :cols]) + nt(dcq[1], g_cross[1, :, :cols]))
+    dr1, gg1, gs1, gb1 = norm_rows_back(dh1, n1, i1, gains[0])
+    e1 = dr1.astype(bf16)
+
+    dsq, dsk, dsv = [], [], []
+    for t in halves:
+        da = nn(e1, g_self[t, :, c3:]).astype(bf16)
+        y = sy[t]
+        a, b, c = att_bwd(y, y, y, sa[t], da, sl[t], True, 256, 0, blk, 2 * blk)
+        dsq.append(a)
+        dsk.append(b)
+        dsv.append(c)
+    grad_self = [
+        jnp.concatenate([tn(x, dsq[t]), tn(x, dsk[t]), tn(x, dsv[t]), tn(e1, sa[t])], 1)
+        for t in halves
+    ]
+    s_att = scatter([jnp.concatenate([grad_cross[t], grad_self[t]], 1) for t in halves])
+    dx = dr1 + sum(
+        nt(dsq[t], g_self[t, :, :cols])
+        + nt(dsk[t], g_self[t, :, cols : 2 * cols])
+        + nt(dsv[t], g_self[t, :, 2 * cols : c3])
+        for t in halves
+    )
+    d_layer_in = to_pieces(dx.astype(bf16), place)
+
+    def col_sums(pair):
+        return jnp.stack([jnp.sum(p.astype(f32), 0) for p in pair])
+
+    gh = jnp.stack([col_sums(dsq), col_sums(dsv), col_sums(dcq), col_sums(dcv)], 1)
+    flat = jnp.concatenate(
+        [
+            v.reshape(-1)
+            for v in (gh, gu, gg1, gg2, gg3, gb1, gb2, gb3, gs1, gs2, gs3)
+        ]
+    )
+    flat = sum_everywhere(flat.reshape(-1, 128), fsdp_count).reshape(-1)
+    head_sum = lax.dynamic_index_in_dim(flat[: 8 * cols].reshape(2, 4, cols), place, 0, False)
+    unit_sum = lax.dynamic_index_in_dim(
+        flat[8 * cols : 8 * cols + 2 * units].reshape(2, units), place, 0, False
+    )
+    rest = flat[8 * cols + 2 * units :].reshape(9, width)
+
+    cross_part, self_part = s_att[:, : 4 * cols], s_att[:, 4 * cols :]
+    return (
+        mixed,
+        d_layer_in,
+        d_memory,
+        self_part[:, :c3].reshape(shard, 3, cols),
+        self_part[:, c3:].T,
+        cross_part[:, :c3].reshape(shard, 3, cols),
+        cross_part[:, c3:].T,
+        s_ffn[:, :units],
+        s_ffn[:, units:].T,
+        head_sum,
+        unit_sum,
+        rest[:3],
+        rest[3:],
+    )
+
+
+def on_device(layer_in, *rest):
+    fsdp_count = lax.axis_size("fsdp")
+    pair = lax.axis_size("tp") == 2 and layer_in.shape[0] == 2
+    if pair and fsdp_count & (fsdp_count - 1) == 0:
+        return whole_sequences(layer_in, *rest)
+    return shared_sequences(layer_in, *rest)
 
 
 def solution(mesh):

time: 2270 us -> 1020 us (0.45)
  waiting for transfers between devices: 1100 us -> 385 us
  local copies, waits for them, and re-layouts: 394 us -> 53.3 us
  matrix products: 542 us -> 275 us
  Pallas kernels: 0 us -> 141 us
  other arithmetic: 200 us -> 123 us
    all_gather x13 -> x3, waiting for transfers between devices: 442 us -> 146 us  [gather(): both = lax.all_gather(mine, ('tp', 'fsdp'), axis=0, tiled=True)]
    dot_general x77 -> x54, matrix products: 542 us -> 275 us  [the longest x14 116 us: nn(): return lax.dot_general(a, b, NN, preferred_element_type=f32)]
    reduce_scatter x11 -> x1, waiting for transfers between devices: 432 us -> 179 us  [scatter(): lax.psum_scatter(low, ('tp', 'fsdp'), scatter_dimension=0, tiled=True)]
    unnamed x27 -> x6, waiting for transfers between devices: 177 us -> 0.08 us
    pallas_call x0 -> x8, Pallas kernels: none -> 141 us  [the longest x4 81.4 us: att_bwd(): pl.pallas_call(functools.partial(att_bwd_kernel, bq=bq, causal=causal), g...]
    convert_element_type x25 -> x8, other arithmetic: 123 us -> 3.67 us  [the longest x2 1.25 us: scatter(): lax.psum_scatter(low, ('tp', 'fsdp'), scatter_dimension=0, tiled=True)]
    concatenate x2 -> x6, other arithmetic: 2.59 us -> 91.5 us  [the longest x2 86.5 us: scatter(): low = jnp.concatenate([p.astype(bf16) for p in parts], 0)]
    while x154 -> x0, local copies, waits for them, and re-layouts: 88.1 us -> none
  transfers between devices with their start and end apart: 26 -> 17, of which waited for: 20 -> 10; matrix products, arithmetic and copies ran while one was open for 34% -> 25% of each run, Pallas kernels for 0% -> 6%
where the time goes in v1:
time: 1020 us; the launch traced here: 1010 us
  waiting for transfers between devices  385 us (38%)
  matrix products  275 us (27%)
  Pallas kernels  141 us (14%)
  other arithmetic  123 us (12%)
  local copies, waits for them, and re-layouts  53.3 us (5%)
  between operations  15.4 us (2%)
  starting transfers between devices  13 us (1%)
    reduce_scatter x1, waiting for transfers between devices, scatter(): lax.psum_scatter(low, ('tp', 'fsdp'), scatter_dimension=0, tiled=True)  179 us
    all_gather x3, waiting for transfers between devices, gather(): both = lax.all_gather(mine, ('tp', 'fsdp'), axis=0, tiled=True)  146 us
    dot_general x14, matrix products, nn(): return lax.dot_general(a, b, NN, preferred_element_type=f32)  116 us
    dot_general x20, matrix products, nt(): return lax.dot_general(a, b, NT, preferred_element_type=f32)  89.7 us
    concatenate x2, other arithmetic, scatter(): low = jnp.concatenate([p.astype(bf16) for p in parts], 0)  86.5 us
    pallas_call x4, Pallas kernels, att_bwd(): pl.pallas_call(functools.partial(att_bwd_kernel, bq=bq, causal=causal), g...  81.4 us
    dot_general x20, matrix products, tn(): lax.dot_general(a, b, (((0,), (0,)), ((), ())), preferred_element_type=f32)  68.8 us
    pallas_call x4, Pallas kernels, att_fwd(): pl.pallas_call(functools.partial(att_fwd_kernel, bq=bq, causal=causal), g...  59.5 us
  transfers between devices with their start and end apart: 17, of which 10 were waited for; matrix products, arithmetic and copies ran while one was open for 25% of the time, Pallas kernels for 6%

profile of v1, /device:TPU:0, one launch (start us, length us, event | category | flops | bytes accessed | tf_op | source)
XLA Modules:
  0.0 1006.5 jit_solution(14269614139227620697)
XLA Ops:
  15.9 3.0 collective-permute-start.1
  27.3 24.8 %collective-permute-done = bf16[512,1024]{1,0:T(8,128)(2,1)S(1)} collective-permute-done((bf16[512,1024]{1,0:T(8,128)(2,1)}, bf16[512,1024]{1,0:T(8,128)(2,1)S(1)}, u32[]{:S(2)}, u32[]{:S(2)}) %collective-permute-start) | collective-permute-done | bytes 1048608 | tf_op jit(solution)/shard_map/ppermute | solution.py:558
  52.1 63.1 %all-gather.4.cloned.1.call-done = bf16[2048,2048]{1,0:T(8,128)(2,1)} async-done(((bf16[64,2048]{1,0:T(8,128)(2,1)}), bf16[2048,2048]{1,0:T(8,128)(2,1)}) %all-gather.4.cloned.1.call-update) | async-done | bytes 8388624 | tf_op jit(solution)/shard_map/all_gather | solution.py:617
  115.3 8.3 multiply_convert_fusion.5.q_ref.k_ref.v_ref
  123.6 11.9 %shard_map.228 = (bf16[1024,512]{1,0:T(8,128)(2,1)}, f32[4,2,1024]{2,1,0:T(2,128)}) custom-call(bf16[1024,1536]{1,0:T(8,128)(2,1)} %multiply_convert_fusion.5.q_ref.k_ref.v_ref, bf16[1024,1536]{1,0:T(8,128)(2,1)} %multiply_convert_fusion.5.q_ref.k_ref.v_ref, bf16[1024,1536]{1,0:T(8,128)(2,1)} %multiply_convert_fusion.5.q_ref.k_ref.v_ref), custom_call_target="tpu_custom_call" | custom-call | tf_op jit(solution)/shard_map/pallas_call | solution.py:447
  135.5 8.3 multiply_convert_fusion.4.q_ref.k_ref.v_ref
  143.8 12.0 %shard_map.229 = (bf16[1024,512]{1,0:T(8,128)(2,1)}, f32[4,2,1024]{2,1,0:T(2,128)}) custom-call(bf16[1024,1536]{1,0:T(8,128)(2,1)} %multiply_convert_fusion.4.q_ref.k_ref.v_ref, bf16[1024,1536]{1,0:T(8,128)(2,1)} %multiply_convert_fusion.4.q_ref.k_ref.v_ref, bf16[1024,1536]{1,0:T(8,128)(2,1)} %multiply_convert_fusion.4.q_ref.k_ref.v_ref), custom_call_target="tpu_custom_call" | custom-call | tf_op jit(solution)/shard_map/pallas_call | solution.py:447
  158.4 3.4 fusion.56
  164.5 29.8 %all-gather.6.cloned.1.call-done = bf16[2048,2048]{1,0:T(8,128)(2,1)} async-done(((bf16[64,2048]{1,0:T(8,128)(2,1)}), bf16[2048,2048]{1,0:T(8,128)(2,1)}) %all-gather.6.cloned.1.call-update) | async-done | bytes 8388624 | tf_op jit(solution)/shard_map/all_gather | solution.py:617
  194.3 3.5 multiply_convert_fusion.7.q_ref
  197.9 5.9 add_convert_fusion.6.k_ref.v_ref
  203.8 17.7 %shard_map.230 = (bf16[1024,512]{1,0:T(8,128)(2,1)}, f32[4,2,1024]{2,1,0:T(2,128)}) custom-call(bf16[1024,512]{1,0:T(8,128)(2,1)} %multiply_convert_fusion.7.q_ref, bf16[1024,1024]{1,0:T(8,128)(2,1)} %add_convert_fusion.6.k_ref.v_ref, bf16[1024,1024]{1,0:T(8,128)(2,1)} %add_convert_fusion.6.k_ref.v_ref), custom_call_target="tpu_custom_call" | custom-call | tf_op jit(solution)/shard_map/pallas_call | solution.py:447
  221.4 3.5 multiply_convert_fusion.6.q_ref
  224.9 6.3 add_convert_fusion.5.k_ref.v_ref
  231.2 18.0 %shard_map.231 = (bf16[1024,512]{1,0:T(8,128)(2,1)}, f32[4,2,1024]{2,1,0:T(2,128)}) custom-call(bf16[1024,512]{1,0:T(8,128)(2,1)} %multiply_convert_fusion.6.q_ref, bf16[1024,1024]{1,0:T(8,128)(2,1)} %add_convert_fusion.5.k_ref.v_ref, bf16[1024,1024]{1,0:T(8,128)(2,1)} %add_convert_fusion.5.k_ref.v_ref), custom_call_target="tpu_custom_call" | custom-call | tf_op jit(solution)/shard_map/pallas_call | solution.py:447
  249.2 2.7 fusion.43
  252.0 3.0 fusion.57
  257.9 52.9 %all-gather.8.cloned.1.call-done = bf16[2048,4096]{1,0:T(8,128)(2,1)} async-done(((bf16[64,4096]{1,0:T(8,128)(2,1)}), bf16[2048,4096]{1,0:T(8,128)(2,1)}) %all-gather.8.cloned.1.call-update) | async-done | bytes 16777232 | tf_op jit(solution)/shard_map/all_gather | solution.py:617
  310.8 15.3 %multiply_convert_fusion.2 = (bf16[1024,2048]{1,0:T(8,128)(2,1)S(1)}, f32[1024,2048]{1,0:T(8,128)}) fusion(f32[2048]{0:T(1024)S(1)} %bitcast.320, bf16[1024,1024]{1,0:T(8,128)(2,1)S(1)} %fusion.8, bf16[2,1024,4096]{2,1,0:T(8,128)(2,1)} %bitcast.332), kind=kOutput, calls=%fused_computation.10 | convolution fusion | flops 4355784704 | bytes 18882560 | tf_op jit(solution)/shard_map/dot_general | solution.py:533
  326.1 16.5 %multiply_convert_fusion.3 = (bf16[1024,2048]{1,0:T(8,128)(2,1)S(1)}, f32[1024,2048]{1,0:T(8,128)}) fusion(f32[2048]{0:T(1024)S(1)} %bitcast.318, bf16[1024,1024]{1,0:T(8,128)(2,1)S(1)} %fusion.8, bf16[2,1024,4096]{2,1,0:T(8,128)(2,1)} %bitcast.333), kind=kOutput, calls=%fused_computation.12 | convolution fusion | flops 4355784704 | bytes 18882560 | tf_op jit(solution)/shard_map/dot_general | solution.py:533
  342.6 8.2 fusion.11
  350.8 7.4 fusion.58
  359.4 5.3 fusion.6
  364.8 6.3 fusion.46
  371.4 17.3 %convert_reduce_fusion = (f32[2048]{0:T(1024)}, bf16[1024,2048]{1,0:T(8,128)(2,1)S(1)}) fusion(f32[1024,2048]{1,0:T(8,128)} %get-tuple-element.159, f32[2048]{0:T(1024)S(1)} %bitcast.321, bf16[1024,1024]{1,0:T(8,128)(2,1)S(1)} %convert_element_type.157, bf16[2,1024,4096]{2,1,0:T(8,128)(2,1)} %bitcast.336), kind=kOutput, calls=%fused_computation.4 | convolution fusion | flops 4370462720 | bytes 18890752 | tf_op jit(solution)/shard_map/dot_general | solution.py:533
  388.7 16.0 %convert_reduce_fusion.1 = (f32[2048]{0:T(1024)}, bf16[1024,2048]{1,0:T(8,128)(2,1)S(1)}) fusion(f32[1024,2048]{1,0:T(8,128)S(1)} %bitcast.341, f32[2048]{0:T(1024)S(1)} %bitcast.319, bf16[1024,1024]{1,0:T(8,128)(2,1)S(1)} %convert_element_type.157, bf16[2,1024,4096]{2,1,0:T(8,128)(2,1)} %bitcast.337), kind=kOutput, calls=%fused_computation.5 | convolution fusion | flops 4370462720 | bytes 18890752 | tf_op jit(solution)/shard_map/dot_general | solution.py:533
  404.7 9.8 fusion.9
  414.5 10.1 multiply_reduce_fusion
  426.8 4.3 convolution_convert_fusion.22.do_ref
  431.1 3.4 convolution_convert_fusion.23.do_ref
  434.6 23.7 %shard_map.232 = (bf16[1024,512]{1,0:T(8,128)(2,1)}, bf16[1024,512]{1,0:T(8,128)(2,1)}, bf16[1024,512]{1,0:T(8,128)(2,1)}) custom-call(bf16[1024,512]{1,0:T(8,128)(2,1)} %multiply_convert_fusion.7.q_ref, bf16[1024,1024]{1,0:T(8,128)(2,1)} %add_convert_fusion.6.k_ref.v_ref, bf16[1024,1024]{1,0:T(8,128)(2,1)} %add_convert_fusion.6.k_ref.v_ref, ...), custom_call_target="tpu_custom_call" | custom-call | tf_op jit(solution)/shard_map/pallas_call | solution.py:496
  458.2 4.8 fusion.42
  463.1 24.0 %shard_map.233 = (bf16[1024,512]{1,0:T(8,128)(2,1)}, bf16[1024,512]{1,0:T(8,128)(2,1)}, bf16[1024,512]{1,0:T(8,128)(2,1)}) custom-call(bf16[1024,512]{1,0:T(8,128)(2,1)} %multiply_convert_fusion.6.q_ref, bf16[1024,1024]{1,0:T(8,128)(2,1)} %add_convert_fusion.5.k_ref.v_ref, bf16[1024,1024]{1,0:T(8,128)(2,1)} %add_convert_fusion.5.k_ref.v_ref, ...), custom_call_target="tpu_custom_call" | custom-call | tf_op jit(solution)/shard_map/pallas_call | solution.py:496
  487.1 6.5 multiply_reduce_fusion.1
  495.4 4.2 convolution_convert_fusion.20.do_ref
  499.6 3.6 convolution_convert_fusion.21.do_ref
  507.9 3.9 fusion.23
  511.8 4.0 fusion.22
  518.1 16.9 %shard_map.235 = (bf16[1024,512]{1,0:T(8,128)(2,1)}, bf16[1024,512]{1,0:T(8,128)(2,1)}, bf16[1024,512]{1,0:T(8,128)(2,1)}) custom-call(bf16[1024,1536]{1,0:T(8,128)(2,1)} %multiply_convert_fusion.4.q_ref.k_ref.v_ref, bf16[1024,1536]{1,0:T(8,128)(2,1)} %multiply_convert_fusion.4.q_ref.k_ref.v_ref, ...), custom_call_target="tpu_custom_call" | custom-call | tf_op jit(solution)/shard_map/pallas_call | solution.py:496
  535.0 3.6 fusion.20
  545.7 4.0 fusion.31
  549.7 4.0 fusion.30
  556.0 16.8 %shard_map.234 = (bf16[1024,512]{1,0:T(8,128)(2,1)}, bf16[1024,512]{1,0:T(8,128)(2,1)}, bf16[1024,512]{1,0:T(8,128)(2,1)}) custom-call(bf16[1024,1536]{1,0:T(8,128)(2,1)} %multiply_convert_fusion.5.q_ref.k_ref.v_ref, bf16[1024,1536]{1,0:T(8,128)(2,1)} %multiply_convert_fusion.5.q_ref.k_ref.v_ref, ...), custom_call_target="tpu_custom_call" | custom-call | tf_op jit(solution)/shard_map/pallas_call | solution.py:496
  572.9 3.6 fusion.28
  583.5 14.0 %pad_maximum_fusion = bf16[2048,4096]{0,1:T(8,128)(2,1)} fusion(bf16[1024,4096]{0,1:T(8,128)(2,1)} %fusion.17, bf16[1024,4096]{0,1:T(8,128)(2,1)} %fusion.25), kind=kLoop, calls=%fused_computation | loop fusion | flops 33554432 | bytes 33554432 | tf_op jit(solution)/shard_map/concatenate | solution.py:621
  597.5 20.6 %copy.42 = bf16[2048,4096]{1,0:T(8,128)(2,1)} copy(bf16[2048,4096]{0,1:T(8,128)(2,1)} %pad_maximum_fusion) | data formatting | bytes 33554432
  619.7 7.6 convolution_convert_fusion
  627.4 4.9 convolution_convert_fusion.2
  632.3 4.9 convolution_convert_fusion.1
  637.3 4.9 convolution_convert_fusion.3
  642.2 72.5 %maximum_maximum_fusion = bf16[2048,4096]{1,0:T(8,128)(2,1)} fusion(bf16[1024,2048]{1,0:T(8,128)(2,1)S(1)} %convolution_convert_fusion, bf16[1024,2048]{1,0:T(8,128)(2,1)S(1)} %convolution_convert_fusion.1, bf16[1024,2048]{1,0:T(8,128)(2,1)S(1)} %convolution_convert_fusion.2, bf16[1024,2048]{1,0:T(8,128)(2,1)S(1)} %convolution_convert_fusion.3), kind=kLoop, calls=%fused_computation.1 | loop fusion | flops 67108864 | bytes 33554432 | tf_op jit(solution)/shard_map/concatenate | solution.py:621
  721.0 4.7 fusion.35
  725.7 2.7 fusion.39
  731.0 3.3 fusion.36
  734.3 3.3 fusion.37
  737.7 6.6 add_convert_fusion.3
  744.3 2.9 fusion.34
  750.6 4.3 collective-permute-done.8
  770.1 15.0 %collective-permute-done.11 = f32[136,128]{1,0:T(8,128)S(1)} collective-permute-done((f32[136,128]{1,0:T(8,128)S(1)}, f32[136,128]{1,0:T(8,128)S(1)}, u32[]{:S(2)}, u32[]{:S(2)}) %collective-permute-start.11) | collective-permute-done | bytes 69664 | tf_op jit(solution)/shard_map/ppermute | solution.py:558
  787.6 3.2 maximum_select_fusion.2
  790.9 3.2 maximum_select_fusion.4
  794.1 12.2 %collective-permute-done.6 = bf16[1,512,1024]{2,1,0:T(8,128)(2,1)} collective-permute-done((bf16[1,512,1024]{2,1,0:T(8,128)(2,1)}, bf16[1,512,1024]{2,1,0:T(8,128)(2,1)}, u32[]{:S(2)}, u32[]{:S(2)}) %collective-permute-start.6) | collective-permute-done | bytes 1048608 | tf_op jit(solution)/shard_map/ppermute | solution.py:558
  806.3 3.2 maximum_select_fusion.5
  812.4 178.6 %reduce-scatter.5.cloned.1.call-done = bf16[64,4096]{1,0:T(8,128)(2,1)} async-done(((bf16[2048,4096]{1,0:T(8,128)(2,1)}), bf16[64,4096]{1,0:T(8,128)(2,1)}) %reduce-scatter.5.cloned.1.call-update) | async-done | bytes 524304 | tf_op jit(solution)/shard_map/reduce_scatter | solution.py:622
  (327 shorter events, 96.7 us)
Async XLA Ops:
  7.2 11.6 %copy-start.25 = (bf16[2,512,1024]{2,1,0:T(8,128)(2,1)S(1)}, bf16[2,512,1024]{2,1,0:T(8,128)(2,1)}, u32[]{:S(2)}) copy-start(bf16[2,512,1024]{2,1,0:T(8,128)(2,1)} %param.13) | copy-start | bytes 6291460
  7.2 108.1 %all-gather.4.cloned.1.call-start = ((), (), s32[]{:S(2)}) async-start(), calls=%async_computation.2 | async-start | bytes 8650752 | tf_op jit(solution)/shard_map/all_gather | solution.py:617
  9.9 184.4 %all-gather.6.cloned.1.call-start = ((), (), s32[]{:S(2)}) async-start(), calls=%async_computation.3 | async-start | bytes 8650752 | tf_op jit(solution)/shard_map/all_gather | solution.py:617
  12.5 298.3 %all-gather.8.cloned.1.call-start = ((), (), s32[]{:S(2)}) async-start(), calls=%async_computation.4 | async-start | bytes 17301504 | tf_op jit(solution)/shard_map/all_gather | solution.py:617
  14.4 795.0 %reduce-scatter.7.cloned.1.call-start = ((), (), s32[]{:S(2)}) async-start(), calls=%async_computation.6 | async-start | bytes 17301504
  15.9 11.2 %collective-permute-start.1 = (bf16[4096]{0:T(1024)(128)(2,1)S(1)}, bf16[4096]{0:T(1024)(128)(2,1)S(1)}, u32[]{:S(2)}, u32[]{:S(2)}) collective-permute-start(bf16[4096]{0:T(1024)(128)(2,1)S(1)} %constant_dynamic-update-slice_fusion.2), channel_id=1, source_target_pairs={{0,1},{1,0},{2,3},{3,2},{4,5},{5,4},{6,7},{7,6},{8,9},{9,8},{10,11... | collective-permute-start | bytes 24584 | tf_op jit(solution)/shard_map/ppermute | solution.py:558
  18.8 4.7 copy-start.27
  20.0 138.4 %copy-start.28 = (bf16[512,1024]{1,0:T(8,128)(2,1)}, bf16[512,1024]{1,0:T(8,128)(2,1)S(1)}, u32[]{:S(2)}) copy-start(bf16[512,1024]{1,0:T(8,128)(2,1)S(1)} %get-tuple-element.123) | copy-start | bytes 3145732
  20.0 5.8 copy-start.55
  20.0 6.5 copy-start.56
  20.0 95.3 %copy-start.76 = (f32[1536]{0:T(1024)S(1)}, f32[1536]{0:T(1024)}, u32[]{:S(2)}) copy-start(f32[1536]{0:T(1024)} %constant.82.clone.1) | copy-start | bytes 18436
  20.0 32.2 %collective-permute-start = (bf16[512,1024]{1,0:T(8,128)(2,1)}, bf16[512,1024]{1,0:T(8,128)(2,1)S(1)}, u32[]{:S(2)}, u32[]{:S(2)}) collective-permute-start(bf16[512,1024]{1,0:T(8,128)(2,1)} %get-tuple-element.124), channel_id=1, source_target_pairs={{0,1},{1,0},{2,3},{3,2},{4,5},{5,4},{6,7},{7,6},{8,9},{9,8},{10,11... | collective-permute-start | bytes 3145736 | tf_op jit(solution)/shard_map/ppermute | solution.py:558
  22.3 175.6 %collective-permute-start.2 = (bf16[512,1024]{1,0:T(8,128)(2,1)}, bf16[512,1024]{1,0:T(8,128)(2,1)}, u32[]{:S(2)}, u32[]{:S(2)}) collective-permute-start(bf16[512,1024]{1,0:T(8,128)(2,1)} %get-tuple-element.122), channel_id=1, source_target_pairs={{0,1},{1,0},{2,3},{3,2},{4,5},{5,4},{6,7},{7,6},{8,9},{9,8},{10,11... | collective-permute-start | bytes 3145736 | tf_op jit(solution)/shard_map/ppermute | solution.py:558
  25.1 333.7 %collective-permute-start.4 = (bf16[512,1024]{1,0:T(8,128)(2,1)}, bf16[512,1024]{1,0:T(8,128)(2,1)}, u32[]{:S(2)}, u32[]{:S(2)}) collective-permute-start(bf16[512,1024]{1,0:T(8,128)(2,1)} %get-tuple-element.117), channel_id=1, source_target_pairs={{0,1},{1,0},{2,3},{3,2},{4,5},{5,4},{6,7},{7,6},{8,9},{9,8},{10,11... | collective-permute-start | bytes 3145736 | tf_op jit(solution)/shard_map/ppermute | solution.py:558
  27.0 224.9 %copy-start.52 = (f32[1,1024]{1,0:T(1,128)}, f32[1,1024]{1,0:T(1,128)S(1)}, u32[]{:S(2)}) copy-start(f32[1,1024]{1,0:T(1,128)S(1)} %get-tuple-element.149) | copy-start | bytes 12292
  52.1 106.2 %copy-start.66 = (bf16[512,1024]{1,0:T(8,128)(2,1)}, bf16[512,1024]{1,0:T(8,128)(2,1)S(1)}, u32[]{:S(2)}) copy-start(bf16[512,1024]{1,0:T(8,128)(2,1)S(1)} %collective-permute-done) | copy-start | bytes 3145732
  143.8 12.0 %copy-start.44 = (bf16[1024,512]{1,0:T(8,128)(2,1)S(1)}, bf16[1024,512]{1,0:T(8,128)(2,1)}, u32[]{:S(2)}) copy-start(bf16[1024,512]{1,0:T(8,128)(2,1)} %get-tuple-element.33.o_ref) | copy-start | bytes 3145732
  161.8 90.1 %copy-start.48 = (f32[1024]{0:T(1024)}, f32[1024]{0:T(1024)S(1)}, u32[]{:S(2)}) copy-start(f32[1024]{0:T(1024)S(1)} %broadcast_multiply_fusion.8) | copy-start | bytes 12292
  162.4 89.5 %copy-start.50 = (f32[1024]{0:T(1024)}, f32[1024]{0:T(1024)S(1)}, u32[]{:S(2)}) copy-start(f32[1024]{0:T(1024)S(1)} %add_rsqrt_fusion.2) | copy-start | bytes 12292
  164.5 56.9 %copy-start.21 = (bf16[1024,1024]{1,0:T(8,128)(2,1)}, bf16[1024,1024]{1,0:T(8,128)(2,1)S(1)}, u32[]{:S(2)}) copy-start(bf16[1024,1024]{1,0:T(8,128)(2,1)S(1)} %fusion.7) | copy-start | bytes 6291460
  231.2 18.0 %copy-start.32 = (bf16[1024,512]{1,0:T(8,128)(2,1)S(1)}, bf16[1024,512]{1,0:T(8,128)(2,1)}, u32[]{:S(2)}) copy-start(bf16[1024,512]{1,0:T(8,128)(2,1)} %get-tuple-element.35.o_ref) | copy-start | bytes 3145732
  257.9 68.2 %copy-start.19 = (bf16[1024,1024]{1,0:T(8,128)(2,1)}, bf16[1024,1024]{1,0:T(8,128)(2,1)S(1)}, u32[]{:S(2)}) copy-start(bf16[1024,1024]{1,0:T(8,128)(2,1)S(1)} %fusion.8) | copy-start | bytes 6291460
  326.1 24.7 %copy-start.77 = (bf16[1024,2048]{1,0:T(8,128)(2,1)}, bf16[1024,2048]{1,0:T(8,128)(2,1)S(1)}, u32[]{:S(2)}) copy-start(bf16[1024,2048]{1,0:T(8,128)(2,1)S(1)} %get-tuple-element.158) | copy-start | bytes 12582916
  342.6 8.2 copy-start.78
  342.6 8.2 copy-start.6
  358.8 6.0 copy-start.57
  371.1 17.6 %slice-start.2 = ((s8[8388608]{0:T(1024)(128)(4,1)}), s8[4194304]{0:T(1024)(128)(4,1)S(1)}, s32[]{:S(2)}) async-start(s8[8388608]{0:T(1024)(128)(4,1)} %bitcast.340), calls=%async_computation.9 | async-start | bytes 8388608
  371.4 17.3 %copy-start.23 = (bf16[1024,1024]{1,0:T(8,128)(2,1)}, bf16[1024,1024]{1,0:T(8,128)(2,1)S(1)}, u32[]{:S(2)}) copy-start(bf16[1024,1024]{1,0:T(8,128)(2,1)S(1)} %convert_element_type.157) | copy-start | bytes 6291460
  371.4 17.3 %slice-start.3 = ((s8[8388608]{0:T(1024)(128)(4,1)}), s8[4194304]{0:T(1024)(128)(4,1)S(1)}, s32[]{:S(2)}) async-start(s8[8388608]{0:T(1024)(128)(4,1)} %bitcast.340), calls=%async_computation.10 | async-start | bytes 8388608
  388.7 25.8 %copy-start.80 = (bf16[1024,2048]{1,0:T(8,128)(2,1)}, bf16[1024,2048]{1,0:T(8,128)(2,1)S(1)}, u32[]{:S(2)}) copy-start(bf16[1024,2048]{1,0:T(8,128)(2,1)S(1)} %get-tuple-element.165) | copy-start | bytes 12582916
  404.7 9.8 copy-start.82
  426.5 4.6 copy-start.7
  463.0 24.0 %copy-start.2 = (f32[1024,1024]{1,0:T(8,128)S(1)}, f32[1024,1024]{1,0:T(8,128)}, u32[]{:S(2)}) copy-start(f32[1024,1024]{1,0:T(8,128)} %copy-done) | copy-start | bytes 12582916
  463.0 24.0 %copy-start.49 = (f32[1024]{0:T(1024)S(1)}, f32[1024]{0:T(1024)}, u32[]{:S(2)}) copy-start(f32[1024]{0:T(1024)} %copy-done.48) | copy-start | bytes 12292
  463.0 24.0 %copy-start.51 = (f32[1024]{0:T(1024)S(1)}, f32[1024]{0:T(1024)}, u32[]{:S(2)}) copy-start(f32[1024]{0:T(1024)} %copy-done.50) | copy-start | bytes 12292
  463.1 24.0 %copy-start.53 = (f32[1,1024]{1,0:T(1,128)S(1)}, f32[1,1024]{1,0:T(1,128)}, u32[]{:S(2)}) copy-start(f32[1,1024]{1,0:T(1,128)} %copy-done.52) | copy-start | bytes 12292
  495.0 4.6 copy-start.3
  511.8 4.0 copy-start.35
  518.1 16.9 %copy-start.29 = (bf16[512,1024]{1,0:T(8,128)(2,1)S(1)}, bf16[512,1024]{1,0:T(8,128)(2,1)}, u32[]{:S(2)}) copy-start(bf16[512,1024]{1,0:T(8,128)(2,1)} %copy-done.28) | copy-start | bytes 3145732
  518.1 16.9 %copy-start.67 = (bf16[512,1024]{1,0:T(8,128)(2,1)S(1)}, bf16[512,1024]{1,0:T(8,128)(2,1)}, u32[]{:S(2)}) copy-start(bf16[512,1024]{1,0:T(8,128)(2,1)} %copy-done.66) | copy-start | bytes 3145732
  545.7 4.0 copy-start.36
  618.2 372.9 %reduce-scatter.5.cloned.1.call-start = ((), (), s32[]{:S(2)}) async-start(), calls=%async_computation.5 | async-start | bytes 17301504 | tf_op jit(solution)/shard_map/reduce_scatter | solution.py:622
  619.7 7.6 copy-start.79
  627.4 4.9 copy-start.20
  627.4 4.9 copy-start.81
  632.3 4.9 copy-start.83
  714.7 4.0 copy-start.63
  714.8 4.0 copy-start.16
  714.8 4.3 copy-start.40
  714.8 4.5 copy-start.11
  714.8 4.7 copy-start.37
  717.5 70.1 %collective-permute-start.3 = (bf16[1,512,1024]{2,1,0:T(8,128)(2,1)}, bf16[1,512,1024]{2,1,0:T(8,128)(2,1)}, u32[]{:S(2)}, u32[]{:S(2)}) collective-permute-start(bf16[1,512,1024]{2,1,0:T(8,128)(2,1)} %get-tuple-element.120), channel_id=1, source_target_pairs={{0,1},{1,0},{2,3},{3,2},{4,5},{5,4},{6,7},{7,6},{8,9},{9,8},{10,11... | collective-permute-start | bytes 3145736 | tf_op jit(solution)/shard_map/ppermute | solution.py:558
  720.9 4.8 copy-start.75
  720.9 26.3 %collective-permute-start.7 = (f32[136,128]{1,0:T(8,128)S(1)}, f32[136,128]{1,0:T(8,128)S(1)}, u32[]{:S(2)}, u32[]{:S(2)}) collective-permute-start(f32[136,128]{1,0:T(8,128)S(1)} %bitcast.267), channel_id=1, source_target_pairs={{0,2},{2,0},{4,6},{6,4},{8,10},{10,8},{12,14},{14,12},{16,18},{18,... | collective-permute-start | bytes 208904 | tf_op jit(solution)/shard_map/ppermute | solution.py:586
  721.0 7.4 slice-start
  747.3 7.7 collective-permute-start.8
  748.0 13.9 %copy-start.17 = (f32[1024,1024]{1,0:T(8,128)S(1)}, f32[1024,1024]{1,0:T(8,128)}, u32[]{:S(2)}) copy-start(f32[1024,1024]{1,0:T(8,128)} %fusion.35) | copy-start | bytes 12582916
  750.6 11.2 %copy-start.12 = (bf16[1024,512]{1,0:T(8,128)(2,1)S(1)}, bf16[1024,512]{1,0:T(8,128)(2,1)}, u32[]{:S(2)}) copy-start(bf16[1024,512]{1,0:T(8,128)(2,1)} %get-tuple-element.52) | copy-start | bytes 3145732
  755.0 4.7 collective-permute-start.9
  757.4 33.5 %collective-permute-start.5 = (bf16[1,512,1024]{2,1,0:T(8,128)(2,1)}, bf16[1,512,1024]{2,1,0:T(8,128)(2,1)}, u32[]{:S(2)}, u32[]{:S(2)}) collective-permute-start(bf16[1,512,1024]{2,1,0:T(8,128)(2,1)} %get-tuple-element.116), channel_id=1, source_target_pairs={{0,1},{1,0},{2,3},{3,2},{4,5},{5,4},{6,7},{7,6},{8,9},{9,8},{10,11... | collective-permute-start | bytes 3145736 | tf_op jit(solution)/shard_map/ppermute | solution.py:558
  759.7 7.1 collective-permute-start.10
  766.8 18.3 %collective-permute-start.11 = (f32[136,128]{1,0:T(8,128)S(1)}, f32[136,128]{1,0:T(8,128)S(1)}, u32[]{:S(2)}, u32[]{:S(2)}) collective-permute-start(f32[136,128]{1,0:T(8,128)S(1)} %add.396), channel_id=1, source_target_pairs={{0,1},{1,0},{2,3},{3,2},{4,5},{5,4},{6,7},{7,6},{8,9},{9,8},{10,11... | collective-permute-start | bytes 208904 | tf_op jit(solution)/shard_map/ppermute | solution.py:558
  769.0 37.3 %collective-permute-start.6 = (bf16[1,512,1024]{2,1,0:T(8,128)(2,1)}, bf16[1,512,1024]{2,1,0:T(8,128)(2,1)}, u32[]{:S(2)}, u32[]{:S(2)}) collective-permute-start(bf16[1,512,1024]{2,1,0:T(8,128)(2,1)} %get-tuple-element.114), channel_id=1, source_target_pairs={{0,1},{1,0},{2,3},{3,2},{4,5},{5,4},{6,7},{7,6},{8,9},{9,8},{10,11... | collective-permute-start | bytes 3145736 | tf_op jit(solution)/shard_map/ppermute | solution.py:558
  812.4 182.7 %copy-start.18 = (f32[64,1536]{0,1:T(8,128)S(1)}, f32[64,1536]{0,1:T(8,128)}, u32[]{:S(2)}) copy-start(f32[64,1536]{0,1:T(8,128)} %get-tuple-element.126) | copy-start | bytes 1179652
  (41 other events, 106.1 us)
Sparse Core Ops, SparseCore 0:
  11.4 103.7 all-gather.3
  118.7 75.5 all-gather.5
  197.8 112.9 all-gather.7
  618.3 183.5 reduce-scatter.6
  804.1 186.9 reduce-scatter.4

commit v2 on v1

--- a/solution.py
+++ b/solution.py
@@ -504,6 +504,288 @@
     )(q,k,v,o,do,lse)
 
 
+MESH = pl.DeviceIdType.MESH
+LINKS = ("z1", "z2", "y", "x", "c")
+
+
+def partners():
+    t = lax.axis_index("tp")
+    f = lax.axis_index("fsdp")
+    z, y, c = f // 4, (f // 2) % 2, f % 2
+
+    def at(z_, y_, c_, t_):
+        return (z_ * 4 + y_ * 2 + c_, t_)
+
+    ids = dict(
+        z1=at(z + 1 - 2 * (z % 2), y, c, t),
+        z2=at((z + 2) % 4, y, c, t),
+        y=at(z, 1 - y, c, t),
+        x=at(z, y, c, 1 - t),
+        c=at(z, y, 1 - c, t),
+    )
+    return (t, z, y, c), ids
+
+
+def greet(ids):
+    barrier = pltpu.get_barrier_semaphore()
+    for name in LINKS:
+        pl.semaphore_signal(barrier, inc=1, device_id=ids[name], device_id_type=MESH)
+    pl.semaphore_wait(barrier, len(LINKS))
+
+
+def pipeline(chunks, stages, begin):
+    started = {}
+    for step in range(chunks + stages):
+        for s in range(stages, -1, -1):
+            k = step - s
+            if 0 <= k < chunks:
+                if s > 0:
+                    for copy in started[k, s - 1]:
+                        copy.wait_recv()
+                started[k, s] = begin(k, s)
+    for copies in started.values():
+        for copy in copies:
+            copy.wait_send()
+
+
+def gather_kernel(shard_ref, w_ref, send, recv, own, *, cw, chunks):
+    (t, z, y, c), ids = partners()
+    mine = pltpu.make_async_copy(shard_ref, w_ref.at[t, z, y, c], own)
+    mine.start()
+    greet(ids)
+    pair = (z // 2) * 2
+    h = cw // 2
+
+    def begin(k, s):
+        both, a, b = pl.ds(k * cw, cw), pl.ds(k * cw, h), pl.ds(k * cw + h, h)
+        if s == 0:
+            moves = [(shard_ref.at[:, both], w_ref.at[t, z, y, c, :, both], "z1", 0)]
+        elif s == 1:
+            if k == 0:
+                mine.wait()
+            r = w_ref.at[t, pl.ds(pair, 2), y, c, :, both]
+            moves = [(r, r, "z2", 1)]
+        elif s == 2:
+            ra, rb = w_ref.at[t, :, y, c, :, a], w_ref.at[t, :, y, c, :, b]
+            moves = [(ra, ra, "y", 2), (rb, rb, "x", 3)]
+        elif s == 3:
+            ra, rb = w_ref.at[t, :, :, c, :, a], w_ref.at[:, :, y, c, :, b]
+            moves = [(ra, ra, "x", 4), (rb, rb, "y", 5)]
+        elif s == 4:
+            r = w_ref.at[:, :, :, c, :, both]
+            moves = [(r, r, "c", 6)]
+        else:
+            moves = []
+        copies = []
+        for src, dst, to, j in moves:
+            copy = pltpu.make_async_remote_copy(
+                src_ref=src,
+                dst_ref=dst,
+                send_sem=send.at[k, j],
+                recv_sem=recv.at[k, j],
+                device_id=ids[to],
+                device_id_type=MESH,
+            )
+            copy.start()
+            copies.append(copy)
+        return copies
+
+    pipeline(chunks, 5, begin)
+
+
+def gather_weights(shard, cid, chunks):
+    rows, cols = shard.shape
+    whole = pl.pallas_call(
+        functools.partial(gather_kernel, cw=cols // chunks, chunks=chunks),
+        in_specs=[pl.BlockSpec(memory_space=pltpu.VMEM)],
+        out_specs=pl.BlockSpec(memory_space=pl.ANY),
+        out_shape=jax.ShapeDtypeStruct((2, 4, 2, 2, rows, cols), shard.dtype),
+        scratch_shapes=[
+            pltpu.SemaphoreType.DMA((chunks, 7)),
+            pltpu.SemaphoreType.DMA((chunks, 7)),
+            pltpu.SemaphoreType.DMA,
+        ],
+        compiler_params=pltpu.CompilerParams(collective_id=cid, has_side_effects=True),
+        cost_estimate=pl.CostEstimate(
+            flops=0, bytes_accessed=32 * rows * cols * 20, transcendentals=0
+        ),
+    )(shard)
+    return whole.reshape(2, 16 * rows, cols)
+
+
+def scatter_kernel(*refs, chunks):
+    g_refs, refs = refs[: 2 * chunks], refs[2 * chunks :]
+    small_ref, out_ref, small_out, own, r1, s2, r2, k2, s3, r3, k3, s4, r4, k4, s5, r5 = refs[:16]
+    sm, rm, send, recv, own_sem, small_send, small_recv = refs[16:]
+    (t, z, y, c), ids = partners()
+    pair = (z // 2) * 2
+    away = 2 - pair
+    other = 1 - z % 2
+    rows = own.shape[3]
+    cw = own.shape[4] // chunks
+    h = cw // 2
+
+    def loc(k, half):
+        return pltpu.make_async_copy(
+            g_refs[2 * k + half].at[:, :, c],
+            own.at[half, :, :, :, pl.ds(k * cw, cw)],
+            own_sem.at[k, half],
+        )
+
+    for k in range(chunks):
+        loc(k, 0).start()
+        loc(k, 1).start()
+    greet(ids)
+
+    def go(k, j, src, dst, to):
+        copy = pltpu.make_async_remote_copy(
+            src_ref=src,
+            dst_ref=dst,
+            send_sem=send.at[k, j],
+            recv_sem=recv.at[k, j],
+            device_id=ids[to],
+            device_id_type=MESH,
+        )
+        copy.start()
+        return copy
+
+    def small_go(j):
+        copy = pltpu.make_async_remote_copy(
+            src_ref=sm.at[j],
+            dst_ref=rm.at[j],
+            send_sem=small_send.at[j],
+            recv_sem=small_recv.at[j],
+            device_id=ids[("c", "x", "y", "z2", "z1")[j]],
+            device_id_type=MESH,
+        )
+        copy.start()
+        return copy
+
+    def up(v):
+        return v.astype(f32)
+
+    def begin(k, s):
+        ca = slice(k * cw, k * cw + h)
+        cb = slice(k * cw + h, (k + 1) * cw)
+        if s == 0:
+            cols = pl.ds(k * cw, cw)
+            return [
+                go(k, 7 * half, g_refs[2 * k + half].at[:, :, 1 - c], r1.at[half, :, :, :, cols], "c")
+                for half in (0, 1)
+            ]
+        if s == 1:
+            loc(k, 0).wait()
+            loc(k, 1).wait()
+            shape = (8, rows, h)
+            sent = up(own[1 - t, :, :, :, ca]) + up(r1[1 - t, :, :, :, ca])
+            s2[k, 0] = sent.astype(bf16).reshape(shape)
+            da = go(k, 1, s2.at[k, 0], r2.at[k, 0], "x")
+            sent = up(own[:, :, 1 - y, :, cb]) + up(r1[:, :, 1 - y, :, cb])
+            s2[k, 1] = sent.astype(bf16).reshape(shape)
+            db = go(k, 2, s2.at[k, 1], r2.at[k, 1], "y")
+            k2[k, 0] = (up(own[t, :, :, :, ca]) + up(r1[t, :, :, :, ca])).reshape(shape)
+            k2[k, 1] = (up(own[:, :, y, :, cb]) + up(r1[:, :, y, :, cb])).reshape(shape)
+            return [da, db]
+        if s == 2:
+            for i in range(4):
+                j = 2 * i + 1 - y
+                s3[k, 0, i] = (k2[k, 0, j] + up(r2[k, 0, j])).astype(bf16)
+            da = go(k, 3, s3.at[k, 0], r3.at[k, 0], "y")
+            for i in range(4):
+                j = 4 * (1 - t) + i
+                s3[k, 1, i] = (k2[k, 1, j] + up(r2[k, 1, j])).astype(bf16)
+            db = go(k, 4, s3.at[k, 1], r3.at[k, 1], "x")
+            for i in range(4):
+                k3[k, 0, i] = k2[k, 0, 2 * i + y] + up(r2[k, 0, 2 * i + y])
+                k3[k, 1, i] = k2[k, 1, 4 * t + i] + up(r2[k, 1, 4 * t + i])
+            return [da, db]
+        if s == 3:
+            for j in range(2):
+                for i in range(2):
+                    s4[k, j, i] = (k3[k, j, away + i] + up(r3[k, j, away + i])).astype(bf16)
+            d = go(k, 5, s4.at[k], r4.at[k], "z2")
+            for j in range(2):
+                for i in range(2):
+                    k4[k, j, i] = k3[k, j, pair + i] + up(r3[k, j, pair + i])
+            return [d]
+        if s == 4:
+            for j in range(2):
+                s5[k, j] = (k4[k, j, other] + up(r4[k, j, other])).astype(bf16)
+            return [go(k, 6, s5.at[k], r5.at[k], "z1")]
+        for j in range(2):
+            mine = k4[k, j, z % 2] + up(r4[k, j, z % 2]) + up(r5[k, j])
+            out_ref[:, k * cw + j * h : k * cw + (j + 1) * h] = mine
+        return []
+
+    smalls = []
+
+    def begin_with_small(k, s):
+        if k == 0:
+            if s == 0:
+                sm[0] = small_ref[...]
+            else:
+                smalls[s - 1].wait_recv()
+                total = sm[s - 1] + rm[s - 1]
+                if s < 5:
+                    sm[s] = total
+                else:
+                    small_out[...] = total
+            if s < 5:
+                smalls.append(small_go(s))
+        return begin(k, s)
+
+    pipeline(chunks, 5, begin_with_small)
+    for copy in smalls:
+        copy.wait_send()
+
+
+def scatter_grads(pairs, small, cid):
+    chunks = len(pairs)
+    width, cw = pairs[0][0].shape
+    rows, h, cols = width // 16, cw // 2, cw * chunks
+    V = pltpu.VMEM
+    dma = pltpu.SemaphoreType.DMA
+    flat = [g.reshape(4, 2, 2, rows, cw) for pair in pairs for g in pair]
+    whole = pl.BlockSpec(memory_space=pltpu.VMEM)
+    return pl.pallas_call(
+        functools.partial(scatter_kernel, chunks=chunks),
+        in_specs=[pl.BlockSpec(memory_space=pl.ANY)] * len(flat) + [whole],
+        out_specs=[whole, whole],
+        out_shape=[
+            jax.ShapeDtypeStruct((rows, cols), f32),
+            jax.ShapeDtypeStruct(small.shape, f32),
+        ],
+        scratch_shapes=[
+            V((2, 4, 2, rows, cols), bf16),
+            V((2, 4, 2, rows, cols), bf16),
+            V((chunks, 2, 8, rows, h), bf16),
+            V((chunks, 2, 8, rows, h), bf16),
+            V((chunks, 2, 8, rows, h), f32),
+            V((chunks, 2, 4, rows, h), bf16),
+            V((chunks, 2, 4, rows, h), bf16),
+            V((chunks, 2, 4, rows, h), f32),
+            V((chunks, 2, 2, rows, h), bf16),
+            V((chunks, 2, 2, rows, h), bf16),
+            V((chunks, 2, 2, rows, h), f32),
+            V((chunks, 2, rows, h), bf16),
+            V((chunks, 2, rows, h), bf16),
+            V((5,) + small.shape, f32),
+            V((5,) + small.shape, f32),
+            dma((chunks, 8)),
+            dma((chunks, 8)),
+            dma((chunks, 2)),
+            dma((5,)),
+            dma((5,)),
+        ],
+        compiler_params=pltpu.CompilerParams(
+            collective_id=cid, has_side_effects=True, vmem_limit_bytes=60 * 2**20
+        ),
+        cost_estimate=pl.CostEstimate(
+            flops=0, bytes_accessed=32 * rows * cols * 20, transcendentals=0
+        ),
+    )(*flat, small)
+
+
 ERFC_SLOPE = 0.44
 ERFC_COEFS = (
     0.12411048270139104,
@@ -529,6 +811,100 @@
     return u * phi, phi + u * (e * 0.3989422804014327)
 
 
+def up_kernel(x_ref, w_ref, b_ref, act_ref, slope_ref):
+    for i in range(4):
+        rows = slice(256 * i, 256 * (i + 1))
+        u = lax.dot_general(x_ref[rows, :], w_ref[0], NN, preferred_element_type=f32) + b_ref[...]
+        g, d = gelu_and_slope(u)
+        act_ref[rows, :] = g.astype(bf16)
+        slope_ref[rows, :] = d.astype(bf16)
+
+
+def hidden_units(x, w, bias, tile):
+    rows, width = x.shape
+    units = w.shape[2] // 2
+    per = units // tile
+    col = pl.BlockSpec((rows, tile), lambda j: (0, j))
+    return pl.pallas_call(
+        up_kernel,
+        grid=(2 * per,),
+        in_specs=[
+            pl.BlockSpec((rows, width), lambda j: (0, 0)),
+            pl.BlockSpec((1, width, tile), lambda j: (j // per, 0, j % per)),
+            pl.BlockSpec((1, tile), lambda j: (0, j)),
+        ],
+        out_specs=[col, col],
+        out_shape=[jax.ShapeDtypeStruct((rows, 2 * units), bf16)] * 2,
+        compiler_params=pltpu.CompilerParams(vmem_limit_bytes=56 * 2**20),
+    )(x, w, bias)
+
+
+def units_back_kernel(e_ref, w_ref, slope_ref, du_ref, sum_ref):
+    total = 0.0
+    for i in range(4):
+        rows = slice(256 * i, 256 * (i + 1))
+        d = lax.dot_general(e_ref[rows, :], w_ref[0], NN, preferred_element_type=f32)
+        du = (d * slope_ref[rows, :].astype(f32)).astype(bf16)
+        du_ref[rows, :] = du
+        total = total + jnp.sum(du.astype(f32), 0, keepdims=True)
+    sum_ref[...] = total
+
+
+def hidden_units_back(e, w, slope, tile):
+    rows, width = e.shape
+    units = w.shape[2] // 2
+    per = units // tile
+    col = pl.BlockSpec((rows, tile), lambda j: (0, j))
+    return pl.pallas_call(
+        units_back_kernel,
+        grid=(2 * per,),
+        in_specs=[
+            pl.BlockSpec((rows, width), lambda j: (0, 0)),
+            pl.BlockSpec((1, width, tile), lambda j: (j // per, 0, per + j % per)),
+            col,
+        ],
+        out_specs=[col, pl.BlockSpec((1, tile), lambda j: (0, j))],
+        out_shape=[
+            jax.ShapeDtypeStruct((rows, 2 * units), bf16),
+            jax.ShapeDtypeStruct((1, 2 * units), f32),
+        ],
+        compiler_params=pltpu.CompilerParams(vmem_limit_bytes=56 * 2**20),
+    )(e, w, slope)
+
+
+def weight_grads_kernel(a_ref,b_ref,da_ref,db_ref,out_ref,at,bt,*,tiles):
+    j=pl.program_id(0)
+    @pl.when(j==0)
+    def _():
+        at[...]=a_ref[...].T
+        bt[...]=b_ref[...].T
+    kind=(j//tiles)%2
+    @pl.when(kind==0)
+    def _():
+        out_ref[0]=lax.dot_general(at[...],da_ref[...],NN,preferred_element_type=f32).astype(bf16)
+    @pl.when(kind==1)
+    def _():
+        out_ref[0]=lax.dot_general(bt[...],db_ref[...],NN,preferred_element_type=f32).astype(bf16)
+
+def weight_grads(a,b,da,db,tile=512):
+    rows,width=a.shape; half=da.shape[1]//2; tiles=half//tile
+    whole=pl.BlockSpec((rows,width),lambda j:(0,0))
+    t=lambda j: j//(2*tiles)
+    kind=lambda j:(j//tiles)%2
+    i=lambda j: j%tiles
+    return pl.pallas_call(
+        functools.partial(weight_grads_kernel,tiles=tiles),
+        grid=(4*tiles,),
+        in_specs=[whole,whole,
+          pl.BlockSpec((rows,tile),lambda j:(0,t(j)*tiles+jnp.where(kind(j)==0,i(j),tiles-1))),
+          pl.BlockSpec((rows,tile),lambda j:(0,t(j)*tiles+jnp.where(kind(j)==1,i(j),0)))],
+        out_specs=pl.BlockSpec((1,width,tile),lambda j:(t(j),0,kind(j)*tiles+i(j))),
+        out_shape=jax.ShapeDtypeStruct((2,width,2*half),bf16),
+        scratch_shapes=[pltpu.VMEM((width,rows),bf16)]*2,
+        compiler_params=pltpu.CompilerParams(vmem_limit_bytes=56*2**20),
+    )(a,b,da,db)
+
+
 def nn(a, b):
     return lax.dot_general(a, b, NN, preferred_element_type=f32)
 
@@ -578,14 +954,6 @@
     own = lax.dynamic_index_in_dim(halves, place, 0, keepdims=True)
     away = lax.dynamic_index_in_dim(halves, 1 - place, 0, keepdims=True)
     return in_order(place, own, trade(away))
-
-
-def sum_everywhere(x, fsdp_count):
-    step = 1
-    while step < fsdp_count:
-        x = x + lax.ppermute(x, "fsdp", [(i, i ^ step) for i in range(fsdp_count)])
-        step *= 2
-    return x + trade(x)
 
 
 def whole_sequences(
@@ -604,7 +972,6 @@
     row_bias,
 ):
     place = lax.axis_index("tp")
-    fsdp_count = lax.axis_size("fsdp")
     width = layer_in.shape[2]
     cols = w_self_in.shape[2]
     units = w_up.shape[1]
@@ -613,20 +980,18 @@
     shifts = row_bias.astype(f32)
 
     def gather(*parts):
-        mine = jnp.concatenate(parts, 1) if len(parts) > 1 else parts[0]
+        mine = jnp.concatenate(parts, 1)
         both = lax.all_gather(mine, ("tp", "fsdp"), axis=0, tiled=True)
         return both.reshape(2, width, mine.shape[1])
-
-    def scatter(parts):
-        low = jnp.concatenate([p.astype(bf16) for p in parts], 0)
-        return lax.psum_scatter(low, ("tp", "fsdp"), scatter_dimension=0, tiled=True).astype(f32)
 
     small = jnp.concatenate([head_bias.reshape(-1), up_bias])
     small = in_order(place, small[None], trade(small)[None])
     hb = small[:, : 4 * cols].reshape(2, 4, cols).astype(f32)
     ub = small[:, 4 * cols :].astype(f32)
 
-    g_self = gather(w_self_in.reshape(shard, 3 * cols), w_self_out.T)
+    g_self = gather_weights(
+        jnp.concatenate([w_self_in.reshape(shard, 3 * cols), w_self_out.T], 1), 1, 4
+    )
     g_cross = gather(w_cross_in.reshape(shard, 3 * cols), w_cross_out.T)
     g_ffn = gather(w_up, w_down.T)
     c3 = 3 * cols
@@ -665,23 +1030,24 @@
     h2, n2, i2 = norm_rows(r2, gains[1], shifts[4])
     h2b = h2.astype(bf16)
 
-    act, slope = [], []
-    for t in halves:
-        g, d = gelu_and_slope(nn(h2b, g_ffn[t, :, :units]) + ub[t])
-        act.append(g.astype(bf16))
-        slope.append(d.astype(bf16))
-    r3 = h2 + (nt(act[0], g_ffn[0, :, units:]) + nt(act[1], g_ffn[1, :, units:])) + shifts[2]
+    act, slope = hidden_units(h2b, g_ffn, ub.reshape(1, 2 * units), 512)
+    r3 = (
+        h2
+        + (nt(act[:, :units], g_ffn[0, :, units:]) + nt(act[:, units:], g_ffn[1, :, units:]))
+        + shifts[2]
+    )
     h3, n3, i3 = norm_rows(r3, gains[2], shifts[5])
     mixed = to_pieces(h3.astype(bf16), place)
 
     dr3, gg3, gs3, gb3 = norm_rows_back(cot.astype(f32), n3, i3, gains[2])
     e3 = dr3.astype(bf16)
-    du = [(nn(e3, g_ffn[t, :, units:]) * slope[t].astype(f32)).astype(bf16) for t in halves]
-    s_ffn = scatter(
-        [jnp.concatenate([tn(h2b, du[t]), tn(e3, act[t])], 1) for t in halves]
-    )
-    gu = jnp.stack([jnp.sum(du[t].astype(f32), 0) for t in halves])
-    dh2 = dr3 + (nt(du[0], g_ffn[0, :, :units]) + nt(du[1], g_ffn[1, :, :units]))
+    du, gu = hidden_units_back(e3, g_ffn, slope, 512)
+    grad_ffn = weight_grads(h2b, e3, du, act, 1024)
+    grad_ffn, du = lax.optimization_barrier((grad_ffn, du))
+    s_ffn = lax.psum_scatter(
+        grad_ffn.reshape(2 * width, 2 * units), ("tp", "fsdp"), scatter_dimension=0, tiled=True
+    ).astype(f32)
+    dh2 = dr3 + (nt(du[:, :units], g_ffn[0, :, :units]) + nt(du[:, units:], g_ffn[1, :, :units]))
     dr2, gg2, gs2, gb2 = norm_rows_back(dh2, n2, i2, gains[1])
     e2 = dr2.astype(bf16)
 
@@ -692,11 +1058,12 @@
         dcq.append(a)
         dck.append(b)
         dcv.append(c)
-    grad_cross = [
-        jnp.concatenate(
-            [tn(h1b, dcq[t]), tn(mem, dck[t]), tn(mem, dcv[t]), tn(e2, ca[t])], 1
-        )
-        for t in halves
+    low = lambda v: v.astype(bf16)
+    grads = [
+        tuple(low(tn(h1b, dcq[t])) for t in halves),
+        tuple(low(tn(mem, dck[t])) for t in halves),
+        tuple(low(tn(mem, dcv[t])) for t in halves),
+        tuple(low(tn(e2, ca[t])) for t in halves),
     ]
     dmem = sum(
         nt(dck[t], g_cross[t, :, cols : 2 * cols]) + nt(dcv[t], g_cross[t, :, 2 * cols : c3])
@@ -715,11 +1082,12 @@
         dsq.append(a)
         dsk.append(b)
         dsv.append(c)
-    grad_self = [
-        jnp.concatenate([tn(x, dsq[t]), tn(x, dsk[t]), tn(x, dsv[t]), tn(e1, sa[t])], 1)
-        for t in halves
+    grads += [
+        tuple(low(tn(x, dsq[t])) for t in halves),
+        tuple(low(tn(x, dsk[t])) for t in halves),
+        tuple(low(tn(x, dsv[t])) for t in halves),
+        tuple(low(tn(e1, sa[t])) for t in halves),
     ]
-    s_att = scatter([jnp.concatenate([grad_cross[t], grad_self[t]], 1) for t in halves])
     dx = dr1 + sum(
         nt(dsq[t], g_self[t, :, :cols])
         + nt(dsk[t], g_self[t, :, cols : 2 * cols])
@@ -738,7 +1106,8 @@
             for v in (gh, gu, gg1, gg2, gg3, gb1, gb2, gb3, gs1, gs2, gs3)
         ]
     )
-    flat = sum_everywhere(flat.reshape(-1, 128), fsdp_count).reshape(-1)
+    s_att, flat = scatter_grads(grads, flat.reshape(-1, 128), 2)
+    flat = flat.reshape(-1)
     head_sum = lax.dynamic_index_in_dim(flat[: 8 * cols].reshape(2, 4, cols), place, 0, False)
     unit_sum = lax.dynamic_index_in_dim(
         flat[8 * cols : 8 * cols + 2 * units].reshape(2, units), place, 0, False
@@ -764,9 +1133,8 @@
 
 
 def on_device(layer_in, *rest):
-    fsdp_count = lax.axis_size("fsdp")
-    pair = lax.axis_size("tp") == 2 and layer_in.shape[0] == 2
-    if pair and fsdp_count & (fsdp_count - 1) == 0:
+    paired = lax.axis_size("tp") == 2 and layer_in.shape[0] == 2
+    if paired and lax.axis_size("fsdp") == 16:
         return whole_sequences(layer_in, *rest)
     return shared_sequences(layer_in, *rest)
 

time: 1020 us -> 759 us (0.74)
  waiting for transfers between devices: 385 us -> 0.07 us
  Pallas kernels: 141 us -> 444 us
  other arithmetic: 123 us -> 44.4 us
  matrix products: 275 us -> 202 us
  local copies, waits for them, and re-layouts: 53.3 us -> 34.5 us
    pallas_call x0 -> x5, Pallas kernels: none -> 302 us  [the longest x1 132 us: gather_weights(): pl.pallas_call(functools.partial(gather_kernel, cw=cols // chunks, chunks...]
    reduce_scatter x1, waiting for transfers between devices: 179 us -> 0.01 us  [whole_sequences(): lax.psum_scatter(grad_ffn.reshape(2 * width, 2 * units), ('tp', 'fsdp'),...]
    all_gather x3 -> x2, waiting for transfers between devices: 146 us -> 0.01 us  [gather(): both = lax.all_gather(mine, ('tp', 'fsdp'), axis=0, tiled=True)]
    concatenate x5 -> x3, other arithmetic: 91.5 us -> 4.14 us  [the longest x2 3.42 us: gather(): mine = jnp.concatenate(parts, 1)]
    dot_general x14 -> x10, matrix products: 116 us -> 50.8 us  [nn(): return lax.dot_general(a, b, NN, preferred_element_type=f32)]
    ppermute x8 -> x7, waiting for transfers between devices: 52.1 us -> 0.02 us  [trade(): return lax.ppermute(x, 'tp', [(0, 1), (1, 0)])]
    unnamed x196 -> x144, local copies, waits for them, and re-layouts: 35.3 us -> 8.18 us
    dot_general x20 -> x16, matrix products: 68.8 us -> 53.7 us  [tn(): lax.dot_general(a, b, (((0,), (0,)), ((), ())), preferred_element_type=f32)]
  transfers between devices with their start and end apart: 17 -> 10, of which waited for: 10 -> 0; matrix products, arithmetic and copies ran while one was open for 25% -> 34% of each run, Pallas kernels for 6% -> 54%
where the time goes in v2:
time: 759 us; the launch traced here: 749 us
  Pallas kernels  444 us (58%)
  matrix products  202 us (27%)
  other arithmetic  44.4 us (6%)
  local copies, waits for them, and re-layouts  34.5 us (5%)
  between operations  15.1 us (2%)
  starting transfers between devices  9.64 us (1%)
    pallas_call x1, Pallas kernels, gather_weights(): pl.pallas_call(functools.partial(gather_kernel, cw=cols // chunks, chunks...  132 us
    dot_general x20, matrix products, nt(): return lax.dot_general(a, b, NT, preferred_element_type=f32)  97.4 us
    pallas_call x1, Pallas kernels, scatter_grads(): pl.pallas_call(functools.partial(scatter_kernel, chunks=chunks), in_specs...  97.4 us
    pallas_call x4, Pallas kernels, att_bwd(): pl.pallas_call(functools.partial(att_bwd_kernel, bq=bq, causal=causal), g...  81.3 us
    pallas_call x4, Pallas kernels, att_fwd(): pl.pallas_call(functools.partial(att_fwd_kernel, bq=bq, causal=causal), g...  60.2 us
    dot_general x16, matrix products, tn(): lax.dot_general(a, b, (((0,), (0,)), ((), ())), preferred_element_type=f32)  53.7 us
    dot_general x10, matrix products, nn(): return lax.dot_general(a, b, NN, preferred_element_type=f32)  50.8 us
    pallas_call x1, Pallas kernels, hidden_units(): pl.pallas_call(up_kernel, grid=(2 * per,), in_specs=[pl.BlockSpec((rows,...  30.6 us
  transfers between devices with their start and end apart: 10, of which 0 were waited for; matrix products, arithmetic and copies ran while one was open for 34% of the time, Pallas kernels for 54%

profile of v2, /device:TPU:0, one launch (start us, length us, event | category | flops | bytes accessed | tf_op | source)
XLA Modules:
  0.0 749.4 jit_solution(4291300087244410999)
XLA Ops:
  13.3 3.0 collective-permute-start.1
  23.8 132.4 %shard_map.228 = bf16[2,4,2,2,64,2048]{5,4,3,2,1,0:T(8,128)(2,1)} custom-call(bf16[64,2048]{1,0:T(8,128)(2,1)} %pad_maximum_fusion.1.shard_ref), custom_call_target="tpu_custom_call" | custom-call | bytes 83886080 | tf_op jit(solution)/shard_map/pallas_call | solution.py:598
  157.1 7.7 %multiply_convert_fusion.q_ref.k_ref.v_ref = bf16[1024,1536]{1,0:T(8,128)(2,1)} fusion(bf16[2,1024,2048]{2,1,0:T(8,128)(2,1)} %bitcast.242, f32[1536]{0:T(1024)S(1)} %get-tuple-element.151, f32[1536]{0:T(1024)S(1)} %copy-done.60, bf16[512,1024]{1,0:T(8,128)(2,1)} %collective-permute-done, bf16[512,1024]{1,0:T(8,128)(2,1)S(1)} %get-tuple-element.124, pred[]{:T(512)S(6)} %eq.2), kind=kOutput, calls=%fused_computation.3 | convolution fusion | flops 3235381248 | bytes 8400897 | tf_op jit(solution)/shard_map/dot_general | solution.py:909
  164.7 11.9 %shard_map.230 = (bf16[1024,512]{1,0:T(8,128)(2,1)}, f32[4,2,1024]{2,1,0:T(2,128)}) custom-call(bf16[1024,1536]{1,0:T(8,128)(2,1)} %multiply_convert_fusion.q_ref.k_ref.v_ref, bf16[1024,1536]{1,0:T(8,128)(2,1)} %multiply_convert_fusion.q_ref.k_ref.v_ref, bf16[1024,1536]{1,0:T(8,128)(2,1)} %multiply_convert_fusion.q_ref.k_ref.v_ref), custom_call_target="tpu_custom_call" | custom-call | tf_op jit(solution)/shard_map/pallas_call | solution.py:447
  176.7 7.7 %multiply_convert_fusion.1.q_ref.k_ref.v_ref = bf16[1024,1536]{1,0:T(8,128)(2,1)} fusion(bf16[2,1024,2048]{2,1,0:T(8,128)(2,1)} %bitcast.243, f32[1536]{0:T(1024)S(1)} %copy-done.60, f32[1536]{0:T(1024)S(1)} %get-tuple-element.152, bf16[512,1024]{1,0:T(8,128)(2,1)} %collective-permute-done, bf16[512,1024]{1,0:T(8,128)(2,1)S(1)} %get-tuple-element.124, ...), kind=kOutput, calls=%fused_computation.4 | convolution fusion | flops 3235381248 | bytes 8400897 | tf_op jit(solution)/shard_map/dot_general | solution.py:909
  184.4 12.6 %shard_map.229 = (bf16[1024,512]{1,0:T(8,128)(2,1)}, f32[4,2,1024]{2,1,0:T(2,128)}) custom-call(bf16[1024,1536]{1,0:T(8,128)(2,1)} %multiply_convert_fusion.1.q_ref.k_ref.v_ref, bf16[1024,1536]{1,0:T(8,128)(2,1)} %multiply_convert_fusion.1.q_ref.k_ref.v_ref, bf16[1024,1536]{1,0:T(8,128)(2,1)} %multiply_convert_fusion.1.q_ref.k_ref.v_ref), custom_call_target="tpu_custom_call" | custom-call | tf_op jit(solution)/shard_map/pallas_call | solution.py:447
  197.0 2.9 fusion.31
  200.0 3.7 fusion.45
  207.7 4.2 multiply_convert_fusion.3.q_ref
  211.9 5.9 add_convert_fusion.4.k_ref.v_ref
  217.8 17.9 %shard_map.231 = (bf16[1024,512]{1,0:T(8,128)(2,1)}, f32[4,2,1024]{2,1,0:T(2,128)}) custom-call(bf16[1024,512]{1,0:T(8,128)(2,1)} %multiply_convert_fusion.3.q_ref, bf16[1024,1024]{1,0:T(8,128)(2,1)} %add_convert_fusion.4.k_ref.v_ref, bf16[1024,1024]{1,0:T(8,128)(2,1)} %add_convert_fusion.4.k_ref.v_ref), custom_call_target="tpu_custom_call" | custom-call | tf_op jit(solution)/shard_map/pallas_call | solution.py:447
  235.8 3.5 multiply_convert_fusion.2.q_ref
  239.2 5.9 add_convert_fusion.3.k_ref.v_ref
  245.2 17.7 %shard_map.232 = (bf16[1024,512]{1,0:T(8,128)(2,1)}, f32[4,2,1024]{2,1,0:T(2,128)}) custom-call(bf16[1024,512]{1,0:T(8,128)(2,1)} %multiply_convert_fusion.2.q_ref, bf16[1024,1024]{1,0:T(8,128)(2,1)} %add_convert_fusion.3.k_ref.v_ref, bf16[1024,1024]{1,0:T(8,128)(2,1)} %add_convert_fusion.3.k_ref.v_ref), custom_call_target="tpu_custom_call" | custom-call | tf_op jit(solution)/shard_map/pallas_call | solution.py:447
  262.9 2.7 fusion.33
  265.7 3.0 fusion.46
  272.7 30.6 %shard_map.233 = (bf16[1024,4096]{1,0:T(8,128)(2,1)}, bf16[1024,4096]{1,0:T(8,128)(2,1)}) custom-call(bf16[1024,1024]{1,0:T(8,128)(2,1)} %fusion.16.x_ref.a_ref, bf16[2,1024,4096]{2,1,0:T(8,128)(2,1)} %bitcast.236, f32[1,4096]{1,0:T(1,128)} %bitcast.304), custom_call_target="tpu_custom_call" | custom-call | tf_op jit(solution)/shard_map/pallas_call | solution.py:828
  303.3 10.1 %fusion.9 = f32[1024,1024]{1,0:T(8,128)} fusion(bf16[2,1024,4096]{2,1,0:T(8,128)(2,1)} %bitcast.237, bf16[1024,4096]{1,0:T(8,128)(2,1)} %get-tuple-element.45.db_ref), kind=kOutput, calls=%fused_computation.17 | convolution fusion | flops 4294967296 | bytes 12582912 | tf_op jit(solution)/shard_map/dot_general | solution.py:913
  313.4 8.6 %fusion.47 = (f32[1024]{0:T(1024)S(1)}, f32[1024,1024]{1,0:T(8,128)S(1)}) fusion(f32[1024]{0:T(1024)S(1)} %bitcast.337, f32[1024,1024]{1,0:T(8,128)} %fusion.9, bf16[2,1024,4096]{2,1,0:T(8,128)(2,1)} %bitcast.238, bf16[1024,4096]{1,0:T(8,128)(2,1)S(1)} %copy-done.8, f32[1024]{0:T(1024)S(1)} %bitcast.317, f32[1024]{0:T(1024)S(1)} %bitcast.312, ...), kind=kOutput, calls=%fused_computation.190 | convolution fusion | flops 4303354880 | bytes 20996096 | tf_op jit(solution)/shard_map/dot_general | solution.py:913
  322.6 4.0 fusion.6
  326.6 5.0 fusion.36
  335.3 16.1 %shard_map.234 = (bf16[1024,4096]{1,0:T(8,128)(2,1)}, f32[1,4096]{1,0:T(1,128)}) custom-call(bf16[1024,1024]{1,0:T(8,128)(2,1)} %convert_element_type.163.e_ref.b_ref, bf16[2,1024,4096]{2,1,0:T(8,128)(2,1)} %bitcast.239, bf16[1024,4096]{1,0:T(8,128)(2,1)} %get-tuple-element.46.slope_ref), custom_call_target="tpu_custom_call" | custom-call | tf_op jit(solution)/shard_map/pallas_call | solution.py:858
  351.4 25.9 %shard_map.235 = bf16[2,1024,4096]{2,1,0:T(8,128)(2,1)} custom-call(bf16[1024,1024]{1,0:T(8,128)(2,1)} %fusion.16.x_ref.a_ref, bf16[1024,1024]{1,0:T(8,128)(2,1)} %convert_element_type.163.e_ref.b_ref, bf16[1024,4096]{1,0:T(8,128)(2,1)} %get-tuple-element.48.da_ref, bf16[1024,4096]{1,0:T(8,128)(2,1)} %get-tuple-element.45.db_ref), custom_call_target="tpu_custom_call" | custom-call | tf_op jit(solution)/shard_map/pallas_call | solution.py:895
  378.8 3.7 collective-permute-start.3
  382.6 10.7 %fusion.7 = f32[1024,1024]{1,0:T(8,128)} fusion(bf16[2,1024,4096]{2,1,0:T(8,128)(2,1)} %bitcast.240, bf16[1024,4096]{1,0:T(8,128)(2,1)} %get-tuple-element.48.da_ref), kind=kOutput, calls=%fused_computation.13 | convolution fusion | flops 4294967296 | bytes 12582912 | tf_op jit(solution)/shard_map/dot_general | solution.py:913
  393.3 10.6 %multiply_reduce_fusion = (f32[1024]{0:T(1024)S(1)}, f32[1024]{0:T(1024)S(1)}, f32[1024]{0:T(1024)S(1)}, f32[1024]{0:T(1024)S(1)}, f32[1024,1024]{1,0:T(8,128)}) fusion(f32[1024,1024]{1,0:T(8,128)S(1)} %copy-done.5, f32[1024]{0:T(1024)S(1)} %add_rsqrt_fusion.1, f32[1024]{0:T(1024)S(1)} %broadcast_multiply_fusion.7, f32[1024]{0:T(1024)S(1)} %bitcast.313, ...), kind=kOutput, calls=%fused_computation.20 | convolution fusion | flops 4306497536 | bytes 25194496 | tf_op jit(solution)/shard_map/dot_general | solution.py:913
  403.9 3.0 fusion.38
  407.2 4.2 convolution_convert_fusion.18.do_ref
  411.4 23.5 %shard_map.237 = (bf16[1024,512]{1,0:T(8,128)(2,1)}, bf16[1024,512]{1,0:T(8,128)(2,1)}, bf16[1024,512]{1,0:T(8,128)(2,1)}) custom-call(bf16[1024,512]{1,0:T(8,128)(2,1)} %multiply_convert_fusion.2.q_ref, bf16[1024,1024]{1,0:T(8,128)(2,1)} %add_convert_fusion.3.k_ref.v_ref, bf16[1024,1024]{1,0:T(8,128)(2,1)} %add_convert_fusion.3.k_ref.v_ref, ...), custom_call_target="tpu_custom_call" | custom-call | tf_op jit(solution)/shard_map/pallas_call | solution.py:496
  434.9 3.4 convolution_convert_fusion.19.do_ref
  438.3 23.9 %shard_map.236 = (bf16[1024,512]{1,0:T(8,128)(2,1)}, bf16[1024,512]{1,0:T(8,128)(2,1)}, bf16[1024,512]{1,0:T(8,128)(2,1)}) custom-call(bf16[1024,512]{1,0:T(8,128)(2,1)} %multiply_convert_fusion.3.q_ref, bf16[1024,1024]{1,0:T(8,128)(2,1)} %add_convert_fusion.4.k_ref.v_ref, bf16[1024,1024]{1,0:T(8,128)(2,1)} %add_convert_fusion.4.k_ref.v_ref, ...), custom_call_target="tpu_custom_call" | custom-call | tf_op jit(solution)/shard_map/pallas_call | solution.py:496
  465.7 2.7 fusion.32
  468.4 3.9 multiply_reduce_fusion.1
  474.1 4.2 convolution_convert_fusion.16.do_ref
  478.3 17.1 %shard_map.239 = (bf16[1024,512]{1,0:T(8,128)(2,1)}, bf16[1024,512]{1,0:T(8,128)(2,1)}, bf16[1024,512]{1,0:T(8,128)(2,1)}) custom-call(bf16[1024,1536]{1,0:T(8,128)(2,1)} %multiply_convert_fusion.q_ref.k_ref.v_ref, bf16[1024,1536]{1,0:T(8,128)(2,1)} %multiply_convert_fusion.q_ref.k_ref.v_ref, bf16[1024,1536]{1,0:T(8,128)(2,1)} %multiply_convert_fusion.q_ref.k_ref.v_ref, ...), custom_call_target="tpu_custom_call" | custom-call | tf_op jit(solution)/shard_map/pallas_call | solution.py:496
  495.4 4.1 convolution_convert_fusion.17.do_ref
  499.5 16.9 %shard_map.238 = (bf16[1024,512]{1,0:T(8,128)(2,1)}, bf16[1024,512]{1,0:T(8,128)(2,1)}, bf16[1024,512]{1,0:T(8,128)(2,1)}) custom-call(bf16[1024,1536]{1,0:T(8,128)(2,1)} %multiply_convert_fusion.1.q_ref.k_ref.v_ref, bf16[1024,1536]{1,0:T(8,128)(2,1)} %multiply_convert_fusion.1.q_ref.k_ref.v_ref, ...), custom_call_target="tpu_custom_call" | custom-call | tf_op jit(solution)/shard_map/pallas_call | solution.py:496
  521.2 4.6 fusion.28
  525.8 4.7 fusion.30
  530.5 3.3 fusion.27
  533.8 3.2 fusion.29
  537.0 3.2 fusion.26
  540.3 9.1 %add_convert_fusion.1 = bf16[1024,1024]{1,0:T(8,128)(2,1)S(1)} fusion(f32[1024,1024]{1,0:T(8,128)S(1)} %get-tuple-element.111, f32[1024,1024]{1,0:T(8,128)} %fusion.27, f32[1024,1024]{1,0:T(8,128)} %fusion.26, f32[1024,1024]{1,0:T(8,128)} %fusion.28, f32[1024,1024]{1,0:T(8,128)} %fusion.30, f32[1024,1024]{1,0:T(8,128)} %fusion.29, ...), kind=kOutput, calls=%fused_computation.23 | convolution fusion | flops 1081081856 | bytes 29360128 | tf_op jit(solution)/shard_map/dot_general | solution.py:913
  554.0 2.3 convolution_convert_fusion.9
  556.3 2.3 convolution_convert_fusion.14
  560.8 2.5 convolution_convert_fusion
  565.6 4.0 convolution_convert_fusion.10
  569.6 4.0 convolution_convert_fusion.11
  573.6 3.9 convolution_convert_fusion.4
  577.5 3.9 convolution_convert_fusion.6
  581.5 4.0 convolution_convert_fusion.2
  585.4 4.0 convolution_convert_fusion.5
  589.4 3.9 convolution_convert_fusion.7
  593.4 3.9 convolution_convert_fusion.3
  597.3 4.2 convolution_convert_fusion.12
  601.5 3.9 convolution_convert_fusion.13
  605.5 97.4 %shard_map.240 = (f32[64,4096]{1,0:T(8,128)}, f32[136,128]{1,0:T(8,128)}) custom-call(bf16[4,2,2,64,512]{4,3,2,1,0:T(8,128)(2,1)} %bitcast.266, bf16[4,2,2,64,512]{4,3,2,1,0:T(8,128)(2,1)} %bitcast.265, bf16[4,2,2,64,512]{4,3,2,1,0:T(8,128)(2,1)} %bitcast.278, bf16[4,2,2,64,512]{4,3,2,1,0:T(8,128)(2,1)} %bitcast.277, bf16[4,2,2,64,512]{4,3,2,1,0:T(8,128)(2,1)} %bitcast.270, ...), custom_call_target="tpu_custom_call" | custom-call | bytes 167772160 | tf_op jit(solution)/shard_map/pallas_call | solution.py:750
  702.8 2.6 fusion.24
  705.5 2.6 fusion.25
  708.1 2.6 fusion.23
  711.5 2.5 add_convert_fusion
  729.2 3.2 maximum_select_fusion.2
  732.4 3.2 maximum_select_fusion.4
  735.6 3.2 maximum_select_fusion.5
  (248 shorter events, 67.2 us)
Async XLA Ops:
  7.2 9.1 %copy-start.21 = (bf16[2,512,1024]{2,1,0:T(8,128)(2,1)S(1)}, bf16[2,512,1024]{2,1,0:T(8,128)(2,1)}, u32[]{:S(2)}) copy-start(bf16[2,512,1024]{2,1,0:T(8,128)(2,1)} %param.13) | copy-start | bytes 6291460
  7.2 200.5 %all-gather.3.cloned.1.call-start = ((), (), s32[]{:S(2)}) async-start(), calls=%async_computation.1 | async-start | bytes 8650752 | tf_op jit(solution)/shard_map/all_gather | solution.py:984
  9.9 262.8 %all-gather.5.cloned.1.call-start = ((), (), s32[]{:S(2)}) async-start(), calls=%async_computation.2 | async-start | bytes 17301504 | tf_op jit(solution)/shard_map/all_gather | solution.py:984
  11.8 726.9 %reduce-scatter.2.cloned.1.call-start = ((), (), s32[]{:S(2)}) async-start(), calls=%async_computation.3 | async-start | bytes 17301504 | tf_op jit(solution)/shard_map/reduce_scatter | solution.py:1047
  13.3 142.9 %collective-permute-start.1 = (bf16[4096]{0:T(1024)(128)(2,1)S(1)}, bf16[4096]{0:T(1024)(128)(2,1)S(1)}, u32[]{:S(2)}, u32[]{:S(2)}) collective-permute-start(bf16[4096]{0:T(1024)(128)(2,1)S(1)} %constant_dynamic-update-slice_fusion.2), channel_id=1, source_target_pairs={{0,1},{1,0},{2,3},{3,2},{4,5},{5,4},{6,7},{7,6},{8,9},{9,8},{10,11... | collective-permute-start | bytes 24584 | tf_op jit(solution)/shard_map/ppermute | solution.py:934
  16.2 4.7 copy-start.23
  17.4 182.6 %copy-start.24 = (bf16[512,1024]{1,0:T(8,128)(2,1)}, bf16[512,1024]{1,0:T(8,128)(2,1)S(1)}, u32[]{:S(2)}) copy-start(bf16[512,1024]{1,0:T(8,128)(2,1)S(1)} %get-tuple-element.124) | copy-start | bytes 3145732
  17.4 5.5 copy-start.45
  17.4 5.5 copy-start.49
  17.4 5.6 copy-start.48
  17.4 6.3 copy-start.50
  17.4 139.6 %collective-permute-start = (bf16[512,1024]{1,0:T(8,128)(2,1)}, bf16[512,1024]{1,0:T(8,128)(2,1)}, u32[]{:S(2)}, u32[]{:S(2)}) collective-permute-start(bf16[512,1024]{1,0:T(8,128)(2,1)} %get-tuple-element.125), channel_id=1, source_target_pairs={{0,1},{1,0},{2,3},{3,2},{4,5},{5,4},{6,7},{7,6},{8,9},{9,8},{10,11... | collective-permute-start | bytes 3145736 | tf_op jit(solution)/shard_map/ppermute | solution.py:934
  19.7 192.2 %collective-permute-start.2 = (bf16[512,1024]{1,0:T(8,128)(2,1)}, bf16[512,1024]{1,0:T(8,128)(2,1)}, u32[]{:S(2)}, u32[]{:S(2)}) collective-permute-start(bf16[512,1024]{1,0:T(8,128)(2,1)} %get-tuple-element.123), channel_id=1, source_target_pairs={{0,1},{1,0},{2,3},{3,2},{4,5},{5,4},{6,7},{7,6},{8,9},{9,8},{10,11... | collective-permute-start | bytes 3145736 | tf_op jit(solution)/shard_map/ppermute | solution.py:934
  22.2 300.4 %collective-permute-start.4 = (bf16[512,1024]{1,0:T(8,128)(2,1)}, bf16[512,1024]{1,0:T(8,128)(2,1)S(1)}, u32[]{:S(2)}, u32[]{:S(2)}) collective-permute-start(bf16[512,1024]{1,0:T(8,128)(2,1)} %get-tuple-element.118), channel_id=1, source_target_pairs={{0,1},{1,0},{2,3},{3,2},{4,5},{5,4},{6,7},{7,6},{8,9},{9,8},{10,11... | collective-permute-start | bytes 3145736 | tf_op jit(solution)/shard_map/ppermute | solution.py:934
  23.7 133.3 %copy-start.60 = (f32[1536]{0:T(1024)S(1)}, f32[1536]{0:T(1024)}, u32[]{:S(2)}) copy-start(f32[1536]{0:T(1024)} %constant.67.clone.1) | copy-start | bytes 18436
  197.0 2.9 copy-start.42
  207.7 4.2 copy-start.26
  217.8 18.0 %copy-start.15 = (bf16[1024,1024]{1,0:T(8,128)(2,1)S(1)}, bf16[1024,1024]{1,0:T(8,128)(2,1)}, u32[]{:S(2)}) copy-start(bf16[1024,1024]{1,0:T(8,128)(2,1)} %fusion.15) | copy-start | bytes 6291460
  245.1 17.7 %copy-start.28 = (bf16[1024,512]{1,0:T(8,128)(2,1)S(1)}, bf16[1024,512]{1,0:T(8,128)(2,1)}, u32[]{:S(2)}) copy-start(bf16[1024,512]{1,0:T(8,128)(2,1)} %get-tuple-element.43.o_ref) | copy-start | bytes 3145732
  262.8 2.7 copy-start.1
  262.9 2.8 copy-start.30
  303.3 10.1 %copy-start.4 = (f32[1024,1024]{1,0:T(8,128)S(1)}, f32[1024,1024]{1,0:T(8,128)}, u32[]{:S(2)}) copy-start(f32[1024,1024]{1,0:T(8,128)} %copy-done.3) | copy-start | bytes 12582916
  303.3 10.1 %copy-start.8 = (bf16[1024,4096]{1,0:T(8,128)(2,1)S(1)}, bf16[1024,4096]{1,0:T(8,128)(2,1)}, u32[]{:S(2)}) copy-start(bf16[1024,4096]{1,0:T(8,128)(2,1)} %get-tuple-element.45.db_ref) | copy-start | bytes 25165828
  322.6 4.0 copy-start.10
  378.8 14.4 %slice-start.2 = ((s8[8388608]{0:T(1024)(128)(4,1)}), s8[4194304]{0:T(1024)(128)(4,1)S(1)}, s32[]{:S(2)}) async-start(s8[8388608]{0:T(1024)(128)(4,1)} %bitcast.258), calls=%async_computation.6 | async-start | bytes 8388608
  378.8 14.4 %copy-start.5 = (f32[1024,1024]{1,0:T(8,128)S(1)}, f32[1024,1024]{1,0:T(8,128)}, u32[]{:S(2)}) copy-start(f32[1024,1024]{1,0:T(8,128)} %copy-done.3) | copy-start | bytes 12582916
  378.8 14.4 %copy-start.7 = (f32[1024,1024]{1,0:T(8,128)S(1)}, f32[1024,1024]{1,0:T(8,128)}, u32[]{:S(2)}) copy-start(f32[1024,1024]{1,0:T(8,128)} %copy-done.6) | copy-start | bytes 12582916
  378.8 14.4 %slice-start.3 = ((s8[8388608]{0:T(1024)(128)(4,1)}), s8[4194304]{0:T(1024)(128)(4,1)S(1)}, s32[]{:S(2)}) async-start(s8[8388608]{0:T(1024)(128)(4,1)} %bitcast.258), calls=%async_computation.7 | async-start | bytes 8388608
  378.8 350.4 %collective-permute-start.3 = (bf16[1,512,1024]{2,1,0:T(8,128)(2,1)}, bf16[1,512,1024]{2,1,0:T(8,128)(2,1)}, u32[]{:S(2)}, u32[]{:S(2)}) collective-permute-start(bf16[1,512,1024]{2,1,0:T(8,128)(2,1)} %get-tuple-element.121), channel_id=1, source_target_pairs={{0,1},{1,0},{2,3},{3,2},{4,5},{5,4},{6,7},{7,6},{8,9},{9,8},{10,11... | collective-permute-start | bytes 3145736 | tf_op jit(solution)/shard_map/ppermute | solution.py:934
  407.2 27.7 %copy-start.17 = (bf16[1024,1024]{1,0:T(8,128)(2,1)}, bf16[1024,1024]{1,0:T(8,128)(2,1)S(1)}, u32[]{:S(2)}) copy-start(bf16[1024,1024]{1,0:T(8,128)(2,1)S(1)} %convert_element_type.164) | copy-start | bytes 6291460
  438.3 23.9 %copy-start.12 = (bf16[1024,512]{1,0:T(8,128)(2,1)S(1)}, bf16[1024,512]{1,0:T(8,128)(2,1)}, u32[]{:S(2)}) copy-start(bf16[1024,512]{1,0:T(8,128)(2,1)} %get-tuple-element.52) | copy-start | bytes 3145732
  438.3 25.7 %copy-start.11 = (bf16[1024,512]{1,0:T(8,128)(2,1)S(1)}, bf16[1024,512]{1,0:T(8,128)(2,1)}, u32[]{:S(2)}) copy-start(bf16[1024,512]{1,0:T(8,128)(2,1)} %get-tuple-element.64) | copy-start | bytes 3145732
  462.2 3.5 copy-start.34
  465.7 2.7 copy-start.2
  474.1 4.2 copy-start.19
  499.5 19.9 %copy-start.13 = (bf16[1024,512]{1,0:T(8,128)(2,1)S(1)}, bf16[1024,512]{1,0:T(8,128)(2,1)}, u32[]{:S(2)}) copy-start(bf16[1024,512]{1,0:T(8,128)(2,1)} %get-tuple-element.60) | copy-start | bytes 3145732
  516.4 4.7 copy-start.38
  521.1 4.7 copy-start.40
  521.1 9.4 %slice-start = ((s8[8388608]{0:T(1024)(128)(4,1)}), s8[4194304]{0:T(1024)(128)(4,1)S(1)}, s32[]{:S(2)}) async-start(s8[8388608]{0:T(1024)(128)(4,1)} %bitcast.250), calls=%async_computation.4 | async-start | bytes 8388608
  525.8 4.7 slice-start.1
  525.8 4.7 copy-start.36
  530.5 3.3 copy-start.58
  533.8 3.2 copy-start.56
  550.6 181.8 %collective-permute-start.5 = (bf16[1,512,1024]{2,1,0:T(8,128)(2,1)}, bf16[1,512,1024]{2,1,0:T(8,128)(2,1)}, u32[]{:S(2)}, u32[]{:S(2)}) collective-permute-start(bf16[1,512,1024]{2,1,0:T(8,128)(2,1)} %get-tuple-element.117), channel_id=1, source_target_pairs={{0,1},{1,0},{2,3},{3,2},{4,5},{5,4},{6,7},{7,6},{8,9},{9,8},{10,11... | collective-permute-start | bytes 3145736 | tf_op jit(solution)/shard_map/ppermute | solution.py:934
  551.7 2.3 copy-start.46
  551.7 2.3 copy-start.29
  554.0 2.3 copy-start.16
  556.3 2.3 copy-start.35
  560.8 2.5 copy-start.44
  565.6 4.0 copy-start.33
  569.6 4.0 copy-start.25
  569.6 4.0 copy-start.57
  573.6 3.9 copy-start.37
  577.5 4.0 copy-start.14
  581.5 4.0 copy-start.59
  585.4 4.0 copy-start.41
  589.4 3.9 copy-start.39
  593.4 3.9 copy-start.52
  597.3 4.2 copy-start.54
  702.8 2.6 copy-start.55
  705.4 2.6 copy-start.53
  708.1 2.6 copy-start.32
  714.0 15.2 %copy-start.9 = (bf16[1,512,1024]{2,1,0:T(8,128)(2,1)S(1)}, bf16[1,512,1024]{2,1,0:T(8,128)(2,1)}, u32[]{:S(2)}) copy-start(bf16[1,512,1024]{2,1,0:T(8,128)(2,1)} %get-tuple-element.120) | copy-start | bytes 3145732
  715.2 20.4 %collective-permute-start.6 = (bf16[1,512,1024]{2,1,0:T(8,128)(2,1)}, bf16[1,512,1024]{2,1,0:T(8,128)(2,1)}, u32[]{:S(2)}, u32[]{:S(2)}) collective-permute-start(bf16[1,512,1024]{2,1,0:T(8,128)(2,1)} %get-tuple-element.115), channel_id=1, source_target_pairs={{0,1},{1,0},{2,3},{3,2},{4,5},{5,4},{6,7},{7,6},{8,9},{9,8},{10,11... | collective-permute-start | bytes 3145736 | tf_op jit(solution)/shard_map/ppermute | solution.py:934
  (11 other events, 22.0 us)
Sparse Core Ops, SparseCore 0:
  11.4 105.5 all-gather.2
  120.5 116.3 all-gather.4
  377.4 189.0 reduce-scatter.1

commit v3 on v2

--- a/solution.py
+++ b/solution.py
@@ -536,7 +536,7 @@
 def pipeline(chunks, stages, begin):
     started = {}
     for step in range(chunks + stages):
-        for s in range(stages, -1, -1):
+        for s in range(stages + 1):
             k = step - s
             if 0 <= k < chunks:
                 if s > 0:
@@ -548,75 +548,107 @@
             copy.wait_send()
 
 
-def gather_kernel(shard_ref, w_ref, send, recv, own, *, cw, chunks):
+def start_copy(src, dst, send, recv, to):
+    copy = pltpu.make_async_remote_copy(
+        src_ref=src,
+        dst_ref=dst,
+        send_sem=send,
+        recv_sem=recv,
+        device_id=to,
+        device_id_type=MESH,
+    )
+    copy.start()
+    return copy
+
+
+def gather_kernel(shard_ref, *refs, cw, chunks, swaps):
+    ins, outs = refs[:swaps], refs[swaps + 1 : 2 * swaps + 1]
+    w_ref = refs[swaps]
+    send, recv, own, swap_send, swap_recv, swap_own = refs[2 * swaps + 1 :]
     (t, z, y, c), ids = partners()
     mine = pltpu.make_async_copy(shard_ref, w_ref.at[t, z, y, c], own)
     mine.start()
+    kept = [
+        pltpu.make_async_copy(ins[i].at[t], outs[i].at[t], swap_own.at[i]) for i in range(swaps)
+    ]
+    for copy in kept:
+        copy.start()
     greet(ids)
     pair = (z // 2) * 2
-    h = cw // 2
+    traded = []
 
     def begin(k, s):
-        both, a, b = pl.ds(k * cw, cw), pl.ds(k * cw, h), pl.ds(k * cw + h, h)
+        cols = pl.ds(k * cw, cw)
         if s == 0:
-            moves = [(shard_ref.at[:, both], w_ref.at[t, z, y, c, :, both], "z1", 0)]
-        elif s == 1:
+            r, to = w_ref.at[t, z, y, c, :, cols], "z1"
+            copies = [start_copy(shard_ref.at[:, cols], r, send.at[k, 0], recv.at[k, 0], ids[to])]
+            for i in range(swaps):
+                part = ins[i].shape[1] // chunks
+                rows = pl.ds(k * part, part)
+                traded.append(
+                    start_copy(
+                        ins[i].at[1 - t, rows],
+                        outs[i].at[t, rows],
+                        swap_send.at[i, k],
+                        swap_recv.at[i, k],
+                        ids["x"],
+                    )
+                )
+            return copies
+        if s == 5:
+            return []
+        if s == 1:
             if k == 0:
                 mine.wait()
-            r = w_ref.at[t, pl.ds(pair, 2), y, c, :, both]
-            moves = [(r, r, "z2", 1)]
+            r, to = w_ref.at[t, pl.ds(pair, 2), y, c, :, cols], "z2"
         elif s == 2:
-            ra, rb = w_ref.at[t, :, y, c, :, a], w_ref.at[t, :, y, c, :, b]
-            moves = [(ra, ra, "y", 2), (rb, rb, "x", 3)]
+            r, to = w_ref.at[t, :, y, c, :, cols], "x"
         elif s == 3:
-            ra, rb = w_ref.at[t, :, :, c, :, a], w_ref.at[:, :, y, c, :, b]
-            moves = [(ra, ra, "x", 4), (rb, rb, "y", 5)]
-        elif s == 4:
-            r = w_ref.at[:, :, :, c, :, both]
-            moves = [(r, r, "c", 6)]
+            r, to = w_ref.at[:, :, y, c, :, cols], "y"
         else:
-            moves = []
-        copies = []
-        for src, dst, to, j in moves:
-            copy = pltpu.make_async_remote_copy(
-                src_ref=src,
-                dst_ref=dst,
-                send_sem=send.at[k, j],
-                recv_sem=recv.at[k, j],
-                device_id=ids[to],
-                device_id_type=MESH,
-            )
-            copy.start()
-            copies.append(copy)
-        return copies
+            r, to = w_ref.at[:, :, :, c, :, cols], "c"
+        return [start_copy(r, r, send.at[k, s], recv.at[k, s], ids[to])]
 
     pipeline(chunks, 5, begin)
-
-
-def gather_weights(shard, cid, chunks):
+    for copy in traded:
+        copy.wait()
+    for copy in kept:
+        copy.wait()
+
+
+def gather_weights(shard, pieces, cid, chunks):
     rows, cols = shard.shape
-    whole = pl.pallas_call(
-        functools.partial(gather_kernel, cw=cols // chunks, chunks=chunks),
-        in_specs=[pl.BlockSpec(memory_space=pltpu.VMEM)],
-        out_specs=pl.BlockSpec(memory_space=pl.ANY),
-        out_shape=jax.ShapeDtypeStruct((2, 4, 2, 2, rows, cols), shard.dtype),
+    swaps = len(pieces)
+    anywhere = pl.BlockSpec(memory_space=pl.ANY)
+    dma = pltpu.SemaphoreType.DMA
+    outs = pl.pallas_call(
+        functools.partial(gather_kernel, cw=cols // chunks, chunks=chunks, swaps=swaps),
+        in_specs=[pl.BlockSpec(memory_space=pltpu.VMEM)] + [anywhere] * swaps,
+        out_specs=[anywhere] * (1 + swaps),
+        out_shape=[jax.ShapeDtypeStruct((2, 4, 2, 2, rows, cols), shard.dtype)]
+        + [jax.ShapeDtypeStruct(p.shape, p.dtype) for p in pieces],
         scratch_shapes=[
-            pltpu.SemaphoreType.DMA((chunks, 7)),
-            pltpu.SemaphoreType.DMA((chunks, 7)),
-            pltpu.SemaphoreType.DMA,
+            dma((chunks, 5)),
+            dma((chunks, 5)),
+            dma,
+            dma((swaps, chunks)),
+            dma((swaps, chunks)),
+            dma((swaps,)),
         ],
         compiler_params=pltpu.CompilerParams(collective_id=cid, has_side_effects=True),
         cost_estimate=pl.CostEstimate(
             flops=0, bytes_accessed=32 * rows * cols * 20, transcendentals=0
         ),
-    )(shard)
-    return whole.reshape(2, 16 * rows, cols)
-
-
-def scatter_kernel(*refs, chunks):
-    g_refs, refs = refs[: 2 * chunks], refs[2 * chunks :]
-    small_ref, out_ref, small_out, own, r1, s2, r2, k2, s3, r3, k3, s4, r4, k4, s5, r5 = refs[:16]
-    sm, rm, send, recv, own_sem, small_send, small_recv = refs[16:]
+    )(shard, *pieces)
+    whole = outs[0].reshape(2, 16 * rows, cols)
+    return whole, [p.reshape(p.shape[0] * p.shape[1], p.shape[2]) for p in outs[1:]]
+
+
+def scatter_kernel(*refs, chunks, ahead):
+    g_refs, refs = refs[: 2 * chunks], refs[2 * chunks + ahead :]
+    rows_ref, small_ref, out_ref, small_out, pieces_ref, own, r1 = refs[:7]
+    s2, r2, k2, s3, r3, k3, s4, r4, k4, s5, r5 = refs[7:18]
+    sm, rm, send, recv, own_sem, small_send, small_recv, swap_send, swap_recv, swap_own = refs[18:]
     (t, z, y, c), ids = partners()
     pair = (z // 2) * 2
     away = 2 - pair
@@ -635,31 +667,17 @@
     for k in range(chunks):
         loc(k, 0).start()
         loc(k, 1).start()
+    kept = pltpu.make_async_copy(rows_ref.at[t], pieces_ref.at[t], swap_own)
+    kept.start()
     greet(ids)
+    traded = []
 
     def go(k, j, src, dst, to):
-        copy = pltpu.make_async_remote_copy(
-            src_ref=src,
-            dst_ref=dst,
-            send_sem=send.at[k, j],
-            recv_sem=recv.at[k, j],
-            device_id=ids[to],
-            device_id_type=MESH,
-        )
-        copy.start()
-        return copy
+        return start_copy(src, dst, send.at[k, j], recv.at[k, j], ids[to])
 
     def small_go(j):
-        copy = pltpu.make_async_remote_copy(
-            src_ref=sm.at[j],
-            dst_ref=rm.at[j],
-            send_sem=small_send.at[j],
-            recv_sem=small_recv.at[j],
-            device_id=ids[("c", "x", "y", "z2", "z1")[j]],
-            device_id_type=MESH,
-        )
-        copy.start()
-        return copy
+        to = ids[("c", "x", "y", "z2", "z1")[j]]
+        return start_copy(sm.at[j], rm.at[j], small_send.at[j], small_recv.at[j], to)
 
     def up(v):
         return v.astype(f32)
@@ -720,6 +738,11 @@
     smalls = []
 
     def begin_with_small(k, s):
+        if s == 0:
+            part = rows_ref.shape[1] // chunks
+            some = pl.ds(k * part, part)
+            src, dst = rows_ref.at[1 - t, some], pieces_ref.at[t, some]
+            traded.append(start_copy(src, dst, swap_send.at[k], swap_recv.at[k], ids["x"]))
         if k == 0:
             if s == 0:
                 sm[0] = small_ref[...]
@@ -737,23 +760,29 @@
     pipeline(chunks, 5, begin_with_small)
     for copy in smalls:
         copy.wait_send()
-
-
-def scatter_grads(pairs, small, cid):
+    for copy in traded:
+        copy.wait()
+    kept.wait()
+
+
+def scatter_grads(pairs, ahead, seq_rows, small, cid):
     chunks = len(pairs)
     width, cw = pairs[0][0].shape
     rows, h, cols = width // 16, cw // 2, cw * chunks
     V = pltpu.VMEM
     dma = pltpu.SemaphoreType.DMA
     flat = [g.reshape(4, 2, 2, rows, cw) for pair in pairs for g in pair]
+    seq_rows = seq_rows.reshape(2, seq_rows.shape[0] // 2, seq_rows.shape[1])
     whole = pl.BlockSpec(memory_space=pltpu.VMEM)
+    anywhere = pl.BlockSpec(memory_space=pl.ANY)
     return pl.pallas_call(
-        functools.partial(scatter_kernel, chunks=chunks),
-        in_specs=[pl.BlockSpec(memory_space=pl.ANY)] * len(flat) + [whole],
-        out_specs=[whole, whole],
+        functools.partial(scatter_kernel, chunks=chunks, ahead=len(ahead)),
+        in_specs=[anywhere] * (len(flat) + len(ahead) + 1) + [whole],
+        out_specs=[whole, whole, anywhere],
         out_shape=[
             jax.ShapeDtypeStruct((rows, cols), f32),
             jax.ShapeDtypeStruct(small.shape, f32),
+            jax.ShapeDtypeStruct(seq_rows.shape, seq_rows.dtype),
         ],
         scratch_shapes=[
             V((2, 4, 2, rows, cols), bf16),
@@ -776,6 +805,9 @@
             dma((chunks, 2)),
             dma((5,)),
             dma((5,)),
+            dma((chunks,)),
+            dma((chunks,)),
+            dma,
         ],
         compiler_params=pltpu.CompilerParams(
             collective_id=cid, has_side_effects=True, vmem_limit_bytes=60 * 2**20
@@ -783,7 +815,7 @@
         cost_estimate=pl.CostEstimate(
             flops=0, bytes_accessed=32 * rows * cols * 20, transcendentals=0
         ),
-    )(*flat, small)
+    )(*flat, *ahead, seq_rows, small)
 
 
 ERFC_SLOPE = 0.44
@@ -870,6 +902,91 @@
         ],
         compiler_params=pltpu.CompilerParams(vmem_limit_bytes=56 * 2**20),
     )(e, w, slope)
+
+
+def down_kernel(act_ref, w_ref, h_ref, cot_ref, vec_ref, mixed_ref, dr_ref, e_ref, sum_ref):
+    units = w_ref.shape[2]
+    r = h_ref[...] + vec_ref[0:1]
+    for t in range(2):
+        part = act_ref[:, t * units : (t + 1) * units]
+        r = r + lax.dot_general(part, w_ref[t], NT, preferred_element_type=f32)
+    gain = vec_ref[1:2]
+    h, n, inv = norm_rows(r, gain, vec_ref[2:3])
+    mixed_ref[...] = h.astype(bf16)
+    rows_back(cot_ref[...].astype(f32), n, inv, gain, dr_ref, e_ref, sum_ref)
+
+
+def rows_back(e, n, inv, gain, dr_ref, e_ref, sum_ref):
+    dr, gg, gs, gb = norm_rows_back(e, n, inv, gain)
+    dr_ref[...] = dr
+    e_ref[...] = dr.astype(bf16)
+
+    @pl.when(pl.program_id(0) == 0)
+    def _():
+        sum_ref[...] = jnp.zeros_like(sum_ref)
+
+    sum_ref[0:3] += jnp.concatenate([gg[None], gs[None], gb[None]], 0)
+
+
+def down_and_norms(act, w, h, cot, vecs, block):
+    rows, width = h.shape
+    units = w.shape[2] // 2
+    row = pl.BlockSpec((block, width), lambda i: (i, 0))
+    top = pl.BlockSpec((8, width), lambda i: (0, 0))
+    return pl.pallas_call(
+        down_kernel,
+        grid=(rows // block,),
+        in_specs=[
+            pl.BlockSpec((block, 2 * units), lambda i: (i, 0)),
+            pl.BlockSpec((2, width, units), lambda i: (0, 0, 1), pipeline_mode=pl.Buffered(1)),
+            row,
+            row,
+            top,
+        ],
+        out_specs=[row, row, row, top],
+        out_shape=[
+            jax.ShapeDtypeStruct((rows, width), bf16),
+            jax.ShapeDtypeStruct((rows, width), f32),
+            jax.ShapeDtypeStruct((rows, width), bf16),
+            jax.ShapeDtypeStruct((8, width), f32),
+        ],
+        compiler_params=pltpu.CompilerParams(vmem_limit_bytes=56 * 2**20),
+    )(act, w, h, cot, vecs)
+
+
+def up_back_kernel(du_ref, w_ref, dr3_ref, n_ref, inv_ref, vec_ref, dr_ref, e_ref, sum_ref):
+    units = w_ref.shape[2]
+    e = dr3_ref[...]
+    for t in range(2):
+        part = du_ref[:, t * units : (t + 1) * units]
+        e = e + lax.dot_general(part, w_ref[t], NT, preferred_element_type=f32)
+    rows_back(e, n_ref[...], inv_ref[...], vec_ref[0:1], dr_ref, e_ref, sum_ref)
+
+
+def up_back_and_norm(du, w, dr3, n, inv, vecs, block):
+    rows, width = dr3.shape
+    units = w.shape[2] // 2
+    row = pl.BlockSpec((block, width), lambda i: (i, 0))
+    top = pl.BlockSpec((8, width), lambda i: (0, 0))
+    return pl.pallas_call(
+        up_back_kernel,
+        grid=(rows // block,),
+        in_specs=[
+            pl.BlockSpec((block, 2 * units), lambda i: (i, 0)),
+            pl.BlockSpec((2, width, units), lambda i: (0, 0, 0), pipeline_mode=pl.Buffered(1)),
+            row,
+            row,
+            pl.BlockSpec((block, 1), lambda i: (i, 0)),
+            top,
+        ],
+        out_specs=[row, row, top],
+        out_shape=[
+            jax.ShapeDtypeStruct((rows, width), f32),
+            jax.ShapeDtypeStruct((rows, width), bf16),
+            jax.ShapeDtypeStruct((8, width), f32),
+        ],
+        compiler_params=pltpu.CompilerParams(vmem_limit_bytes=56 * 2**20),
+    )(du, w, dr3, n, inv, vecs)
 
 
 def weight_grads_kernel(a_ref,b_ref,da_ref,db_ref,out_ref,at,bt,*,tiles):
@@ -989,15 +1106,25 @@
     hb = small[:, : 4 * cols].reshape(2, 4, cols).astype(f32)
     ub = small[:, 4 * cols :].astype(f32)
 
-    g_self = gather_weights(
-        jnp.concatenate([w_self_in.reshape(shard, 3 * cols), w_self_out.T], 1), 1, 4
-    )
-    g_cross = gather(w_cross_in.reshape(shard, 3 * cols), w_cross_out.T)
+    c3, c4 = 3 * cols, 4 * cols
+    g_att, (x, mem) = gather_weights(
+        jnp.concatenate(
+            [
+                w_self_in.reshape(shard, c3),
+                w_self_out.T,
+                w_cross_in.reshape(shard, c3),
+                w_cross_out.T,
+            ],
+            1,
+        ),
+        (layer_in, memory),
+        1,
+        8,
+    )
+    g_att, w_up, w_down = lax.optimization_barrier((g_att, w_up, w_down))
+    g_self, g_cross = g_att[:, :, :c4], g_att[:, :, c4:]
     g_ffn = gather(w_up, w_down.T)
-    c3 = 3 * cols
-
-    x = own_sequence(layer_in, place)
-    mem = own_sequence(memory, place)
+    g_ffn, out_grad = lax.optimization_barrier((g_ffn, out_grad))
     cot = own_sequence(out_grad, place)
     xf = x.astype(f32)
     halves = (0, 1)
@@ -1031,25 +1158,34 @@
     h2b = h2.astype(bf16)
 
     act, slope = hidden_units(h2b, g_ffn, ub.reshape(1, 2 * units), 512)
-    r3 = (
-        h2
-        + (nt(act[:, :units], g_ffn[0, :, units:]) + nt(act[:, units:], g_ffn[1, :, units:]))
-        + shifts[2]
-    )
-    h3, n3, i3 = norm_rows(r3, gains[2], shifts[5])
-    mixed = to_pieces(h3.astype(bf16), place)
-
-    dr3, gg3, gs3, gb3 = norm_rows_back(cot.astype(f32), n3, i3, gains[2])
-    e3 = dr3.astype(bf16)
+    none = jnp.zeros((5, width), f32)
+    mixed_rows, dr3, e3, sums3 = down_and_norms(
+        act,
+        g_ffn,
+        h2,
+        cot,
+        jnp.concatenate([shifts[2:3], gains[2:3], shifts[5:6], none], 0),
+        256,
+    )
+    gg3, gs3, gb3 = sums3[0], sums3[1], sums3[2]
+    mixed = to_pieces(mixed_rows, place)
+
     du, gu = hidden_units_back(e3, g_ffn, slope, 512)
     grad_ffn = weight_grads(h2b, e3, du, act, 1024)
     grad_ffn, du = lax.optimization_barrier((grad_ffn, du))
     s_ffn = lax.psum_scatter(
         grad_ffn.reshape(2 * width, 2 * units), ("tp", "fsdp"), scatter_dimension=0, tiled=True
     ).astype(f32)
-    dh2 = dr3 + (nt(du[:, :units], g_ffn[0, :, :units]) + nt(du[:, units:], g_ffn[1, :, :units]))
-    dr2, gg2, gs2, gb2 = norm_rows_back(dh2, n2, i2, gains[1])
-    e2 = dr2.astype(bf16)
+    dr2, e2, sums2 = up_back_and_norm(
+        du,
+        g_ffn,
+        dr3,
+        n2,
+        i2,
+        jnp.concatenate([gains[1:2], none, none[:2]], 0),
+        256,
+    )
+    gg2, gs2, gb2 = sums2[0], sums2[1], sums2[2]
 
     dcq, dck, dcv = [], [], []
     for t in halves:
@@ -1094,7 +1230,6 @@
         + nt(dsv[t], g_self[t, :, 2 * cols : c3])
         for t in halves
     )
-    d_layer_in = to_pieces(dx.astype(bf16), place)
 
     def col_sums(pair):
         return jnp.stack([jnp.sum(p.astype(f32), 0) for p in pair])
@@ -1106,7 +1241,9 @@
             for v in (gh, gu, gg1, gg2, gg3, gb1, gb2, gb3, gs1, gs2, gs3)
         ]
     )
-    s_att, flat = scatter_grads(grads, flat.reshape(-1, 128), 2)
+    s_att, flat, d_layer_in = scatter_grads(
+        grads, (mixed, d_memory), dx.astype(bf16), flat.reshape(-1, 128), 2
+    )
     flat = flat.reshape(-1)
     head_sum = lax.dynamic_index_in_dim(flat[: 8 * cols].reshape(2, 4, cols), place, 0, False)
     unit_sum = lax.dynamic_index_in_dim(

time: 759 us -> 701 us (0.924)
  matrix products: 202 us -> 139 us
  Pallas kernels: 444 us -> 487 us
  other arithmetic: 44.4 us -> 25.9 us
  local copies, waits for them, and re-layouts: 34.5 us -> 22.3 us
    pallas_call x1 -> x3, Pallas kernels: 97.4 us -> 147 us  [the longest x1 110 us: scatter_grads(): pl.pallas_call(functools.partial(scatter_kernel, chunks=chunks, ahead=len...]
    dot_general x20 -> x16, matrix products: 97.4 us -> 54.8 us  [nt(): return lax.dot_general(a, b, NT, preferred_element_type=f32)]
    dot_general x16, matrix products: 53.7 us -> 36.7 us  [tn(): lax.dot_general(a, b, (((0,), (0,)), ((), ())), preferred_element_type=f32)]
    reduce_sum x4 -> x1, other arithmetic: 13.3 us -> 1.4 us  [norm_rows_back(): return (grad, jnp.sum(e * n, 0), jnp.sum(e, 0), jnp.sum(grad, 0))]
  transfers between devices with their start and end apart: 10 -> 6, of which waited for: 0 -> 2; matrix products, arithmetic and copies ran while one was open for 34% -> 25% of each run, Pallas kernels for 54% -> 43%
where the time goes in v3:
time: 701 us; the launch traced here: 696 us
  Pallas kernels  487 us (69%)
  matrix products  139 us (20%)
  other arithmetic  25.9 us (4%)
  local copies, waits for them, and re-layouts  22.3 us (3%)
  between operations  15.1 us (2%)
    pallas_call x1, Pallas kernels, gather_weights(): pl.pallas_call(functools.partial(gather_kernel, cw=cols // chunks, chunks...  125 us
    pallas_call x1, Pallas kernels, scatter_grads(): pl.pallas_call(functools.partial(scatter_kernel, chunks=chunks, ahead=len...  110 us
    pallas_call x4, Pallas kernels, att_bwd(): pl.pallas_call(functools.partial(att_bwd_kernel, bq=bq, causal=causal), g...  81.9 us
    pallas_call x4, Pallas kernels, att_fwd(): pl.pallas_call(functools.partial(att_fwd_kernel, bq=bq, causal=causal), g...  60 us
    dot_general x16, matrix products, nt(): return lax.dot_general(a, b, NT, preferred_element_type=f32)  54.8 us
    dot_general x10, matrix products, nn(): return lax.dot_general(a, b, NN, preferred_element_type=f32)  48 us
    dot_general x16, matrix products, tn(): lax.dot_general(a, b, (((0,), (0,)), ((), ())), preferred_element_type=f32)  36.7 us
    pallas_call x1, Pallas kernels, hidden_units(): pl.pallas_call(up_kernel, grid=(2 * per,), in_specs=[pl.BlockSpec((rows,...  30.4 us
  transfers between devices with their start and end apart: 6, of which 2 were waited for; matrix products, arithmetic and copies ran while one was open for 25% of the time, Pallas kernels for 43%

profile of v3, /device:TPU:0, one launch (start us, length us, event | category | flops | bytes accessed | tf_op | source)
XLA Modules:
  0.0 696.0 jit_solution(3235932981154391529)
XLA Ops:
  9.2 1.7 pad_maximum_fusion.shard_ref
  10.9 125.0 %shard_map.228 = (bf16[2,4,2,2,64,4096]{5,4,3,2,1,0:T(8,128)(2,1)}, bf16[2,512,1024]{2,1,0:T(8,128)(2,1)}, bf16[2,512,1024]{2,1,0:T(8,128)(2,1)}) custom-call(bf16[64,4096]{1,0:T(8,128)(2,1)} %pad_maximum_fusion.shard_ref, bf16[2,512,1024]{2,1,0:T(8,128)(2,1)} %refs_0_.1, bf16[2,512,1024]{2,1,0:T(8,128)(2,1)} %refs_1_.1), custom_call_target="tpu_custom_call" | custom-call | bytes 167772160 | tf_op jit(solution)/shard_map/pallas_call | solution.py:624
  138.4 2.3 collective-permute-done
  140.9 7.7 %multiply_convert_fusion.1.q_ref.k_ref.v_ref = bf16[1024,1536]{1,0:T(8,128)(2,1)} fusion(bf16[1024,1024]{1,0:T(8,128)(2,1)} %bitcast.240, f32[1536]{0:T(1024)S(1)} %copy-done.49, f32[1536]{0:T(1024)S(1)} %get-tuple-element.176, bf16[2,1024,4096]{2,1,0:T(8,128)(2,1)} %bitcast.267), kind=kOutput, calls=%fused_computation.1 | convolution fusion | flops 3225944064 | bytes 8400896 | tf_op jit(solution)/shard_map/dot_general | solution.py:1026
  148.6 12.2 %shard_map.229 = (bf16[1024,512]{1,0:T(8,128)(2,1)}, f32[4,2,1024]{2,1,0:T(2,128)}) custom-call(bf16[1024,1536]{1,0:T(8,128)(2,1)} %multiply_convert_fusion.1.q_ref.k_ref.v_ref, bf16[1024,1536]{1,0:T(8,128)(2,1)} %multiply_convert_fusion.1.q_ref.k_ref.v_ref, bf16[1024,1536]{1,0:T(8,128)(2,1)} %multiply_convert_fusion.1.q_ref.k_ref.v_ref), custom_call_target="tpu_custom_call" | custom-call | tf_op jit(solution)/shard_map/pallas_call | solution.py:447
  160.8 6.7 multiply_convert_fusion.q_ref.k_ref.v_ref
  167.5 12.0 %shard_map.230 = (bf16[1024,512]{1,0:T(8,128)(2,1)}, f32[4,2,1024]{2,1,0:T(2,128)}) custom-call(bf16[1024,1536]{1,0:T(8,128)(2,1)} %multiply_convert_fusion.q_ref.k_ref.v_ref, bf16[1024,1536]{1,0:T(8,128)(2,1)} %multiply_convert_fusion.q_ref.k_ref.v_ref, bf16[1024,1536]{1,0:T(8,128)(2,1)} %multiply_convert_fusion.q_ref.k_ref.v_ref), custom_call_target="tpu_custom_call" | custom-call | tf_op jit(solution)/shard_map/pallas_call | solution.py:447
  180.2 2.6 fusion.46
  182.8 2.9 fusion.81
  187.1 4.3 multiply_convert_fusion.2.q_ref
  191.3 5.3 add_convert_fusion.2.k_ref.v_ref
  196.6 18.2 %shard_map.232 = (bf16[1024,512]{1,0:T(8,128)(2,1)}, f32[4,2,1024]{2,1,0:T(2,128)}) custom-call(bf16[1024,512]{1,0:T(8,128)(2,1)} %multiply_convert_fusion.2.q_ref, bf16[1024,1024]{1,0:T(8,128)(2,1)} %add_convert_fusion.2.k_ref.v_ref, bf16[1024,1024]{1,0:T(8,128)(2,1)} %add_convert_fusion.2.k_ref.v_ref), custom_call_target="tpu_custom_call" | custom-call | tf_op jit(solution)/shard_map/pallas_call | solution.py:447
  214.9 3.6 multiply_convert_fusion.3.q_ref
  218.5 5.3 add_convert_fusion.3.k_ref.v_ref
  223.7 17.6 %shard_map.231 = (bf16[1024,512]{1,0:T(8,128)(2,1)}, f32[4,2,1024]{2,1,0:T(2,128)}) custom-call(bf16[1024,512]{1,0:T(8,128)(2,1)} %multiply_convert_fusion.3.q_ref, bf16[1024,1024]{1,0:T(8,128)(2,1)} %add_convert_fusion.3.k_ref.v_ref, bf16[1024,1024]{1,0:T(8,128)(2,1)} %add_convert_fusion.3.k_ref.v_ref), custom_call_target="tpu_custom_call" | custom-call | tf_op jit(solution)/shard_map/pallas_call | solution.py:447
  241.3 3.2 fusion.38
  244.5 4.8 fusion.82
  252.4 4.8 fusion.73
  257.3 30.4 %shard_map.233 = (bf16[1024,4096]{1,0:T(8,128)(2,1)}, bf16[1024,4096]{1,0:T(8,128)(2,1)}) custom-call(bf16[1024,1024]{1,0:T(8,128)(2,1)} %get-tuple-element.133.x_ref.a_ref, bf16[2,1024,4096]{2,1,0:T(8,128)(2,1)} %bitcast.232, f32[1,4096]{1,0:T(1,128)} %bitcast.304), custom_call_target="tpu_custom_call" | custom-call | tf_op jit(solution)/shard_map/pallas_call | solution.py:860
  287.7 2.3 maximum_select_fusion.cot_ref
  290.0 19.2 %shard_map.234 = (bf16[1024,1024]{1,0:T(8,128)(2,1)}, f32[1024,1024]{1,0:T(8,128)}, bf16[1024,1024]{1,0:T(8,128)(2,1)}, f32[8,1024]{1,0:T(8,128)}) custom-call(bf16[1024,4096]{1,0:T(8,128)(2,1)} %get-tuple-element.68.act_ref.db_ref, bf16[2,1024,4096]{2,1,0:T(8,128)(2,1)} %bitcast.233, f32[1024,1024]{1,0:T(8,128)} %get-tuple-element.134.h_ref, ...), custom_call_target="tpu_custom_call" | custom-call | tf_op jit(solution)/shard_map/pallas_call | solution.py:936
  309.2 16.1 %shard_map.235 = (bf16[1024,4096]{1,0:T(8,128)(2,1)}, f32[1,4096]{1,0:T(1,128)}) custom-call(bf16[1024,1024]{1,0:T(8,128)(2,1)} %get-tuple-element.71.e_ref.b_ref, bf16[2,1024,4096]{2,1,0:T(8,128)(2,1)} %bitcast.234, bf16[1024,4096]{1,0:T(8,128)(2,1)} %get-tuple-element.72.slope_ref), custom_call_target="tpu_custom_call" | custom-call | tf_op jit(solution)/shard_map/pallas_call | solution.py:890
  325.4 26.1 %shard_map.236 = bf16[2,1024,4096]{2,1,0:T(8,128)(2,1)} custom-call(bf16[1024,1024]{1,0:T(8,128)(2,1)} %get-tuple-element.133.x_ref.a_ref, bf16[1024,1024]{1,0:T(8,128)(2,1)} %get-tuple-element.71.e_ref.b_ref, bf16[1024,4096]{1,0:T(8,128)(2,1)} %get-tuple-element.74.da_ref.du_ref, bf16[1024,4096]{1,0:T(8,128)(2,1)} %get-tuple-element.68.act_ref.db_ref), custom_call_target="tpu_custom_call" | custom-call | tf_op jit(solution)/shard_map/pallas_call | solution.py:1012
  352.5 17.9 %shard_map.237 = (f32[1024,1024]{1,0:T(8,128)}, bf16[1024,1024]{1,0:T(8,128)(2,1)}, f32[8,1024]{1,0:T(8,128)}) custom-call(bf16[1024,4096]{1,0:T(8,128)(2,1)} %get-tuple-element.74.da_ref.du_ref, bf16[2,1024,4096]{2,1,0:T(8,128)(2,1)} %bitcast.235, f32[1024,1024]{1,0:T(8,128)} %get-tuple-element.75.dr3_ref, f32[1024,1024]{1,0:T(8,128)} %get-tuple-element.135.n_ref, ...), custom_call_target="tpu_custom_call" | custom-call | tf_op jit(solution)/shard_map/pallas_call | solution.py:971
  370.4 4.1 convolution_convert_fusion.19.do_ref
  374.5 24.1 %shard_map.238 = (bf16[1024,512]{1,0:T(8,128)(2,1)}, bf16[1024,512]{1,0:T(8,128)(2,1)}, bf16[1024,512]{1,0:T(8,128)(2,1)}) custom-call(bf16[1024,512]{1,0:T(8,128)(2,1)} %multiply_convert_fusion.3.q_ref, bf16[1024,1024]{1,0:T(8,128)(2,1)} %add_convert_fusion.3.k_ref.v_ref, bf16[1024,1024]{1,0:T(8,128)(2,1)} %add_convert_fusion.3.k_ref.v_ref, ...), custom_call_target="tpu_custom_call" | custom-call | tf_op jit(solution)/shard_map/pallas_call | solution.py:496
  398.7 3.4 convolution_convert_fusion.17.do_ref
  402.1 23.8 %shard_map.239 = (bf16[1024,512]{1,0:T(8,128)(2,1)}, bf16[1024,512]{1,0:T(8,128)(2,1)}, bf16[1024,512]{1,0:T(8,128)(2,1)}) custom-call(bf16[1024,512]{1,0:T(8,128)(2,1)} %multiply_convert_fusion.2.q_ref, bf16[1024,1024]{1,0:T(8,128)(2,1)} %add_convert_fusion.2.k_ref.v_ref, bf16[1024,1024]{1,0:T(8,128)(2,1)} %add_convert_fusion.2.k_ref.v_ref, ...), custom_call_target="tpu_custom_call" | custom-call | tf_op jit(solution)/shard_map/pallas_call | solution.py:496
  426.0 2.7 fusion.40
  428.8 3.9 multiply_reduce_fusion
  434.5 4.2 convolution_convert_fusion.7.do_ref
  438.7 16.7 %shard_map.241 = (bf16[1024,512]{1,0:T(8,128)(2,1)}, bf16[1024,512]{1,0:T(8,128)(2,1)}, bf16[1024,512]{1,0:T(8,128)(2,1)}) custom-call(bf16[1024,1536]{1,0:T(8,128)(2,1)} %multiply_convert_fusion.q_ref.k_ref.v_ref, bf16[1024,1536]{1,0:T(8,128)(2,1)} %multiply_convert_fusion.q_ref.k_ref.v_ref, bf16[1024,1536]{1,0:T(8,128)(2,1)} %multiply_convert_fusion.q_ref.k_ref.v_ref, ...), custom_call_target="tpu_custom_call" | custom-call | tf_op jit(solution)/shard_map/pallas_call | solution.py:496
  455.4 3.4 convolution_convert_fusion.9.do_ref
  458.9 17.2 %shard_map.240 = (bf16[1024,512]{1,0:T(8,128)(2,1)}, bf16[1024,512]{1,0:T(8,128)(2,1)}, bf16[1024,512]{1,0:T(8,128)(2,1)}) custom-call(bf16[1024,1536]{1,0:T(8,128)(2,1)} %multiply_convert_fusion.1.q_ref.k_ref.v_ref, bf16[1024,1536]{1,0:T(8,128)(2,1)} %multiply_convert_fusion.1.q_ref.k_ref.v_ref, ...), custom_call_target="tpu_custom_call" | custom-call | tf_op jit(solution)/shard_map/pallas_call | solution.py:496
  480.6 2.6 fusion.29
  483.2 2.6 fusion.27
  485.9 2.5 fusion.31
  488.4 2.5 add_convert_fusion.1
  497.3 2.3 convolution_convert_fusion
  499.5 2.3 convolution_convert_fusion.1
  501.9 2.3 convolution_convert_fusion.2
  504.1 2.3 convolution_convert_fusion.3
  506.4 2.3 convolution_convert_fusion.6
  508.8 2.3 convolution_convert_fusion.8
  511.0 2.5 convolution_convert_fusion.10
  513.5 2.3 convolution_convert_fusion.11
  515.8 2.2 convolution_convert_fusion.12
  518.1 2.3 convolution_convert_fusion.13
  520.3 2.3 convolution_convert_fusion.14
  522.6 2.2 convolution_convert_fusion.15
  524.9 2.3 convolution_convert_fusion.16
  527.1 2.3 convolution_convert_fusion.18
  529.4 2.3 convolution_convert_fusion.4
  531.7 2.3 convolution_convert_fusion.5
  534.0 2.5 fusion.16
  536.5 2.5 fusion.18
  539.0 2.7 fusion.20
  541.8 4.5 fusion.22
  546.3 4.6 fusion.24
  550.9 7.5 %add_convert_fusion = bf16[1024,1024]{1,0:T(8,128)(2,1)} fusion(f32[1024,1024]{1,0:T(8,128)S(1)} %get-tuple-element.132, f32[1024,1024]{1,0:T(8,128)S(1)} %fusion.18, f32[1024,1024]{1,0:T(8,128)S(1)} %fusion.16, f32[1024,1024]{1,0:T(8,128)S(1)} %fusion.20, f32[1024,1024]{1,0:T(8,128)} %fusion.24, f32[1024,1024]{1,0:T(8,128)} %fusion.22, ...), kind=kOutput, calls=%fused_computation.3 | convolution fusion | flops 1081081856 | bytes 29360128 | tf_op jit(solution)/shard_map/dot_general | solution.py:1030
  558.4 3.2 maximum_select_fusion.2.refs_17_
  561.6 3.2 maximum_select_fusion.1.refs_16_
  564.9 109.8 %shard_map.242 = (f32[64,4096]{1,0:T(8,128)}, f32[136,128]{1,0:T(8,128)}, bf16[2,512,1024]{2,1,0:T(8,128)(2,1)}) custom-call(bf16[4,2,2,64,512]{4,3,2,1,0:T(8,128)(2,1)} %bitcast.264, bf16[4,2,2,64,512]{4,3,2,1,0:T(8,128)(2,1)} %bitcast.263, bf16[4,2,2,64,512]{4,3,2,1,0:T(8,128)(2,1)} %bitcast.262, bf16[4,2,2,64,512]{4,3,2,1,0:T(8,128)(2,1)} %bitcast.261, ...), custom_call_target="tpu_custom_call" | custom-call | bytes 167772160 | tf_op jit(solution)/shard_map/pallas_call | solution.py:778
  685.8 1.8 slice.293
  (197 shorter events, 35.5 us)
Async XLA Ops:
  7.2 128.8 %copy-start.33 = (bf16[64,2048]{1,0:T(8,128)(2,1)S(1)}, bf16[64,2048]{1,0:T(8,128)(2,1)}, u32[]{:S(2)}) copy-start(bf16[64,2048]{1,0:T(8,128)(2,1)} %param.20) | copy-start | bytes 786436
  7.2 128.8 %copy-start.32 = (bf16[2048,64]{0,1:T(8,128)(2,1)S(1)}, bf16[2048,64]{0,1:T(8,128)(2,1)}, u32[]{:S(2)}) copy-start(bf16[2048,64]{0,1:T(8,128)(2,1)} %param.21) | copy-start | bytes 786436
  7.2 129.7 %copy-start.38 = (bf16[4,512]{1,0:T(4,128)(2,1)S(1)}, bf16[4,512]{1,0:T(4,128)(2,1)}, u32[]{:S(2)}) copy-start(bf16[4,512]{1,0:T(4,128)(2,1)} %param.22) | copy-start | bytes 12292
  7.2 129.7 %copy-start.39 = (bf16[2048]{0:T(1024)(128)(2,1)S(1)}, bf16[2048]{0:T(1024)(128)(2,1)}, u32[]{:S(2)}) copy-start(bf16[2048]{0:T(1024)(128)(2,1)} %param.23) | copy-start | bytes 12292
  7.2 130.4 %copy-start.36 = (bf16[3,1024]{1,0:T(4,128)(2,1)S(1)}, bf16[3,1024]{1,0:T(4,128)(2,1)}, u32[]{:S(2)}) copy-start(bf16[3,1024]{1,0:T(4,128)(2,1)} %param.24) | copy-start | bytes 18436
  7.2 130.4 %copy-start.35 = (bf16[6,1024]{1,0:T(8,128)(2,1)S(1)}, bf16[6,1024]{1,0:T(8,128)(2,1)}, u32[]{:S(2)}) copy-start(bf16[6,1024]{1,0:T(8,128)(2,1)} %param.25) | copy-start | bytes 36868
  7.2 242.5 %all-gather.2.cloned.1.call-start = ((), (), s32[]{:S(2)}) async-start(), calls=%async_computation.1 | async-start | bytes 17301504 | tf_op jit(solution)/shard_map/all_gather | solution.py:1101
  8.3 132.6 %copy-start.49 = (f32[1536]{0:T(1024)S(1)}, f32[1536]{0:T(1024)}, u32[]{:S(2)}) copy-start(f32[1536]{0:T(1024)} %constant.48.clone.1) | copy-start | bytes 18436
  136.9 547.0 %reduce-scatter.2.cloned.1.call-start = ((), (), s32[]{:S(2)}) async-start(), calls=%async_computation.2 | async-start | bytes 17301504 | tf_op jit(solution)/shard_map/reduce_scatter | solution.py:1176
  137.0 3.7 collective-permute-start
  148.6 12.2 %copy-start.18 = (bf16[2,512,1024]{2,1,0:T(8,128)(2,1)S(1)}, bf16[2,512,1024]{2,1,0:T(8,128)(2,1)}, u32[]{:S(2)}) copy-start(bf16[2,512,1024]{2,1,0:T(8,128)(2,1)} %get-tuple-element.57) | copy-start | bytes 6291460
  167.5 12.6 %copy-start.30 = (bf16[1024,512]{1,0:T(8,128)(2,1)S(1)}, bf16[1024,512]{1,0:T(8,128)(2,1)}, u32[]{:S(2)}) copy-start(bf16[1024,512]{1,0:T(8,128)(2,1)} %get-tuple-element.60.o_ref) | copy-start | bytes 3145732
  180.2 2.6 copy-start.9
  185.7 58.8 %copy-start = (f32[1024,1024]{1,0:T(8,128)}, f32[1024,1024]{1,0:T(8,128)S(1)}, u32[]{:S(2)}) copy-start(f32[1024,1024]{1,0:T(8,128)S(1)} %get-tuple-element.178) | copy-start | bytes 12582916
  187.0 27.8 %copy-start.11 = (bf16[1024,1024]{1,0:T(8,128)(2,1)}, bf16[1024,1024]{1,0:T(8,128)(2,1)S(1)}, u32[]{:S(2)}) copy-start(bf16[1024,1024]{1,0:T(8,128)(2,1)S(1)} %fusion) | copy-start | bytes 6291460
  187.0 4.3 copy-start.40
  214.8 3.6 copy-start.41
  241.3 3.2 copy-start.20
  244.5 5.2 copy-start.15
  249.7 2.2 copy-start.2
  249.9 37.8 %collective-permute-start.1 = (bf16[512,1024]{1,0:T(8,128)(2,1)S(1)}, bf16[512,1024]{1,0:T(8,128)(2,1)S(1)}, u32[]{:S(2)}, u32[]{:S(2)}) collective-permute-start(bf16[512,1024]{1,0:T(8,128)(2,1)S(1)} %get-tuple-element.141), channel_id=1, source_target_pairs={{0,1},{1,0},{2,3},{3,2},{4,5},{5,4},{6,7},{7,6},{8,9},{9,8},{10,11... | collective-permute-start | bytes 3145736 | tf_op jit(solution)/shard_map/ppermute | solution.py:1051
  374.5 24.2 %copy-start.43 = (bf16[1024,1024]{1,0:T(8,128)(2,1)S(1)}, bf16[1024,1024]{1,0:T(8,128)(2,1)}, u32[]{:S(2)}) copy-start(bf16[1024,1024]{1,0:T(8,128)(2,1)} %get-tuple-element.76) | copy-start | bytes 6291460
  402.1 23.8 %copy-start.23 = (bf16[1024,512]{1,0:T(8,128)(2,1)S(1)}, bf16[1024,512]{1,0:T(8,128)(2,1)}, u32[]{:S(2)}) copy-start(bf16[1024,512]{1,0:T(8,128)(2,1)} %get-tuple-element.78) | copy-start | bytes 3145732
  402.1 26.5 %copy-start.8 = (f32[1024,1024]{1,0:T(8,128)S(1)}, f32[1024,1024]{1,0:T(8,128)}, u32[]{:S(2)}) copy-start(f32[1024,1024]{1,0:T(8,128)} %get-tuple-element.85) | copy-start | bytes 12582916
  426.0 2.7 copy-start.1
  426.0 2.9 copy-start.3
  434.5 20.9 %copy-start.13 = (bf16[1024,1024]{1,0:T(8,128)(2,1)}, bf16[1024,1024]{1,0:T(8,128)(2,1)S(1)}, u32[]{:S(2)}) copy-start(bf16[1024,1024]{1,0:T(8,128)(2,1)S(1)} %convert_element_type.159) | copy-start | bytes 6291460
  458.9 17.3 %copy-start.26 = (bf16[1024,512]{1,0:T(8,128)(2,1)S(1)}, bf16[1024,512]{1,0:T(8,128)(2,1)}, u32[]{:S(2)}) copy-start(bf16[1024,512]{1,0:T(8,128)(2,1)} %get-tuple-element.89) | copy-start | bytes 3145732
  458.9 19.1 %copy-start.5 = (bf16[1024,512]{1,0:T(8,128)(2,1)S(1)}, bf16[1024,512]{1,0:T(8,128)(2,1)}, u32[]{:S(2)}) copy-start(bf16[1024,512]{1,0:T(8,128)(2,1)} %get-tuple-element.93) | copy-start | bytes 3145732
  476.1 3.8 copy-start.24
  476.2 4.0 copy-start.4
  476.2 4.2 copy-start.25
  480.6 2.6 copy-start.46
  483.2 2.6 copy-start.45
  491.0 2.4 copy-start.16
  491.0 4.4 copy-start.37
  491.0 6.2 copy-start.10
  491.0 6.2 copy-start.14
  492.1 66.3 %collective-permute-start.3 = (bf16[1,512,1024]{2,1,0:T(8,128)(2,1)}, bf16[1,512,1024]{2,1,0:T(8,128)(2,1)}, u32[]{:S(2)}, u32[]{:S(2)}) collective-permute-start(bf16[1,512,1024]{2,1,0:T(8,128)(2,1)} %get-tuple-element.137), channel_id=1, source_target_pairs={{0,1},{1,0},{2,3},{3,2},{4,5},{5,4},{6,7},{7,6},{8,9},{9,8},{10,11... | collective-permute-start | bytes 3145736 | tf_op jit(solution)/shard_map/ppermute | solution.py:1051
  494.5 67.2 %collective-permute-start.2 = (bf16[1,512,1024]{2,1,0:T(8,128)(2,1)}, bf16[1,512,1024]{2,1,0:T(8,128)(2,1)}, u32[]{:S(2)}, u32[]{:S(2)}) collective-permute-start(bf16[1,512,1024]{2,1,0:T(8,128)(2,1)} %get-tuple-element.139), channel_id=1, source_target_pairs={{0,1},{1,0},{2,3},{3,2},{4,5},{5,4},{6,7},{7,6},{8,9},{9,8},{10,11... | collective-permute-start | bytes 3145736 | tf_op jit(solution)/shard_map/ppermute | solution.py:1051
  497.2 2.3 copy-start.34
  497.2 2.3 copy-start.31
  499.5 2.3 copy-start.6
  499.5 2.3 copy-start.19
  501.9 2.3 copy-start.29
  504.1 2.3 copy-start.27
  506.4 2.3 copy-start.28
  508.8 2.3 copy-start.21
  508.8 2.3 copy-start.44
  511.0 2.5 copy-start.22
  513.5 2.3 copy-start.42
  522.6 2.3 copy-start.12
  527.1 2.3 copy-start.47
  529.4 2.3 copy-start.48
  546.3 4.7 copy-start.7
  674.7 12.9 %copy-start.17 = (bf16[2,512,1024]{2,1,0:T(8,128)(2,1)S(1)}, bf16[2,512,1024]{2,1,0:T(8,128)(2,1)}, u32[]{:S(2)}) copy-start(bf16[2,512,1024]{2,1,0:T(8,128)(2,1)} %get-tuple-element.199) | copy-start | bytes 6291460
Sparse Core Ops, SparseCore 0:
  137.0 112.6 all-gather.1
  351.6 181.4 reduce-scatter.1

commit v4 on v3

--- a/solution.py
+++ b/solution.py
@@ -408,37 +408,38 @@
 f32=jnp.float32
 bf16=jnp.bfloat16
 
-def scores_t(k_h,q,i,bq,causal):
-    s=lax.dot_general(k_h,q,NT,preferred_element_type=f32)
-    return s
+LN2 = 0.6931471805599453
+LOG2E = 1.4426950408889634
+
 
 def att_fwd_kernel(q_ref,k_ref,v_ref,o_ref,lse_ref,*,bq,causal):
     n=q_ref.shape[0]; nk=k_ref.shape[0]
     lane=lax.broadcasted_iota(jnp.int32,(nk,128),1)
-    k=k_ref[...]; v=v_ref[...]
+    k=k_ref[...]
     zero=jnp.zeros((),bf16)
     kh=[jnp.where(lane<HD,k,zero),jnp.where(lane>=HD,k,zero)]
-    vt=v.astype(f32).T.astype(bf16)
+    vt=v_ref[...].T
     ones=jnp.ones((8,nk),bf16)
     vh=[jnp.concatenate([vt[h*HD:(h+1)*HD],ones],0) for h in range(2)]
     for i in range(n//bq):
         q=q_ref[i*bq:(i+1)*bq,:]
         L=(i+1)*bq if causal else nk
-        outs=[];lses=[]
+        S=[]
         for h in range(2):
             s=lax.dot_general(kh[h][:L],q,NT,preferred_element_type=f32)
             if causal:
                 keep=lax.broadcasted_iota(jnp.int32,(bq,bq),0)<=lax.broadcasted_iota(jnp.int32,(bq,bq),1)
                 sd=jnp.where(keep,s[L-bq:],-1e30)
                 s=jnp.concatenate([s[:L-bq],sd],0) if L>bq else sd
-            m=jnp.max(s,0,keepdims=True)
-            p=jnp.exp(s-m).astype(bf16)
+            S.append(s)
+        M=[jnp.max(s,0,keepdims=True) for s in S]
+        outs=[];lses=[]
+        for h in range(2):
+            p=jnp.exp2(S[h]-M[h]).astype(bf16)
             ol=lax.dot_general(vh[h][:,:L],p,NN,preferred_element_type=f32)
             l=ol[HD:HD+1]
-            outs.append(ol[:HD]*(1.0/l))
-            lses.append(m+jnp.log(l))
-        ot=jnp.concatenate(outs,0)
-        o_ref[i*bq:(i+1)*bq,:]=ot.T.astype(bf16)
+            outs.append(ol[:HD]*(1.0/l)); lses.append(M[h]+jnp.log2(l))
+        o_ref[i*bq:(i+1)*bq,:]=jnp.concatenate(outs,0).T.astype(bf16)
         lse_ref[0,:,i*bq:(i+1)*bq]=jnp.concatenate(lses,0)
 
 def att_fwd(q,k,v,causal,bq=256,qo=0,ko=0,vo=0,width=None):
@@ -453,7 +454,8 @@
         compiler_params=pltpu.CompilerParams(dimension_semantics=("arbitrary",),vmem_limit_bytes=56*2**20),
     )(q,k,v)
 
-def att_bwd_kernel(q_ref,k_ref,v_ref,o_ref,do_ref,lse_ref,dq_ref,dk_ref,dv_ref,dk_acc,dv_acc,*,bq,causal):
+def att_bwd_kernel(q_ref,k_ref,v_ref,o_ref,do_ref,lse_ref,*refs,bq,causal):
+    dq_ref,dk_ref,dv_ref,dk_acc,dv_acc=refs[-5:]
     n=q_ref.shape[0]; nk=k_ref.shape[0]
     lane=lax.broadcasted_iota(jnp.int32,(nk,128),1)
     lq=lax.broadcasted_iota(jnp.int32,(bq,128),1)
@@ -461,7 +463,7 @@
     zero=jnp.zeros((),bf16)
     kh=[jnp.where(lane<HD,k,zero),jnp.where(lane>=HD,k,zero)]
     vh=[jnp.where(lane<HD,v,zero),jnp.where(lane>=HD,v,zero)]
-    kt=k.astype(f32).T.astype(bf16)
+    kt=k.T
     dk_acc[...]=jnp.zeros_like(dk_acc); dv_acc[...]=jnp.zeros_like(dv_acc)
     for i in range(n//bq):
         rows=slice(i*bq,(i+1)*bq)
@@ -480,28 +482,28 @@
                 keep=lax.broadcasted_iota(jnp.int32,(bq,bq),0)<=lax.broadcasted_iota(jnp.int32,(bq,bq),1)
                 sd=jnp.where(keep,s[L-bq:],-1e30)
                 s=jnp.concatenate([s[:L-bq],sd],0) if L>bq else sd
-            p=jnp.exp(s-lse)
+            p=jnp.exp2(s-lse)
             ds=(p*(dp-delta)).astype(bf16)
             pb=p.astype(bf16)
             dv_acc[:L,:]+=lax.dot_general(pb,dm[h],NN,preferred_element_type=f32)
             dk_acc[:L,:]+=lax.dot_general(ds,qm[h],NN,preferred_element_type=f32)
             dqs.append(lax.dot_general(kt[h*HD:(h+1)*HD,:L],ds,NN,preferred_element_type=f32))
         dq_ref[rows,:]=(jnp.concatenate(dqs,0)*0.125).T.astype(bf16)
-    dk_ref[...]=dk_acc[...].astype(bf16)
+    dk_ref[...]=(dk_acc[...]*LN2).astype(bf16)
     dv_ref[...]=dv_acc[...].astype(bf16)
 
-def att_bwd(q,k,v,o,do,lse,causal,bq=256,qo=0,ko=0,vo=0):
+def att_bwd(q,k,v,o,do,lse,causal,bq=256,qo=0,ko=0,vo=0,ahead=()):
     n=q.shape[0]; nk=k.shape[0]; width=o.shape[1]; np_=width//128
     spec=lambda rows,off: pl.BlockSpec((rows,128),lambda p: (0,p+off))
     return pl.pallas_call(
         functools.partial(att_bwd_kernel,bq=bq,causal=causal),
         grid=(np_,),
-        in_specs=[spec(n,qo),spec(nk,ko),spec(nk,vo),spec(n,0),spec(n,0),pl.BlockSpec((1,2,n),lambda p:(p,0,0))],
+        in_specs=[spec(n,qo),spec(nk,ko),spec(nk,vo),spec(n,0),spec(n,0),pl.BlockSpec((1,2,n),lambda p:(p,0,0))]+[pl.BlockSpec(memory_space=pl.ANY)]*len(ahead),
         out_specs=[spec(n,0),spec(nk,0),spec(nk,0)],
         out_shape=[jax.ShapeDtypeStruct((n,width),bf16),jax.ShapeDtypeStruct((nk,width),bf16),jax.ShapeDtypeStruct((nk,width),bf16)],
         scratch_shapes=[pltpu.VMEM((nk,128),f32)]*2,
         compiler_params=pltpu.CompilerParams(dimension_semantics=("arbitrary",),vmem_limit_bytes=56*2**20),
-    )(q,k,v,o,do,lse)
+    )(q,k,v,o,do,lse,*ahead)
 
 
 MESH = pl.DeviceIdType.MESH
@@ -533,7 +535,7 @@
     pl.semaphore_wait(barrier, len(LINKS))
 
 
-def pipeline(chunks, stages, begin):
+def pipeline(chunks, stages, begin, after_step=None):
     started = {}
     for step in range(chunks + stages):
         for s in range(stages + 1):
@@ -543,6 +545,8 @@
                     for copy in started[k, s - 1]:
                         copy.wait_recv()
                 started[k, s] = begin(k, s)
+        if after_step is not None:
+            after_step(step)
     for copies in started.values():
         for copy in copies:
             copy.wait_send()
@@ -644,27 +648,27 @@
     return whole, [p.reshape(p.shape[0] * p.shape[1], p.shape[2]) for p in outs[1:]]
 
 
-def scatter_kernel(*refs, chunks, ahead):
-    g_refs, refs = refs[: 2 * chunks], refs[2 * chunks + ahead :]
-    rows_ref, small_ref, out_ref, small_out, pieces_ref, own, r1 = refs[:7]
-    s2, r2, k2, s3, r3, k3, s4, r4, k4, s5, r5 = refs[7:18]
-    sm, rm, send, recv, own_sem, small_send, small_recv, swap_send, swap_recv, swap_own = refs[18:]
+def scatter_kernel(*refs, given, ahead, wa):
+    g_refs, refs = refs[: 2 * given], refs[2 * given :]
+    made = 4
+    lefts, rights, refs = refs[:2], refs[2 : 2 + 2 * made], refs[2 + 2 * made + ahead :]
+    rows_ref, small_ref, out_ref, small_out, pieces_ref = refs[:5]
+    own, far, turned, r1, s2, r2, s3, r3, s4, r4, s5, r5, sm, rm = refs[5:19]
+    send, recv, own_sem, small_send, small_recv, swap_send, swap_recv, swap_own = refs[19:]
+    chunks = given + made
     (t, z, y, c), ids = partners()
     pair = (z // 2) * 2
     away = 2 - pair
     other = 1 - z % 2
-    rows = own.shape[3]
-    cw = own.shape[4] // chunks
-    h = cw // 2
+    rows, cw = r5.shape[1:]
+    sides = (slice(0, wa), slice(wa, cw))
 
     def loc(k, half):
         return pltpu.make_async_copy(
-            g_refs[2 * k + half].at[:, :, c],
-            own.at[half, :, :, :, pl.ds(k * cw, cw)],
-            own_sem.at[k, half],
+            g_refs[2 * k + half].at[:, :, c], own.at[k, half], own_sem.at[k, half]
         )
 
-    for k in range(chunks):
+    for k in range(given):
         loc(k, 0).start()
         loc(k, 1).start()
     kept = pltpu.make_async_copy(rows_ref.at[t], pieces_ref.at[t], swap_own)
@@ -682,58 +686,59 @@
     def up(v):
         return v.astype(f32)
 
+    def after_core(k, t_, z_, y_, cols):
+        return up(own[k, t_, z_, y_, :, cols]) + up(r1[k, t_, z_, y_, :, cols])
+
+    def after_two(k, z_, y_, t_, j):
+        at = 2 * z_ + y_ if j == 0 else 4 * t_ + z_
+        return after_core(k, t_, z_, y_, sides[j]) + up(r2[k, at, :, sides[j]])
+
+    def after_three(k, z_, j):
+        return after_two(k, z_, y, t, j) + up(r3[k, z_, :, sides[j]])
+
     def begin(k, s):
-        ca = slice(k * cw, k * cw + h)
-        cb = slice(k * cw + h, (k + 1) * cw)
+        a, b = sides
         if s == 0:
-            cols = pl.ds(k * cw, cw)
-            return [
-                go(k, 7 * half, g_refs[2 * k + half].at[:, :, 1 - c], r1.at[half, :, :, :, cols], "c")
-                for half in (0, 1)
-            ]
+            copies = []
+            for half in (0, 1):
+                src = g_refs[2 * k + half].at[:, :, 1 - c] if k < given else far.at[k - given, half]
+                copies.append(go(k, 6 + half, src, r1.at[k, half], "c"))
+            return copies
         if s == 1:
-            loc(k, 0).wait()
-            loc(k, 1).wait()
-            shape = (8, rows, h)
-            sent = up(own[1 - t, :, :, :, ca]) + up(r1[1 - t, :, :, :, ca])
-            s2[k, 0] = sent.astype(bf16).reshape(shape)
-            da = go(k, 1, s2.at[k, 0], r2.at[k, 0], "x")
-            sent = up(own[:, :, 1 - y, :, cb]) + up(r1[:, :, 1 - y, :, cb])
-            s2[k, 1] = sent.astype(bf16).reshape(shape)
-            db = go(k, 2, s2.at[k, 1], r2.at[k, 1], "y")
-            k2[k, 0] = (up(own[t, :, :, :, ca]) + up(r1[t, :, :, :, ca])).reshape(shape)
-            k2[k, 1] = (up(own[:, :, y, :, cb]) + up(r1[:, :, y, :, cb])).reshape(shape)
-            return [da, db]
+            if k < given:
+                loc(k, 0).wait()
+                loc(k, 1).wait()
+            for z_ in range(4):
+                for i in range(2):
+                    s2[k, 2 * z_ + i, :, a] = after_core(k, 1 - t, z_, i, a).astype(bf16)
+            da = go(k, 0, s2.at[k, :, :, pl.ds(0, wa)], r2.at[k, :, :, pl.ds(0, wa)], "x")
+            for z_ in range(4):
+                for i in range(2):
+                    s2[k, 4 * i + z_, :, b] = after_core(k, i, z_, 1 - y, b).astype(bf16)
+            side = pl.ds(wa, cw - wa)
+            return [da, go(k, 1, s2.at[k, :, :, side], r2.at[k, :, :, side], "y")]
         if s == 2:
-            for i in range(4):
-                j = 2 * i + 1 - y
-                s3[k, 0, i] = (k2[k, 0, j] + up(r2[k, 0, j])).astype(bf16)
-            da = go(k, 3, s3.at[k, 0], r3.at[k, 0], "y")
-            for i in range(4):
-                j = 4 * (1 - t) + i
-                s3[k, 1, i] = (k2[k, 1, j] + up(r2[k, 1, j])).astype(bf16)
-            db = go(k, 4, s3.at[k, 1], r3.at[k, 1], "x")
-            for i in range(4):
-                k3[k, 0, i] = k2[k, 0, 2 * i + y] + up(r2[k, 0, 2 * i + y])
-                k3[k, 1, i] = k2[k, 1, 4 * t + i] + up(r2[k, 1, 4 * t + i])
-            return [da, db]
+            for z_ in range(4):
+                s3[k, z_, :, a] = after_two(k, z_, 1 - y, t, 0).astype(bf16)
+            da = go(k, 2, s3.at[k, :, :, pl.ds(0, wa)], r3.at[k, :, :, pl.ds(0, wa)], "y")
+            for z_ in range(4):
+                s3[k, z_, :, b] = after_two(k, z_, y, 1 - t, 1).astype(bf16)
+            side = pl.ds(wa, cw - wa)
+            return [da, go(k, 3, s3.at[k, :, :, side], r3.at[k, :, :, side], "x")]
         if s == 3:
-            for j in range(2):
-                for i in range(2):
-                    s4[k, j, i] = (k3[k, j, away + i] + up(r3[k, j, away + i])).astype(bf16)
-            d = go(k, 5, s4.at[k], r4.at[k], "z2")
-            for j in range(2):
-                for i in range(2):
-                    k4[k, j, i] = k3[k, j, pair + i] + up(r3[k, j, pair + i])
-            return [d]
-        if s == 4:
-            for j in range(2):
-                s5[k, j] = (k4[k, j, other] + up(r4[k, j, other])).astype(bf16)
-            return [go(k, 6, s5.at[k], r5.at[k], "z1")]
+            for i in range(2):
+                for j in range(2):
+                    s4[k, i, :, sides[j]] = after_three(k, away + i, j).astype(bf16)
+            return [go(k, 4, s4.at[k], r4.at[k], "z2")]
         for j in range(2):
-            mine = k4[k, j, z % 2] + up(r4[k, j, z % 2]) + up(r5[k, j])
-            out_ref[:, k * cw + j * h : k * cw + (j + 1) * h] = mine
-        return []
+            if s == 4:
+                sent = after_three(k, pair + other, j) + up(r4[k, other, :, sides[j]])
+                s5[k, :, sides[j]] = sent.astype(bf16)
+            else:
+                mine = after_three(k, z, j) + up(r4[k, z % 2, :, sides[j]])
+                cols = slice(k * cw + sides[j].start, k * cw + sides[j].stop)
+                out_ref[:, cols] = mine + up(r5[k, :, sides[j]])
+        return [go(k, 5, s5.at[k], r5.at[k], "z1")] if s == 4 else []
 
     smalls = []
 
@@ -757,7 +762,22 @@
                 smalls.append(small_go(s))
         return begin(k, s)
 
-    pipeline(chunks, 5, begin_with_small)
+    def make(step):
+        if step == 1:
+            turned[...] = lefts[0][...].T
+        elif step == made + 2:
+            turned[...] = lefts[1][...].T
+        ready = {2: [(0, 0)], 3: [(0, 1)]}
+        for i in range(1, made):
+            ready[3 + i] = [(i, 0), (i, 1)]
+        for i, half in ready.get(step, []):
+            d = rights[2 * i + half][...]
+            g = lax.dot_general(turned[...], d, NN, preferred_element_type=f32)
+            g = g.astype(bf16).reshape(4, 2, 2, rows, cw)
+            own[given + i, half] = jnp.where(c == 0, g[:, :, 0], g[:, :, 1])
+            far[i, half] = jnp.where(c == 0, g[:, :, 1], g[:, :, 0])
+
+    pipeline(chunks, 5, begin_with_small, make)
     for copy in smalls:
         copy.wait_send()
     for copy in traded:
@@ -765,10 +785,12 @@
     kept.wait()
 
 
-def scatter_grads(pairs, ahead, seq_rows, small, cid):
-    chunks = len(pairs)
-    width, cw = pairs[0][0].shape
-    rows, h, cols = width // 16, cw // 2, cw * chunks
+def scatter_grads(pairs, lefts, rights, ahead, seq_rows, small, cid):
+    given = len(pairs)
+    chunks = given + 4
+    tokens, width = lefts[0].shape
+    cw = pairs[0][0].shape[1]
+    rows, cols = width // 16, cw * chunks
     V = pltpu.VMEM
     dma = pltpu.SemaphoreType.DMA
     flat = [g.reshape(4, 2, 2, rows, cw) for pair in pairs for g in pair]
@@ -776,8 +798,11 @@
     whole = pl.BlockSpec(memory_space=pltpu.VMEM)
     anywhere = pl.BlockSpec(memory_space=pl.ANY)
     return pl.pallas_call(
-        functools.partial(scatter_kernel, chunks=chunks, ahead=len(ahead)),
-        in_specs=[anywhere] * (len(flat) + len(ahead) + 1) + [whole],
+        functools.partial(scatter_kernel, given=given, ahead=len(ahead), wa=cw // 4),
+        in_specs=[anywhere] * len(flat)
+        + [whole] * (2 + len(rights))
+        + [anywhere] * (len(ahead) + 1)
+        + [whole],
         out_specs=[whole, whole, anywhere],
         out_shape=[
             jax.ShapeDtypeStruct((rows, cols), f32),
@@ -785,24 +810,23 @@
             jax.ShapeDtypeStruct(seq_rows.shape, seq_rows.dtype),
         ],
         scratch_shapes=[
-            V((2, 4, 2, rows, cols), bf16),
-            V((2, 4, 2, rows, cols), bf16),
-            V((chunks, 2, 8, rows, h), bf16),
-            V((chunks, 2, 8, rows, h), bf16),
-            V((chunks, 2, 8, rows, h), f32),
-            V((chunks, 2, 4, rows, h), bf16),
-            V((chunks, 2, 4, rows, h), bf16),
-            V((chunks, 2, 4, rows, h), f32),
-            V((chunks, 2, 2, rows, h), bf16),
-            V((chunks, 2, 2, rows, h), bf16),
-            V((chunks, 2, 2, rows, h), f32),
-            V((chunks, 2, rows, h), bf16),
-            V((chunks, 2, rows, h), bf16),
+            V((chunks, 2, 4, 2, rows, cw), bf16),
+            V((4, 2, 4, 2, rows, cw), bf16),
+            V((width, tokens), bf16),
+            V((chunks, 2, 4, 2, rows, cw), bf16),
+            V((chunks, 8, rows, cw), bf16),
+            V((chunks, 8, rows, cw), bf16),
+            V((chunks, 4, rows, cw), bf16),
+            V((chunks, 4, rows, cw), bf16),
+            V((chunks, 2, rows, cw), bf16),
+            V((chunks, 2, rows, cw), bf16),
+            V((chunks, rows, cw), bf16),
+            V((chunks, rows, cw), bf16),
             V((5,) + small.shape, f32),
             V((5,) + small.shape, f32),
             dma((chunks, 8)),
             dma((chunks, 8)),
-            dma((chunks, 2)),
+            dma((given, 2)),
             dma((5,)),
             dma((5,)),
             dma((chunks,)),
@@ -810,12 +834,12 @@
             dma,
         ],
         compiler_params=pltpu.CompilerParams(
-            collective_id=cid, has_side_effects=True, vmem_limit_bytes=60 * 2**20
+            collective_id=cid, has_side_effects=True, vmem_limit_bytes=62 * 2**20
         ),
         cost_estimate=pl.CostEstimate(
             flops=0, bytes_accessed=32 * rows * cols * 20, transcendentals=0
         ),
-    )(*flat, *ahead, seq_rows, small)
+    )(*flat, *lefts, *rights, *ahead, seq_rows, small)
 
 
 ERFC_SLOPE = 0.44
@@ -844,8 +868,8 @@
 
 
 def up_kernel(x_ref, w_ref, b_ref, act_ref, slope_ref):
-    for i in range(4):
-        rows = slice(256 * i, 256 * (i + 1))
+    for i in range(8):
+        rows = slice(128 * i, 128 * (i + 1))
         u = lax.dot_general(x_ref[rows, :], w_ref[0], NN, preferred_element_type=f32) + b_ref[...]
         g, d = gelu_and_slope(u)
         act_ref[rows, :] = g.astype(bf16)
@@ -989,6 +1013,35 @@
     )(du, w, dr3, n, inv, vecs)
 
 
+def products_kernel(*refs, count, based):
+    total = refs[2 * count][...] if based else 0.0
+    for i in range(count):
+        total = total + lax.dot_general(
+            refs[i][...], refs[count + i][0], NT, preferred_element_type=f32
+        )
+    refs[-1][...] = total.astype(refs[-1].dtype)
+
+
+def sum_of_products(lefts, w, places, base, block):
+    rows, cols = lefts[0].shape
+    width = w.shape[1]
+    row = pl.BlockSpec((block, width), lambda i: (i, 0))
+    left = pl.BlockSpec((block, cols), lambda i: (i, 0))
+
+    def weight(t, j):
+        return pl.BlockSpec((1, width, cols), lambda i: (t, 0, j), pipeline_mode=pl.Buffered(1))
+
+    based = [] if base is None else [base]
+    return pl.pallas_call(
+        functools.partial(products_kernel, count=len(lefts), based=len(based)),
+        grid=(rows // block,),
+        in_specs=[left] * len(lefts) + [weight(t, j) for t, j in places] + [row] * len(based),
+        out_specs=row,
+        out_shape=jax.ShapeDtypeStruct((rows, width), bf16),
+        compiler_params=pltpu.CompilerParams(vmem_limit_bytes=40 * 2**20),
+    )(*lefts, *([w] * len(lefts)), *based)
+
+
 def weight_grads_kernel(a_ref,b_ref,da_ref,db_ref,out_ref,at,bt,*,tiles):
     j=pl.program_id(0)
     @pl.when(j==0)
@@ -1119,7 +1172,7 @@
         ),
         (layer_in, memory),
         1,
-        8,
+        16,
     )
     g_att, w_up, w_down = lax.optimization_barrier((g_att, w_up, w_down))
     g_self, g_cross = g_att[:, :, :c4], g_att[:, :, c4:]
@@ -1129,7 +1182,7 @@
     xf = x.astype(f32)
     halves = (0, 1)
     zero = jnp.zeros((cols,), f32)
-    scale3 = jnp.concatenate([zero + ATT_SCALE, zero + 1.0, zero + 1.0])
+    scale3 = jnp.concatenate([zero + ATT_SCALE * LOG2E, zero + 1.0, zero + 1.0])
     blk = cols // 128
 
     sy, sa, sl = [], [], []
@@ -1147,7 +1200,7 @@
     cq, ckv, ca, cl = [], [], [], []
     for t in halves:
         kv = (nn(mem, g_cross[t, :, cols:c3]) + jnp.concatenate([zero, hb[t, 3]])).astype(bf16)
-        q = ((nn(h1b, g_cross[t, :, :cols]) + hb[t, 2]) * ATT_SCALE).astype(bf16)
+        q = ((nn(h1b, g_cross[t, :, :cols]) + hb[t, 2]) * (ATT_SCALE * LOG2E)).astype(bf16)
         o, lse = att_fwd(q, kv, kv, False, 512, 0, 0, blk, cols)
         cq.append(q)
         ckv.append(kv)
@@ -1170,7 +1223,7 @@
     gg3, gs3, gb3 = sums3[0], sums3[1], sums3[2]
     mixed = to_pieces(mixed_rows, place)
 
-    du, gu = hidden_units_back(e3, g_ffn, slope, 512)
+    du, gu = hidden_units_back(e3, g_ffn, slope, 1024)
     grad_ffn = weight_grads(h2b, e3, du, act, 1024)
     grad_ffn, du = lax.optimization_barrier((grad_ffn, du))
     s_ffn = lax.psum_scatter(
@@ -1201,11 +1254,10 @@
         tuple(low(tn(mem, dcv[t])) for t in halves),
         tuple(low(tn(e2, ca[t])) for t in halves),
     ]
-    dmem = sum(
-        nt(dck[t], g_cross[t, :, cols : 2 * cols]) + nt(dcv[t], g_cross[t, :, 2 * cols : c3])
-        for t in halves
-    )
-    d_memory = to_pieces(dmem.astype(bf16), place)
+    dmem = sum_of_products(
+        dck + dcv, g_att, [(t, j) for j in (5, 6) for t in halves], None, 256
+    )
+    d_memory = to_pieces(dmem, place)
     dh1 = dr2 + (nt(dcq[0], g_cross[0, :, :cols]) + nt(dcq[1], g_cross[1, :, :cols]))
     dr1, gg1, gs1, gb1 = norm_rows_back(dh1, n1, i1, gains[0])
     e1 = dr1.astype(bf16)
@@ -1214,21 +1266,13 @@
     for t in halves:
         da = nn(e1, g_self[t, :, c3:]).astype(bf16)
         y = sy[t]
-        a, b, c = att_bwd(y, y, y, sa[t], da, sl[t], True, 256, 0, blk, 2 * blk)
+        ahead = (mixed, dmem) if t == 0 else ()
+        a, b, c = att_bwd(y, y, y, sa[t], da, sl[t], True, 256, 0, blk, 2 * blk, ahead)
         dsq.append(a)
         dsk.append(b)
         dsv.append(c)
-    grads += [
-        tuple(low(tn(x, dsq[t])) for t in halves),
-        tuple(low(tn(x, dsk[t])) for t in halves),
-        tuple(low(tn(x, dsv[t])) for t in halves),
-        tuple(low(tn(e1, sa[t])) for t in halves),
-    ]
-    dx = dr1 + sum(
-        nt(dsq[t], g_self[t, :, :cols])
-        + nt(dsk[t], g_self[t, :, cols : 2 * cols])
-        + nt(dsv[t], g_self[t, :, 2 * cols : c3])
-        for t in halves
+    dx = sum_of_products(
+        dsq + dsk + dsv, g_att, [(t, j) for j in range(3) for t in halves], dr1, 256
     )
 
     def col_sums(pair):
@@ -1241,8 +1285,9 @@
             for v in (gh, gu, gg1, gg2, gg3, gb1, gb2, gb3, gs1, gs2, gs3)
         ]
     )
+    made = [dsq[0], dsq[1], dsk[0], dsk[1], dsv[0], dsv[1], sa[0], sa[1]]
     s_att, flat, d_layer_in = scatter_grads(
-        grads, (mixed, d_memory), dx.astype(bf16), flat.reshape(-1, 128), 2
+        grads, (x, e1), made, (d_memory,), dx, flat.reshape(-1, 128), 2
     )
     flat = flat.reshape(-1)
     head_sum = lax.dynamic_index_in_dim(flat[: 8 * cols].reshape(2, 4, cols), place, 0, False)

time: 701 us -> 661 us (0.943)
  matrix products: 139 us -> 85.9 us
  waiting for transfers between devices: 2.6 us -> 14.5 us
  Pallas kernels: 487 us -> 477 us
  local copies, waits for them, and re-layouts: 22.3 us -> 31.5 us
    dot_general x16 -> x6, matrix products: 54.8 us -> 19.9 us  [nt(): return lax.dot_general(a, b, NT, preferred_element_type=f32)]
    dot_general x16 -> x8, matrix products: 36.7 us -> 18.3 us  [tn(): lax.dot_general(a, b, (((0,), (0,)), ((), ())), preferred_element_type=f32)]
    pallas_call x1 -> x3, Pallas kernels: 110 us -> 126 us  [the longest x1 108 us: scatter_grads(): pl.pallas_call(functools.partial(scatter_kernel, given=given, ahead=len(a...]
    pallas_call x4, Pallas kernels: 60 us -> 48 us  [att_fwd(): pl.pallas_call(functools.partial(att_fwd_kernel, bq=bq, causal=causal), g...]
    all_gather x1, waiting for transfers between devices: 0.28 us -> 12.2 us  [gather(): both = lax.all_gather(mine, ('tp', 'fsdp'), axis=0, tiled=True)]
    pallas_call x1, Pallas kernels: 125 us -> 115 us  [gather_weights(): pl.pallas_call(functools.partial(gather_kernel, cw=cols // chunks, chunks...]
    unnamed x115 -> x119, local copies, waits for them, and re-layouts: 3.05 us -> 11.5 us
  transfers between devices with their start and end apart: 6 -> 6, of which waited for: 2 -> 2; matrix products, arithmetic and copies ran while one was open for 25% -> 19% of each run, Pallas kernels for 43% -> 46%
where the time goes in v4:
time: 661 us; the launch traced here: 656 us
  Pallas kernels  477 us (72%)
  matrix products  85.9 us (13%)
  local copies, waits for them, and re-layouts  31.5 us (5%)
  other arithmetic  28.4 us (4%)
  between operations  15 us (2%)
  waiting for transfers between devices  14.5 us (2%)
    pallas_call x1, Pallas kernels, gather_weights(): pl.pallas_call(functools.partial(gather_kernel, cw=cols // chunks, chunks...  115 us
    pallas_call x1, Pallas kernels, scatter_grads(): pl.pallas_call(functools.partial(scatter_kernel, given=given, ahead=len(a...  108 us
    pallas_call x4, Pallas kernels, att_bwd(): pl.pallas_call(functools.partial(att_bwd_kernel, bq=bq, causal=causal), g...  81.7 us
    pallas_call x4, Pallas kernels, att_fwd(): pl.pallas_call(functools.partial(att_fwd_kernel, bq=bq, causal=causal), g...  48 us
    dot_general x10, matrix products, nn(): return lax.dot_general(a, b, NN, preferred_element_type=f32)  47.7 us
    pallas_call x1, Pallas kernels, hidden_units(): pl.pallas_call(up_kernel, grid=(2 * per,), in_specs=[pl.BlockSpec((rows,...  27.7 us
    pallas_call x1, Pallas kernels, weight_grads(): pl.pallas_call(functools.partial(weight_grads_kernel, tiles=tiles), grid=...  26.4 us
    dot_general x6, matrix products, nt(): return lax.dot_general(a, b, NT, preferred_element_type=f32)  19.9 us
  transfers between devices with their start and end apart: 6, of which 2 were waited for; matrix products, arithmetic and copies ran while one was open for 19% of the time, Pallas kernels for 46%

profile of v4, /device:TPU:0, one launch (start us, length us, event | category | flops | bytes accessed | tf_op | source)
XLA Modules:
  0.0 655.9 jit_solution(15321562599827364791)
XLA Ops:
  9.2 1.7 pad_maximum_fusion.shard_ref
  10.9 115.2 %shard_map.228 = (bf16[2,4,2,2,64,4096]{5,4,3,2,1,0:T(8,128)(2,1)}, bf16[2,512,1024]{2,1,0:T(8,128)(2,1)}, bf16[2,512,1024]{2,1,0:T(8,128)(2,1)}) custom-call(bf16[64,4096]{1,0:T(8,128)(2,1)} %pad_maximum_fusion.shard_ref, bf16[2,512,1024]{2,1,0:T(8,128)(2,1)} %refs_0_.1, bf16[2,512,1024]{2,1,0:T(8,128)(2,1)} %refs_1_.1), custom_call_target="tpu_custom_call" | custom-call | bytes 167772160 | tf_op jit(solution)/shard_map/pallas_call | solution.py:628
  128.5 2.3 collective-permute-done
  131.0 7.8 %multiply_convert_fusion.1.q_ref.k_ref.v_ref = bf16[1024,1536]{1,0:T(8,128)(2,1)} fusion(bf16[1024,1024]{1,0:T(8,128)(2,1)} %bitcast.201, f32[1536]{0:T(1024)S(1)} %copy-done.51, f32[1536]{0:T(1024)S(1)} %get-tuple-element.176, bf16[2,1024,4096]{2,1,0:T(8,128)(2,1)} %bitcast.170), kind=kOutput, calls=%fused_computation.1 | convolution fusion | flops 3225944064 | bytes 8400896 | tf_op jit(solution)/shard_map/dot_general | solution.py:1079
  138.8 10.0 %shard_map.229 = (bf16[1024,512]{1,0:T(8,128)(2,1)}, f32[4,2,1024]{2,1,0:T(2,128)}) custom-call(bf16[1024,1536]{1,0:T(8,128)(2,1)} %multiply_convert_fusion.1.q_ref.k_ref.v_ref, bf16[1024,1536]{1,0:T(8,128)(2,1)} %multiply_convert_fusion.1.q_ref.k_ref.v_ref, bf16[1024,1536]{1,0:T(8,128)(2,1)} %multiply_convert_fusion.1.q_ref.k_ref.v_ref), custom_call_target="tpu_custom_call" | custom-call | tf_op jit(solution)/shard_map/pallas_call | solution.py:448
  148.8 6.7 %multiply_convert_fusion.q_ref.k_ref.v_ref = bf16[1024,1536]{1,0:T(8,128)(2,1)} fusion(bf16[1024,1024]{1,0:T(8,128)(2,1)S(1)} %bitcast.203, f32[1536]{0:T(1024)S(1)} %get-tuple-element.175, bf16[2,1024,4096]{2,1,0:T(8,128)(2,1)} %bitcast.171, f32[1536]{0:T(1024)S(1)} %copy-done.51), kind=kOutput, calls=%fused_computation | convolution fusion | flops 3225944064 | bytes 8400896 | tf_op jit(solution)/shard_map/dot_general | solution.py:1079
  155.5 9.4 %shard_map.230 = (bf16[1024,512]{1,0:T(8,128)(2,1)}, f32[4,2,1024]{2,1,0:T(2,128)}) custom-call(bf16[1024,1536]{1,0:T(8,128)(2,1)} %multiply_convert_fusion.q_ref.k_ref.v_ref, bf16[1024,1536]{1,0:T(8,128)(2,1)} %multiply_convert_fusion.q_ref.k_ref.v_ref, bf16[1024,1536]{1,0:T(8,128)(2,1)} %multiply_convert_fusion.q_ref.k_ref.v_ref), custom_call_target="tpu_custom_call" | custom-call | tf_op jit(solution)/shard_map/pallas_call | solution.py:448
  165.6 2.6 fusion.28
  168.2 2.9 fusion.53
  172.5 4.4 multiply_convert_fusion.2.q_ref
  176.9 5.3 add_convert_fusion.k_ref.v_ref
  182.1 14.4 %shard_map.232 = (bf16[1024,512]{1,0:T(8,128)(2,1)}, f32[4,2,1024]{2,1,0:T(2,128)}) custom-call(bf16[1024,512]{1,0:T(8,128)(2,1)} %multiply_convert_fusion.2.q_ref, bf16[1024,1024]{1,0:T(8,128)(2,1)} %add_convert_fusion.k_ref.v_ref, bf16[1024,1024]{1,0:T(8,128)(2,1)} %add_convert_fusion.k_ref.v_ref), custom_call_target="tpu_custom_call" | custom-call | tf_op jit(solution)/shard_map/pallas_call | solution.py:448
  196.5 3.6 multiply_convert_fusion.3.q_ref
  200.2 5.3 add_convert_fusion.1.k_ref.v_ref
  205.4 14.2 %shard_map.231 = (bf16[1024,512]{1,0:T(8,128)(2,1)}, f32[4,2,1024]{2,1,0:T(2,128)}) custom-call(bf16[1024,512]{1,0:T(8,128)(2,1)} %multiply_convert_fusion.3.q_ref, bf16[1024,1024]{1,0:T(8,128)(2,1)} %add_convert_fusion.1.k_ref.v_ref, bf16[1024,1024]{1,0:T(8,128)(2,1)} %add_convert_fusion.1.k_ref.v_ref), custom_call_target="tpu_custom_call" | custom-call | tf_op jit(solution)/shard_map/pallas_call | solution.py:448
  219.6 3.0 fusion.20
  222.7 4.7 fusion.54
  227.4 12.2 %all-gather.2.cloned.1.call-done = bf16[2048,4096]{1,0:T(8,128)(2,1)} async-done(((bf16[64,4096]{1,0:T(8,128)(2,1)}), bf16[2048,4096]{1,0:T(8,128)(2,1)}) %all-gather.2.cloned.1.call-update) | async-done | bytes 16777232 | tf_op jit(solution)/shard_map/all_gather | solution.py:1154
  242.3 4.8 fusion.45
  247.2 27.7 %shard_map.233 = (bf16[1024,4096]{1,0:T(8,128)(2,1)}, bf16[1024,4096]{1,0:T(8,128)(2,1)}) custom-call(bf16[1024,1024]{1,0:T(8,128)(2,1)} %get-tuple-element.133.x_ref.a_ref, bf16[2,1024,4096]{2,1,0:T(8,128)(2,1)} %bitcast.196, f32[1,4096]{1,0:T(1,128)} %bitcast.227), custom_call_target="tpu_custom_call" | custom-call | tf_op jit(solution)/shard_map/pallas_call | solution.py:884
  274.9 2.3 maximum_select_fusion.cot_ref
  277.2 19.2 %shard_map.234 = (bf16[1024,1024]{1,0:T(8,128)(2,1)}, f32[1024,1024]{1,0:T(8,128)}, bf16[1024,1024]{1,0:T(8,128)(2,1)}, f32[8,1024]{1,0:T(8,128)}) custom-call(bf16[1024,4096]{1,0:T(8,128)(2,1)} %get-tuple-element.68.act_ref.db_ref, bf16[2,1024,4096]{2,1,0:T(8,128)(2,1)} %bitcast.197, f32[1024,1024]{1,0:T(8,128)} %get-tuple-element.134.h_ref, ...), custom_call_target="tpu_custom_call" | custom-call | tf_op jit(solution)/shard_map/pallas_call | solution.py:960
  296.4 15.0 %shard_map.235 = (bf16[1024,4096]{1,0:T(8,128)(2,1)}, f32[1,4096]{1,0:T(1,128)}) custom-call(bf16[1024,1024]{1,0:T(8,128)(2,1)} %get-tuple-element.71.e_ref.b_ref, bf16[2,1024,4096]{2,1,0:T(8,128)(2,1)} %bitcast.198, bf16[1024,4096]{1,0:T(8,128)(2,1)} %get-tuple-element.72.slope_ref), custom_call_target="tpu_custom_call" | custom-call | tf_op jit(solution)/shard_map/pallas_call | solution.py:914
  311.4 26.4 %shard_map.236 = bf16[2,1024,4096]{2,1,0:T(8,128)(2,1)} custom-call(bf16[1024,1024]{1,0:T(8,128)(2,1)} %get-tuple-element.133.x_ref.a_ref, bf16[1024,1024]{1,0:T(8,128)(2,1)} %get-tuple-element.71.e_ref.b_ref, bf16[1024,4096]{1,0:T(8,128)(2,1)} %get-tuple-element.74.da_ref.du_ref, bf16[1024,4096]{1,0:T(8,128)(2,1)} %get-tuple-element.68.act_ref.db_ref), custom_call_target="tpu_custom_call" | custom-call | tf_op jit(solution)/shard_map/pallas_call | solution.py:1065
  338.9 17.9 %shard_map.237 = (f32[1024,1024]{1,0:T(8,128)}, bf16[1024,1024]{1,0:T(8,128)(2,1)}, f32[8,1024]{1,0:T(8,128)}) custom-call(bf16[1024,4096]{1,0:T(8,128)(2,1)} %get-tuple-element.74.da_ref.du_ref, bf16[2,1024,4096]{2,1,0:T(8,128)(2,1)} %bitcast.199, f32[1024,1024]{1,0:T(8,128)} %get-tuple-element.75.dr3_ref, f32[1024,1024]{1,0:T(8,128)} %get-tuple-element.135.n_ref, ...), custom_call_target="tpu_custom_call" | custom-call | tf_op jit(solution)/shard_map/pallas_call | solution.py:995
  356.8 4.1 convolution_convert_fusion.11.do_ref
  360.9 23.8 %shard_map.238 = (bf16[1024,512]{1,0:T(8,128)(2,1)}, bf16[1024,512]{1,0:T(8,128)(2,1)}, bf16[1024,512]{1,0:T(8,128)(2,1)}) custom-call(bf16[1024,512]{1,0:T(8,128)(2,1)} %multiply_convert_fusion.3.q_ref, bf16[1024,1024]{1,0:T(8,128)(2,1)} %add_convert_fusion.1.k_ref.v_ref, bf16[1024,1024]{1,0:T(8,128)(2,1)} %add_convert_fusion.1.k_ref.v_ref, ...), custom_call_target="tpu_custom_call" | custom-call | tf_op jit(solution)/shard_map/pallas_call | solution.py:498
  384.7 3.5 convolution_convert_fusion.9.do_ref
  388.2 23.8 %shard_map.239 = (bf16[1024,512]{1,0:T(8,128)(2,1)}, bf16[1024,512]{1,0:T(8,128)(2,1)}, bf16[1024,512]{1,0:T(8,128)(2,1)}) custom-call(bf16[1024,512]{1,0:T(8,128)(2,1)} %multiply_convert_fusion.2.q_ref, bf16[1024,1024]{1,0:T(8,128)(2,1)} %add_convert_fusion.k_ref.v_ref, bf16[1024,1024]{1,0:T(8,128)(2,1)} %add_convert_fusion.k_ref.v_ref, ...), custom_call_target="tpu_custom_call" | custom-call | tf_op jit(solution)/shard_map/pallas_call | solution.py:498
  412.1 2.7 fusion.22
  415.0 3.9 multiply_reduce_fusion
  418.9 1.4 fusion.44
  420.7 2.0 copy-done.30
  422.7 1.5 constant_dynamic-slice_fusion.4
  426.1 7.4 %shard_map.240.refs_1_ = bf16[1024,1024]{1,0:T(8,128)(2,1)S(1)} custom-call(bf16[1024,512]{1,0:T(8,128)(2,1)S(1)} %copy-done.11, bf16[1024,512]{1,0:T(8,128)(2,1)S(1)} %copy-done.13, bf16[1024,512]{1,0:T(8,128)(2,1)S(1)} %copy-done.6, bf16[1024,512]{1,0:T(8,128)(2,1)S(1)} %copy-done.7, bf16[2,1024,4096]{2,1,0:T(8,128)(2,1)} %bitcast.184, ...), custom_call_target="tpu_custom_call" | custom-call | tf_op jit(solution)/shard_map/pallas_call | solution.py:1035
  433.6 1.6 constant_dynamic-slice_fusion.2
  436.2 3.5 convolution_convert_fusion.do_ref
  439.7 17.1 %shard_map.242 = (bf16[1024,512]{1,0:T(8,128)(2,1)}, bf16[1024,512]{1,0:T(8,128)(2,1)}, bf16[1024,512]{1,0:T(8,128)(2,1)}) custom-call(bf16[1024,1536]{1,0:T(8,128)(2,1)} %multiply_convert_fusion.q_ref.k_ref.v_ref, bf16[1024,1536]{1,0:T(8,128)(2,1)} %multiply_convert_fusion.q_ref.k_ref.v_ref, bf16[1024,1536]{1,0:T(8,128)(2,1)} %multiply_convert_fusion.q_ref.k_ref.v_ref, ...), custom_call_target="tpu_custom_call" | custom-call | tf_op jit(solution)/shard_map/pallas_call | solution.py:498
  456.8 1.4 convert_reduce_fusion.6
  458.3 1.5 convert_reduce_fusion.4
  461.5 3.7 convolution_convert_fusion.1.do_ref
  465.2 2.3 convolution_convert_fusion.2
  467.5 2.3 convolution_convert_fusion.3
  469.8 2.3 convolution_convert_fusion.4
  472.1 2.3 convolution_convert_fusion.5
  474.4 2.3 convolution_convert_fusion.6
  476.6 2.3 convolution_convert_fusion.7
  479.0 2.3 convolution_convert_fusion.8
  481.2 2.3 convolution_convert_fusion.10
  483.5 3.4 maximum_select_fusion.1.refs_0_
  486.9 16.9 %shard_map.241 = (bf16[1024,512]{1,0:T(8,128)(2,1)}, bf16[1024,512]{1,0:T(8,128)(2,1)}, bf16[1024,512]{1,0:T(8,128)(2,1)}) custom-call(bf16[1024,1536]{1,0:T(8,128)(2,1)} %multiply_convert_fusion.1.q_ref.k_ref.v_ref, bf16[1024,1536]{1,0:T(8,128)(2,1)} %multiply_convert_fusion.1.q_ref.k_ref.v_ref, ...), custom_call_target="tpu_custom_call" | custom-call | tf_op jit(solution)/shard_map/pallas_call | solution.py:498
  503.7 1.4 convert_reduce_fusion.7
  505.2 1.5 convert_reduce_fusion.5
  506.8 1.2 copy-done.3
  508.0 1.2 copy-done.4
  509.2 1.2 copy-done.9
  510.5 1.2 copy-done.10
  511.7 10.5 %shard_map.243 = bf16[1024,1024]{1,0:T(8,128)(2,1)S(1)} custom-call(bf16[1024,512]{1,0:T(8,128)(2,1)S(1)} %copy-done.3, bf16[1024,512]{1,0:T(8,128)(2,1)S(1)} %copy-done.1, bf16[1024,512]{1,0:T(8,128)(2,1)S(1)} %copy-done.10, bf16[1024,512]{1,0:T(8,128)(2,1)S(1)} %copy-done.9, bf16[1024,512]{1,0:T(8,128)(2,1)S(1)} %copy-done.4, ...), custom_call_target="tpu_custom_call" | custom-call | tf_op jit(solution)/shard_map/pallas_call | solution.py:1035
  522.3 1.3 copy-done.5
  523.7 3.3 maximum_select_fusion.2.refs_18_
  527.0 107.6 %shard_map.244 = (f32[64,4096]{1,0:T(8,128)}, f32[136,128]{1,0:T(8,128)}, bf16[2,512,1024]{2,1,0:T(8,128)(2,1)}) custom-call(bf16[4,2,2,64,512]{4,3,2,1,0:T(8,128)(2,1)} %bitcast.215, bf16[4,2,2,64,512]{4,3,2,1,0:T(8,128)(2,1)} %bitcast.214, bf16[4,2,2,64,512]{4,3,2,1,0:T(8,128)(2,1)} %bitcast.213, bf16[4,2,2,64,512]{4,3,2,1,0:T(8,128)(2,1)} %bitcast.212, ...), custom_call_target="tpu_custom_call" | custom-call | bytes 167772160 | tf_op jit(solution)/shard_map/pallas_call | solution.py:800
  642.1 1.7 slice_bitcast_fusion.1
  645.7 1.8 slice.243
  647.5 1.3 copy.70
  (185 shorter events, 25.1 us)
Async XLA Ops:
  7.2 118.9 %copy-start.39 = (bf16[64,2048]{1,0:T(8,128)(2,1)S(1)}, bf16[64,2048]{1,0:T(8,128)(2,1)}, u32[]{:S(2)}) copy-start(bf16[64,2048]{1,0:T(8,128)(2,1)} %param.20) | copy-start | bytes 786436
  7.2 118.9 %copy-start.38 = (bf16[2048,64]{0,1:T(8,128)(2,1)S(1)}, bf16[2048,64]{0,1:T(8,128)(2,1)}, u32[]{:S(2)}) copy-start(bf16[2048,64]{0,1:T(8,128)(2,1)} %param.21) | copy-start | bytes 786436
  7.2 119.8 %copy-start.44 = (bf16[4,512]{1,0:T(4,128)(2,1)S(1)}, bf16[4,512]{1,0:T(4,128)(2,1)}, u32[]{:S(2)}) copy-start(bf16[4,512]{1,0:T(4,128)(2,1)} %param.22) | copy-start | bytes 12292
  7.2 119.9 %copy-start.45 = (bf16[2048]{0:T(1024)(128)(2,1)S(1)}, bf16[2048]{0:T(1024)(128)(2,1)}, u32[]{:S(2)}) copy-start(bf16[2048]{0:T(1024)(128)(2,1)} %param.23) | copy-start | bytes 12292
  7.2 120.5 %copy-start.42 = (bf16[3,1024]{1,0:T(4,128)(2,1)S(1)}, bf16[3,1024]{1,0:T(4,128)(2,1)}, u32[]{:S(2)}) copy-start(bf16[3,1024]{1,0:T(4,128)(2,1)} %param.24) | copy-start | bytes 18436
  7.2 120.5 %copy-start.41 = (bf16[6,1024]{1,0:T(8,128)(2,1)S(1)}, bf16[6,1024]{1,0:T(8,128)(2,1)}, u32[]{:S(2)}) copy-start(bf16[6,1024]{1,0:T(8,128)(2,1)} %param.25) | copy-start | bytes 36868
  7.2 232.3 %all-gather.2.cloned.1.call-start = ((), (), s32[]{:S(2)}) async-start(), calls=%async_computation.1 | async-start | bytes 17301504 | tf_op jit(solution)/shard_map/all_gather | solution.py:1154
  8.3 122.7 %copy-start.51 = (f32[1536]{0:T(1024)S(1)}, f32[1536]{0:T(1024)}, u32[]{:S(2)}) copy-start(f32[1536]{0:T(1024)} %constant.48.clone.1) | copy-start | bytes 18436
  127.0 516.8 %reduce-scatter.2.cloned.1.call-start = ((), (), s32[]{:S(2)}) async-start(), calls=%async_computation.2 | async-start | bytes 17301504 | tf_op jit(solution)/shard_map/reduce_scatter | solution.py:1229
  127.1 3.7 collective-permute-start
  138.8 10.0 %copy-start.20 = (bf16[2,512,1024]{2,1,0:T(8,128)(2,1)S(1)}, bf16[2,512,1024]{2,1,0:T(8,128)(2,1)}, u32[]{:S(2)}) copy-start(bf16[2,512,1024]{2,1,0:T(8,128)(2,1)} %get-tuple-element.57) | copy-start | bytes 6291460
  155.5 10.1 %copy-start.26 = (bf16[1024,512]{1,0:T(8,128)(2,1)S(1)}, bf16[1024,512]{1,0:T(8,128)(2,1)}, u32[]{:S(2)}) copy-start(bf16[1024,512]{1,0:T(8,128)(2,1)} %get-tuple-element.60.o_ref.refs_16_) | copy-start | bytes 3145732
  165.6 2.6 copy-start.18
  171.2 51.5 %copy-start.15 = (f32[1024,1024]{1,0:T(8,128)}, f32[1024,1024]{1,0:T(8,128)S(1)}, u32[]{:S(2)}) copy-start(f32[1024,1024]{1,0:T(8,128)S(1)} %get-tuple-element.178) | copy-start | bytes 12582916
  172.5 24.0 %copy-start.27 = (bf16[1024,1024]{1,0:T(8,128)(2,1)}, bf16[1024,1024]{1,0:T(8,128)(2,1)S(1)}, u32[]{:S(2)}) copy-start(bf16[1024,1024]{1,0:T(8,128)(2,1)S(1)} %fusion) | copy-start | bytes 6291460
  172.5 4.4 copy-start.46
  196.5 3.6 copy-start.47
  219.6 3.1 copy-start.32
  222.7 16.9 %copy-start.29 = (bf16[2,512,1024]{2,1,0:T(8,128)(2,1)S(1)}, bf16[2,512,1024]{2,1,0:T(8,128)(2,1)}, u32[]{:S(2)}) copy-start(bf16[2,512,1024]{2,1,0:T(8,128)(2,1)} %param.15) | copy-start | bytes 6291460
  239.6 2.2 copy-start.17
  239.8 35.1 %collective-permute-start.1 = (bf16[512,1024]{1,0:T(8,128)(2,1)S(1)}, bf16[512,1024]{1,0:T(8,128)(2,1)S(1)}, u32[]{:S(2)}, u32[]{:S(2)}) collective-permute-start(bf16[512,1024]{1,0:T(8,128)(2,1)S(1)} %get-tuple-element.141), channel_id=1, source_target_pairs={{0,1},{1,0},{2,3},{3,2},{4,5},{5,4},{6,7},{7,6},{8,9},{9,8},{10,11... | collective-permute-start | bytes 3145736 | tf_op jit(solution)/shard_map/ppermute | solution.py:1104
  360.9 23.8 %copy-start.49 = (bf16[1024,1024]{1,0:T(8,128)(2,1)S(1)}, bf16[1024,1024]{1,0:T(8,128)(2,1)}, u32[]{:S(2)}) copy-start(bf16[1024,1024]{1,0:T(8,128)(2,1)} %get-tuple-element.76) | copy-start | bytes 6291460
  388.2 23.9 %copy-start.35 = (bf16[1024,512]{1,0:T(8,128)(2,1)S(1)}, bf16[1024,512]{1,0:T(8,128)(2,1)}, u32[]{:S(2)}) copy-start(bf16[1024,512]{1,0:T(8,128)(2,1)} %get-tuple-element.78) | copy-start | bytes 3145732
  388.2 26.6 %copy-start.25 = (f32[1024,1024]{1,0:T(8,128)S(1)}, f32[1024,1024]{1,0:T(8,128)}, u32[]{:S(2)}) copy-start(f32[1024,1024]{1,0:T(8,128)} %get-tuple-element.85) | copy-start | bytes 12582916
  412.1 2.7 copy-start.16
  412.1 2.9 copy-start.23
  420.3 2.4 copy-start.30
  420.7 40.8 %copy-start.19 = (bf16[1024,1024]{1,0:T(8,128)(2,1)}, bf16[1024,1024]{1,0:T(8,128)(2,1)S(1)}, u32[]{:S(2)}) copy-start(bf16[1024,1024]{1,0:T(8,128)(2,1)S(1)} %convert_element_type.129.refs_9_) | copy-start | bytes 6291460
  420.7 4.8 copy-start.36
  420.7 5.0 copy-start.7
  420.7 5.2 copy-start.6
  422.7 3.4 copy-start.11
  422.7 3.5 copy-start.13
  424.2 59.4 %collective-permute-start.2 = (bf16[1,512,1024]{2,1,0:T(8,128)(2,1)}, bf16[1,512,1024]{2,1,0:T(8,128)(2,1)}, u32[]{:S(2)}, u32[]{:S(2)}) collective-permute-start(bf16[1,512,1024]{2,1,0:T(8,128)(2,1)} %get-tuple-element.139), channel_id=1, source_target_pairs={{0,1},{1,0},{2,3},{3,2},{4,5},{5,4},{6,7},{7,6},{8,9},{9,8},{10,11... | collective-permute-start | bytes 3145736 | tf_op jit(solution)/shard_map/ppermute | solution.py:1104
  433.6 6.1 copy-start
  435.2 88.5 %collective-permute-start.3 = (bf16[1,512,1024]{2,1,0:T(8,128)(2,1)}, bf16[1,512,1024]{2,1,0:T(8,128)(2,1)}, u32[]{:S(2)}, u32[]{:S(2)}) collective-permute-start(bf16[1,512,1024]{2,1,0:T(8,128)(2,1)} %get-tuple-element.137), channel_id=1, source_target_pairs={{0,1},{1,0},{2,3},{3,2},{4,5},{5,4},{6,7},{7,6},{8,9},{9,8},{10,11... | collective-permute-start | bytes 3145736 | tf_op jit(solution)/shard_map/ppermute | solution.py:1104
  461.5 3.7 copy-start.33
  461.5 3.7 copy-start.50
  465.2 2.3 copy-start.34
  467.5 2.3 copy-start.8
  467.5 2.3 copy-start.48
  472.1 2.3 copy-start.14
  474.4 2.3 copy-start.12
  476.6 2.3 copy-start.24
  476.6 2.3 copy-start.28
  478.9 2.3 copy-start.37
  481.2 2.3 copy-start.22
  486.9 19.9 %copy-start.43 = (f32[1,4096]{1,0:T(1,128)S(1)}, f32[1,4096]{1,0:T(1,128)}, u32[]{:S(2)}) copy-start(f32[1,4096]{1,0:T(1,128)} %get-tuple-element.94) | copy-start | bytes 49156
  486.9 19.9 %copy-start.1 = (bf16[1024,512]{1,0:T(8,128)(2,1)S(1)}, bf16[1024,512]{1,0:T(8,128)(2,1)}, u32[]{:S(2)}) copy-start(bf16[1024,512]{1,0:T(8,128)(2,1)} %get-tuple-element.89.refs_1_.refs_11_) | copy-start | bytes 3145732
  486.9 19.9 %copy-start.2 = (bf16[1024,512]{1,0:T(8,128)(2,1)S(1)}, bf16[1024,512]{1,0:T(8,128)(2,1)}, u32[]{:S(2)}) copy-start(bf16[1024,512]{1,0:T(8,128)(2,1)} %get-tuple-element.93.refs_5_.refs_15_) | copy-start | bytes 3145732
  506.8 1.2 copy-start.3
  508.0 1.2 copy-start.4
  509.2 1.2 copy-start.9
  510.5 1.2 copy-start.10
  511.7 12.0 %copy-start.21 = (bf16[1,512,1024]{2,1,0:T(8,128)(2,1)S(1)}, bf16[1,512,1024]{2,1,0:T(8,128)(2,1)}, u32[]{:S(2)}) copy-start(bf16[1,512,1024]{2,1,0:T(8,128)(2,1)} %get-tuple-element.136) | copy-start | bytes 3145732
  522.2 1.4 copy-start.5
  523.7 3.3 copy-start.40
  634.6 12.9 %copy-start.31 = (bf16[2,512,1024]{2,1,0:T(8,128)(2,1)S(1)}, bf16[2,512,1024]{2,1,0:T(8,128)(2,1)}, u32[]{:S(2)}) copy-start(bf16[2,512,1024]{2,1,0:T(8,128)(2,1)} %get-tuple-element.199) | copy-start | bytes 6291460
Sparse Core Ops, SparseCore 0:
  127.1 112.4 all-gather.1
  338.0 181.7 reduce-scatter.1

commit v5 on v4

--- a/solution.py
+++ b/solution.py
@@ -455,7 +455,8 @@
     )(q,k,v)
 
 def att_bwd_kernel(q_ref,k_ref,v_ref,o_ref,do_ref,lse_ref,*refs,bq,causal):
-    dq_ref,dk_ref,dv_ref,dk_acc,dv_acc=refs[-5:]
+    dq_ref,dk_ref,dv_ref,sum_q_ref,sum_v_ref,dk_acc,dv_acc=refs[-7:]
+    sum_q=0.0
     n=q_ref.shape[0]; nk=k_ref.shape[0]
     lane=lax.broadcasted_iota(jnp.int32,(nk,128),1)
     lq=lax.broadcasted_iota(jnp.int32,(bq,128),1)
@@ -488,9 +489,14 @@
             dv_acc[:L,:]+=lax.dot_general(pb,dm[h],NN,preferred_element_type=f32)
             dk_acc[:L,:]+=lax.dot_general(ds,qm[h],NN,preferred_element_type=f32)
             dqs.append(lax.dot_general(kt[h*HD:(h+1)*HD,:L],ds,NN,preferred_element_type=f32))
-        dq_ref[rows,:]=(jnp.concatenate(dqs,0)*0.125).T.astype(bf16)
+        dq=(jnp.concatenate(dqs,0)*0.125).T.astype(bf16)
+        dq_ref[rows,:]=dq
+        sum_q=sum_q+jnp.sum(dq.astype(f32),0,keepdims=True)
     dk_ref[...]=(dk_acc[...]*LN2).astype(bf16)
-    dv_ref[...]=dv_acc[...].astype(bf16)
+    dv=dv_acc[...].astype(bf16)
+    dv_ref[...]=dv
+    sum_q_ref[...]=sum_q
+    sum_v_ref[...]=jnp.sum(dv.astype(f32),0,keepdims=True)
 
 def att_bwd(q,k,v,o,do,lse,causal,bq=256,qo=0,ko=0,vo=0,ahead=()):
     n=q.shape[0]; nk=k.shape[0]; width=o.shape[1]; np_=width//128
@@ -499,8 +505,8 @@
         functools.partial(att_bwd_kernel,bq=bq,causal=causal),
         grid=(np_,),
         in_specs=[spec(n,qo),spec(nk,ko),spec(nk,vo),spec(n,0),spec(n,0),pl.BlockSpec((1,2,n),lambda p:(p,0,0))]+[pl.BlockSpec(memory_space=pl.ANY)]*len(ahead),
-        out_specs=[spec(n,0),spec(nk,0),spec(nk,0)],
-        out_shape=[jax.ShapeDtypeStruct((n,width),bf16),jax.ShapeDtypeStruct((nk,width),bf16),jax.ShapeDtypeStruct((nk,width),bf16)],
+        out_specs=[spec(n,0),spec(nk,0),spec(nk,0),spec(1,0),spec(1,0)],
+        out_shape=[jax.ShapeDtypeStruct((n,width),bf16),jax.ShapeDtypeStruct((nk,width),bf16),jax.ShapeDtypeStruct((nk,width),bf16),jax.ShapeDtypeStruct((1,width),f32),jax.ShapeDtypeStruct((1,width),f32)],
         scratch_shapes=[pltpu.VMEM((nk,128),f32)]*2,
         compiler_params=pltpu.CompilerParams(dimension_semantics=("arbitrary",),vmem_limit_bytes=56*2**20),
     )(q,k,v,o,do,lse,*ahead)
@@ -565,13 +571,22 @@
     return copy
 
 
-def gather_kernel(shard_ref, *refs, cw, chunks, swaps):
+def gather_kernel(*refs, cw, chunks, swaps, shards):
+    parts = []
+    for ref in refs[:shards]:
+        parts += [ref.at[i] for i in range(ref.shape[0])] if len(ref.shape) == 3 else [ref]
+    refs = refs[shards:]
+    pw = parts[0].shape[1]
     ins, outs = refs[:swaps], refs[swaps + 1 : 2 * swaps + 1]
     w_ref = refs[swaps]
     send, recv, own, swap_send, swap_recv, swap_own = refs[2 * swaps + 1 :]
     (t, z, y, c), ids = partners()
-    mine = pltpu.make_async_copy(shard_ref, w_ref.at[t, z, y, c], own)
-    mine.start()
+    mine = [
+        pltpu.make_async_copy(part, w_ref.at[t, z, y, c, :, pl.ds(i * pw, pw)], own.at[i])
+        for i, part in enumerate(parts)
+    ]
+    for copy in mine:
+        copy.start()
     kept = [
         pltpu.make_async_copy(ins[i].at[t], outs[i].at[t], swap_own.at[i]) for i in range(swaps)
     ]
@@ -585,7 +600,8 @@
         cols = pl.ds(k * cw, cw)
         if s == 0:
             r, to = w_ref.at[t, z, y, c, :, cols], "z1"
-            copies = [start_copy(shard_ref.at[:, cols], r, send.at[k, 0], recv.at[k, 0], ids[to])]
+            src = parts[k * cw // pw].at[:, pl.ds(k * cw % pw, cw)]
+            copies = [start_copy(src, r, send.at[k, 0], recv.at[k, 0], ids[to])]
             for i in range(swaps):
                 part = ins[i].shape[1] // chunks
                 rows = pl.ds(k * part, part)
@@ -603,7 +619,8 @@
             return []
         if s == 1:
             if k == 0:
-                mine.wait()
+                for copy in mine:
+                    copy.wait()
             r, to = w_ref.at[t, pl.ds(pair, 2), y, c, :, cols], "z2"
         elif s == 2:
             r, to = w_ref.at[t, :, y, c, :, cols], "x"
@@ -620,21 +637,23 @@
         copy.wait()
 
 
-def gather_weights(shard, pieces, cid, chunks):
-    rows, cols = shard.shape
+def gather_weights(shards, pieces, cid, chunks):
+    rows, wide = shards[0].shape[-2:]
+    count = sum(s.shape[0] if s.ndim == 3 else 1 for s in shards)
+    cols = count * wide
     swaps = len(pieces)
     anywhere = pl.BlockSpec(memory_space=pl.ANY)
     dma = pltpu.SemaphoreType.DMA
     outs = pl.pallas_call(
-        functools.partial(gather_kernel, cw=cols // chunks, chunks=chunks, swaps=swaps),
-        in_specs=[pl.BlockSpec(memory_space=pltpu.VMEM)] + [anywhere] * swaps,
+        functools.partial(gather_kernel, cw=cols // chunks, chunks=chunks, swaps=swaps, shards=len(shards)),
+        in_specs=[pl.BlockSpec(memory_space=pltpu.VMEM)] * len(shards) + [anywhere] * swaps,
         out_specs=[anywhere] * (1 + swaps),
-        out_shape=[jax.ShapeDtypeStruct((2, 4, 2, 2, rows, cols), shard.dtype)]
+        out_shape=[jax.ShapeDtypeStruct((2, 4, 2, 2, rows, cols), shards[0].dtype)]
         + [jax.ShapeDtypeStruct(p.shape, p.dtype) for p in pieces],
         scratch_shapes=[
             dma((chunks, 5)),
             dma((chunks, 5)),
-            dma,
+            dma((count,)),
             dma((swaps, chunks)),
             dma((swaps, chunks)),
             dma((swaps,)),
@@ -643,7 +662,7 @@
         cost_estimate=pl.CostEstimate(
             flops=0, bytes_accessed=32 * rows * cols * 20, transcendentals=0
         ),
-    )(shard, *pieces)
+    )(*shards, *pieces)
     whole = outs[0].reshape(2, 16 * rows, cols)
     return whole, [p.reshape(p.shape[0] * p.shape[1], p.shape[2]) for p in outs[1:]]
 
@@ -1042,6 +1061,60 @@
     )(*lefts, *([w] * len(lefts)), *based)
 
 
+def unpack_kernel(att_ref, ffn_ref, flat_ref, *outs):
+    self_in, self_out, cross_in, cross_out, up, down, head, unit, gain, row = outs
+    cols, units = head.shape[1], up.shape[1]
+    place = lax.axis_index("tp")
+    for j in range(3):
+        cross_in[j] = att_ref[:, j * cols : (j + 1) * cols]
+        self_in[j] = att_ref[:, (4 + j) * cols : (5 + j) * cols]
+    cross_out[...] = att_ref[:, 3 * cols : 4 * cols]
+    self_out[...] = att_ref[:, 7 * cols : 8 * cols]
+    up[...] = ffn_ref[:, :units].astype(f32)
+    down[...] = ffn_ref[:, units:].astype(f32)
+    lines = cols // 128
+    for i in range(4):
+        for j in range(lines):
+            head[i : i + 1, 128 * j : 128 * (j + 1)] = flat_ref[
+                pl.ds((place * 4 + i) * lines + j, 1), :
+            ]
+    first, lines = 8 * lines, units // 128
+    for j in range(lines):
+        unit[:, 128 * j : 128 * (j + 1)] = flat_ref[pl.ds(first + place * lines + j, 1), :]
+    first, lines = first + 2 * lines, gain.shape[1] // 128
+    for ref in (gain, row):
+        for i in range(ref.shape[0]):
+            for j in range(lines):
+                ref[i : i + 1, 128 * j : 128 * (j + 1)] = flat_ref[first + j : first + j + 1, :]
+            first += lines
+
+
+def unpack(att, ffn, flat, cols, units):
+    rows, width = att.shape[0], 16 * att.shape[0]
+    shapes = [
+        (3, rows, cols),
+        (rows, cols),
+        (3, rows, cols),
+        (rows, cols),
+        (rows, units),
+        (rows, units),
+        (4, cols),
+        (1, units),
+        (3, width),
+        (6, width),
+    ]
+    whole = pl.BlockSpec(memory_space=pltpu.VMEM)
+    outs = pl.pallas_call(
+        unpack_kernel,
+        in_specs=[whole] * 3,
+        out_specs=[whole] * len(shapes),
+        out_shape=[jax.ShapeDtypeStruct(s, f32) for s in shapes],
+    )(att, ffn, flat)
+    self_in, self_out, cross_in, cross_out, up, down = outs[:6]
+    self_in, cross_in = self_in.transpose(1, 0, 2), cross_in.transpose(1, 0, 2)
+    return self_in, self_out.T, cross_in, cross_out.T, up, down.T, outs[6:]
+
+
 def weight_grads_kernel(a_ref,b_ref,da_ref,db_ref,out_ref,at,bt,*,tiles):
     j=pl.program_id(0)
     @pl.when(j==0)
@@ -1161,15 +1234,7 @@
 
     c3, c4 = 3 * cols, 4 * cols
     g_att, (x, mem) = gather_weights(
-        jnp.concatenate(
-            [
-                w_self_in.reshape(shard, c3),
-                w_self_out.T,
-                w_cross_in.reshape(shard, c3),
-                w_cross_out.T,
-            ],
-            1,
-        ),
+        (w_self_in.transpose(1, 0, 2), w_self_out.T, w_cross_in.transpose(1, 0, 2), w_cross_out.T),
         (layer_in, memory),
         1,
         16,
@@ -1228,7 +1293,7 @@
     grad_ffn, du = lax.optimization_barrier((grad_ffn, du))
     s_ffn = lax.psum_scatter(
         grad_ffn.reshape(2 * width, 2 * units), ("tp", "fsdp"), scatter_dimension=0, tiled=True
-    ).astype(f32)
+    )
     dr2, e2, sums2 = up_back_and_norm(
         du,
         g_ffn,
@@ -1240,13 +1305,15 @@
     )
     gg2, gs2, gb2 = sums2[0], sums2[1], sums2[2]
 
-    dcq, dck, dcv = [], [], []
+    dcq, dck, dcv, bcq, bcv = [], [], [], [], []
     for t in halves:
         da = nn(e2, g_cross[t, :, c3:]).astype(bf16)
-        a, b, c = att_bwd(cq[t], ckv[t], ckv[t], ca[t], da, cl[t], False, 256, 0, 0, blk)
+        a, b, c, sq, sv = att_bwd(cq[t], ckv[t], ckv[t], ca[t], da, cl[t], False, 256, 0, 0, blk)
         dcq.append(a)
         dck.append(b)
         dcv.append(c)
+        bcq.append(sq[0])
+        bcv.append(sv[0])
     low = lambda v: v.astype(bf16)
     grads = [
         tuple(low(tn(h1b, dcq[t])) for t in halves),
@@ -1262,23 +1329,22 @@
     dr1, gg1, gs1, gb1 = norm_rows_back(dh1, n1, i1, gains[0])
     e1 = dr1.astype(bf16)
 
-    dsq, dsk, dsv = [], [], []
+    dsq, dsk, dsv, bsq, bsv = [], [], [], [], []
     for t in halves:
         da = nn(e1, g_self[t, :, c3:]).astype(bf16)
         y = sy[t]
         ahead = (mixed, dmem) if t == 0 else ()
-        a, b, c = att_bwd(y, y, y, sa[t], da, sl[t], True, 256, 0, blk, 2 * blk, ahead)
+        a, b, c, sq, sv = att_bwd(y, y, y, sa[t], da, sl[t], True, 256, 0, blk, 2 * blk, ahead)
         dsq.append(a)
         dsk.append(b)
         dsv.append(c)
+        bsq.append(sq[0])
+        bsv.append(sv[0])
     dx = sum_of_products(
         dsq + dsk + dsv, g_att, [(t, j) for j in range(3) for t in halves], dr1, 256
     )
 
-    def col_sums(pair):
-        return jnp.stack([jnp.sum(p.astype(f32), 0) for p in pair])
-
-    gh = jnp.stack([col_sums(dsq), col_sums(dsv), col_sums(dcq), col_sums(dcv)], 1)
+    gh = jnp.stack([jnp.stack([bsq[t], bsv[t], bcq[t], bcv[t]]) for t in halves])
     flat = jnp.concatenate(
         [
             v.reshape(-1)
@@ -1289,28 +1355,24 @@
     s_att, flat, d_layer_in = scatter_grads(
         grads, (x, e1), made, (d_memory,), dx, flat.reshape(-1, 128), 2
     )
-    flat = flat.reshape(-1)
-    head_sum = lax.dynamic_index_in_dim(flat[: 8 * cols].reshape(2, 4, cols), place, 0, False)
-    unit_sum = lax.dynamic_index_in_dim(
-        flat[8 * cols : 8 * cols + 2 * units].reshape(2, units), place, 0, False
-    )
-    rest = flat[8 * cols + 2 * units :].reshape(9, width)
-
-    cross_part, self_part = s_att[:, : 4 * cols], s_att[:, 4 * cols :]
+    d_self_in, d_self_out, d_cross_in, d_cross_out, d_up, d_down, small = unpack(
+        s_att, s_ffn, flat, cols, units
+    )
+    d_head_bias, d_up_bias, d_norm_gain, d_row_bias = small
     return (
         mixed,
-        d_layer_in,
+        d_layer_in.reshape(layer_in.shape),
         d_memory,
-        self_part[:, :c3].reshape(shard, 3, cols),
-        self_part[:, c3:].T,
-        cross_part[:, :c3].reshape(shard, 3, cols),
-        cross_part[:, c3:].T,
-        s_ffn[:, :units],
-        s_ffn[:, units:].T,
-        head_sum,
-        unit_sum,
-        rest[:3],
-        rest[3:],
+        d_self_in,
+        d_self_out,
+        d_cross_in,
+        d_cross_out,
+        d_up,
+        d_down,
+        d_head_bias,
+        d_up_bias.reshape(units),
+        d_norm_gain,
+        d_row_bias,
     )
 
 

time: 661 us -> 644 us (0.974)
  local copies, waits for them, and re-layouts: 31.5 us -> 19.2 us
  other arithmetic: 28.4 us -> 20.2 us
    reduce_sum x8 -> x0, other arithmetic: 6.61 us -> none  [col_sums(): return jnp.stack([jnp.sum(p.astype(f32), 0) for p in pair])]
  transfers between devices with their start and end apart: 6 -> 6, of which waited for: 2 -> 2; matrix products, arithmetic and copies ran while one was open for 19% -> 17% of each run, Pallas kernels for 46% -> 47%
where the time goes in v5:
time: 644 us; the launch traced here: 639 us
  Pallas kernels  480 us (75%)
  matrix products  86.5 us (13%)
  other arithmetic  20.2 us (3%)
  local copies, waits for them, and re-layouts  19.2 us (3%)
  between operations  15.3 us (2%)
  waiting for transfers between devices  14.5 us (2%)
    pallas_call x1, Pallas kernels, gather_weights(): pl.pallas_call(functools.partial(gather_kernel, cw=cols // chunks, chunks...  115 us
    pallas_call x1, Pallas kernels, scatter_grads(): pl.pallas_call(functools.partial(scatter_kernel, given=given, ahead=len(a...  107 us
    pallas_call x4, Pallas kernels, att_bwd(): pl.pallas_call(functools.partial(att_bwd_kernel, bq=bq, causal=causal), g...  82 us
    pallas_call x4, Pallas kernels, att_fwd(): pl.pallas_call(functools.partial(att_fwd_kernel, bq=bq, causal=causal), g...  48 us
    dot_general x10, matrix products, nn(): return lax.dot_general(a, b, NN, preferred_element_type=f32)  47.8 us
    pallas_call x1, Pallas kernels, hidden_units(): pl.pallas_call(up_kernel, grid=(2 * per,), in_specs=[pl.BlockSpec((rows,...  27.7 us
    pallas_call x1, Pallas kernels, weight_grads(): pl.pallas_call(functools.partial(weight_grads_kernel, tiles=tiles), grid=...  26.2 us
    dot_general x6, matrix products, nt(): return lax.dot_general(a, b, NT, preferred_element_type=f32)  20.3 us
  transfers between devices with their start and end apart: 6, of which 2 were waited for; matrix products, arithmetic and copies ran while one was open for 17% of the time, Pallas kernels for 47%

profile of v5, /device:TPU:0, one launch (start us, length us, event | category | flops | bytes accessed | tf_op | source)
XLA Modules:
  0.0 639.2 jit_solution(3896167458978746578)
XLA Ops:
  7.3 115.4 %shard_map.228 = (bf16[2,4,2,2,64,4096]{5,4,3,2,1,0:T(8,128)(2,1)}, bf16[2,512,1024]{2,1,0:T(8,128)(2,1)}, bf16[2,512,1024]{2,1,0:T(8,128)(2,1)}) custom-call(bf16[3,64,512]{2,1,0:T(8,128)(2,1)} %bitcast.198, bf16[64,512]{1,0:T(8,128)(2,1)} %bitcast.201, bf16[3,64,512]{2,1,0:T(8,128)(2,1)} %bitcast.199, bf16[64,512]{1,0:T(8,128)(2,1)} %bitcast.202, ...), custom_call_target="tpu_custom_call" | custom-call | bytes 167772160 | tf_op jit(solution)/shard_map/pallas_call | solution.py:647
  125.1 2.3 collective-permute-done
  127.6 7.8 %multiply_convert_fusion.1.q_ref.k_ref.v_ref = bf16[1024,1536]{1,0:T(8,128)(2,1)} fusion(bf16[1024,1024]{1,0:T(8,128)(2,1)} %bitcast.184, f32[1536]{0:T(1024)S(1)} %copy-done.53, f32[1536]{0:T(1024)S(1)} %get-tuple-element.180, bf16[2,1024,4096]{2,1,0:T(8,128)(2,1)} %bitcast.153), kind=kOutput, calls=%fused_computation.1 | convolution fusion | flops 3225944064 | bytes 8400896 | tf_op jit(solution)/shard_map/dot_general | solution.py:1152
  135.3 9.7 %shard_map.229 = (bf16[1024,512]{1,0:T(8,128)(2,1)}, f32[4,2,1024]{2,1,0:T(2,128)}) custom-call(bf16[1024,1536]{1,0:T(8,128)(2,1)} %multiply_convert_fusion.1.q_ref.k_ref.v_ref, bf16[1024,1536]{1,0:T(8,128)(2,1)} %multiply_convert_fusion.1.q_ref.k_ref.v_ref, bf16[1024,1536]{1,0:T(8,128)(2,1)} %multiply_convert_fusion.1.q_ref.k_ref.v_ref), custom_call_target="tpu_custom_call" | custom-call | tf_op jit(solution)/shard_map/pallas_call | solution.py:448
  145.0 6.7 %multiply_convert_fusion.q_ref.k_ref.v_ref = bf16[1024,1536]{1,0:T(8,128)(2,1)} fusion(bf16[1024,1024]{1,0:T(8,128)(2,1)S(1)} %bitcast.186, f32[1536]{0:T(1024)S(1)} %get-tuple-element.179, bf16[2,1024,4096]{2,1,0:T(8,128)(2,1)} %bitcast.154, f32[1536]{0:T(1024)S(1)} %copy-done.53), kind=kOutput, calls=%fused_computation | convolution fusion | flops 3225944064 | bytes 8400896 | tf_op jit(solution)/shard_map/dot_general | solution.py:1152
  151.7 9.4 %shard_map.230 = (bf16[1024,512]{1,0:T(8,128)(2,1)}, f32[4,2,1024]{2,1,0:T(2,128)}) custom-call(bf16[1024,1536]{1,0:T(8,128)(2,1)} %multiply_convert_fusion.q_ref.k_ref.v_ref, bf16[1024,1536]{1,0:T(8,128)(2,1)} %multiply_convert_fusion.q_ref.k_ref.v_ref, bf16[1024,1536]{1,0:T(8,128)(2,1)} %multiply_convert_fusion.q_ref.k_ref.v_ref), custom_call_target="tpu_custom_call" | custom-call | tf_op jit(solution)/shard_map/pallas_call | solution.py:448
  161.8 2.7 fusion.28
  164.5 2.9 fusion.51
  168.8 4.4 multiply_convert_fusion.2.q_ref
  173.1 5.3 add_convert_fusion.k_ref.v_ref
  178.4 14.6 %shard_map.232 = (bf16[1024,512]{1,0:T(8,128)(2,1)}, f32[4,2,1024]{2,1,0:T(2,128)}) custom-call(bf16[1024,512]{1,0:T(8,128)(2,1)} %multiply_convert_fusion.2.q_ref, bf16[1024,1024]{1,0:T(8,128)(2,1)} %add_convert_fusion.k_ref.v_ref, bf16[1024,1024]{1,0:T(8,128)(2,1)} %add_convert_fusion.k_ref.v_ref), custom_call_target="tpu_custom_call" | custom-call | tf_op jit(solution)/shard_map/pallas_call | solution.py:448
  193.0 3.6 multiply_convert_fusion.3.q_ref
  196.6 5.3 add_convert_fusion.1.k_ref.v_ref
  201.9 14.2 %shard_map.231 = (bf16[1024,512]{1,0:T(8,128)(2,1)}, f32[4,2,1024]{2,1,0:T(2,128)}) custom-call(bf16[1024,512]{1,0:T(8,128)(2,1)} %multiply_convert_fusion.3.q_ref, bf16[1024,1024]{1,0:T(8,128)(2,1)} %add_convert_fusion.1.k_ref.v_ref, bf16[1024,1024]{1,0:T(8,128)(2,1)} %add_convert_fusion.1.k_ref.v_ref), custom_call_target="tpu_custom_call" | custom-call | tf_op jit(solution)/shard_map/pallas_call | solution.py:448
  216.1 3.1 fusion.20
  219.2 4.7 fusion.52
  224.0 12.1 %all-gather.2.cloned.1.call-done = bf16[2048,4096]{1,0:T(8,128)(2,1)} async-done(((bf16[64,4096]{1,0:T(8,128)(2,1)}), bf16[2048,4096]{1,0:T(8,128)(2,1)}) %all-gather.2.cloned.1.call-update) | async-done | bytes 16777232 | tf_op jit(solution)/shard_map/all_gather | solution.py:1227
  236.3 1.3 collective-permute-start.1
  238.8 4.8 fusion.45
  243.7 27.7 %shard_map.233 = (bf16[1024,4096]{1,0:T(8,128)(2,1)}, bf16[1024,4096]{1,0:T(8,128)(2,1)}) custom-call(bf16[1024,1024]{1,0:T(8,128)(2,1)} %get-tuple-element.143.x_ref.a_ref, bf16[2,1024,4096]{2,1,0:T(8,128)(2,1)} %bitcast.179, f32[1,4096]{1,0:T(1,128)} %bitcast.204), custom_call_target="tpu_custom_call" | custom-call | tf_op jit(solution)/shard_map/pallas_call | solution.py:903
  271.4 2.3 maximum_select_fusion.cot_ref
  273.7 19.2 %shard_map.234 = (bf16[1024,1024]{1,0:T(8,128)(2,1)}, f32[1024,1024]{1,0:T(8,128)}, bf16[1024,1024]{1,0:T(8,128)(2,1)}, f32[8,1024]{1,0:T(8,128)}) custom-call(bf16[1024,4096]{1,0:T(8,128)(2,1)} %get-tuple-element.86.act_ref.db_ref, bf16[2,1024,4096]{2,1,0:T(8,128)(2,1)} %bitcast.180, f32[1024,1024]{1,0:T(8,128)} %get-tuple-element.144.h_ref, ...), custom_call_target="tpu_custom_call" | custom-call | tf_op jit(solution)/shard_map/pallas_call | solution.py:979
  292.9 15.0 %shard_map.235 = (bf16[1024,4096]{1,0:T(8,128)(2,1)}, f32[1,4096]{1,0:T(1,128)}) custom-call(bf16[1024,1024]{1,0:T(8,128)(2,1)} %get-tuple-element.89.e_ref.b_ref, bf16[2,1024,4096]{2,1,0:T(8,128)(2,1)} %bitcast.181, bf16[1024,4096]{1,0:T(8,128)(2,1)} %get-tuple-element.90.slope_ref), custom_call_target="tpu_custom_call" | custom-call | tf_op jit(solution)/shard_map/pallas_call | solution.py:933
  307.9 26.2 %shard_map.236 = bf16[2,1024,4096]{2,1,0:T(8,128)(2,1)} custom-call(bf16[1024,1024]{1,0:T(8,128)(2,1)} %get-tuple-element.143.x_ref.a_ref, bf16[1024,1024]{1,0:T(8,128)(2,1)} %get-tuple-element.89.e_ref.b_ref, bf16[1024,4096]{1,0:T(8,128)(2,1)} %get-tuple-element.92.da_ref.du_ref, bf16[1024,4096]{1,0:T(8,128)(2,1)} %get-tuple-element.86.act_ref.db_ref), custom_call_target="tpu_custom_call" | custom-call | tf_op jit(solution)/shard_map/pallas_call | solution.py:1138
  334.1 1.0 copy.34.inv_ref
  335.2 17.9 %shard_map.237 = (f32[1024,1024]{1,0:T(8,128)}, bf16[1024,1024]{1,0:T(8,128)(2,1)}, f32[8,1024]{1,0:T(8,128)}) custom-call(bf16[1024,4096]{1,0:T(8,128)(2,1)} %get-tuple-element.92.da_ref.du_ref, bf16[2,1024,4096]{2,1,0:T(8,128)(2,1)} %bitcast.182, f32[1024,1024]{1,0:T(8,128)} %get-tuple-element.93.dr3_ref, f32[1024,1024]{1,0:T(8,128)} %get-tuple-element.145.n_ref, ...), custom_call_target="tpu_custom_call" | custom-call | tf_op jit(solution)/shard_map/pallas_call | solution.py:1014
  353.1 4.1 convolution_convert_fusion.9.do_ref
  357.2 24.3 %shard_map.239 = (bf16[1024,512]{1,0:T(8,128)(2,1)}, bf16[1024,512]{1,0:T(8,128)(2,1)}, bf16[1024,512]{1,0:T(8,128)(2,1)}, f32[1,512]{1,0:T(1,128)}, f32[1,512]{1,0:T(1,128)}) custom-call(bf16[1024,512]{1,0:T(8,128)(2,1)} %multiply_convert_fusion.2.q_ref, bf16[1024,1024]{1,0:T(8,128)(2,1)} %add_convert_fusion.k_ref.v_ref, ...), custom_call_target="tpu_custom_call" | custom-call | tf_op jit(solution)/shard_map/pallas_call | solution.py:504
  381.5 3.5 convolution_convert_fusion.11.do_ref
  385.0 23.8 %shard_map.238 = (bf16[1024,512]{1,0:T(8,128)(2,1)}, bf16[1024,512]{1,0:T(8,128)(2,1)}, bf16[1024,512]{1,0:T(8,128)(2,1)}, f32[1,512]{1,0:T(1,128)}, f32[1,512]{1,0:T(1,128)}) custom-call(bf16[1024,512]{1,0:T(8,128)(2,1)} %multiply_convert_fusion.3.q_ref, bf16[1024,1024]{1,0:T(8,128)(2,1)} %add_convert_fusion.1.k_ref.v_ref, ...), custom_call_target="tpu_custom_call" | custom-call | tf_op jit(solution)/shard_map/pallas_call | solution.py:504
  408.8 3.0 fusion.22
  411.8 1.2 copy-done.24
  413.1 3.9 multiply_reduce_fusion
  417.0 1.4 fusion.44
  418.8 1.9 copy-done.29
  420.7 1.6 constant_dynamic-slice_fusion.3
  422.3 1.1 collective-permute-start.2
  423.4 7.4 %shard_map.240.refs_1_ = bf16[1024,1024]{1,0:T(8,128)(2,1)S(1)} custom-call(bf16[1024,512]{1,0:T(8,128)(2,1)S(1)} %copy-done.11, bf16[1024,512]{1,0:T(8,128)(2,1)S(1)} %copy-done.8, bf16[1024,512]{1,0:T(8,128)(2,1)S(1)} %copy-done.13, bf16[1024,512]{1,0:T(8,128)(2,1)S(1)} %copy-done.9, bf16[2,1024,4096]{2,1,0:T(8,128)(2,1)} %bitcast.167, ...), custom_call_target="tpu_custom_call" | custom-call | tf_op jit(solution)/shard_map/pallas_call | solution.py:1054
  430.9 1.6 constant_dynamic-slice_fusion.1
  432.5 0.9 collective-permute-start.3
  433.4 3.6 convolution_convert_fusion.do_ref
  437.0 16.9 %shard_map.242 = (bf16[1024,512]{1,0:T(8,128)(2,1)}, bf16[1024,512]{1,0:T(8,128)(2,1)}, bf16[1024,512]{1,0:T(8,128)(2,1)}, f32[1,512]{1,0:T(1,128)}, f32[1,512]{1,0:T(1,128)}) custom-call(bf16[1024,1536]{1,0:T(8,128)(2,1)} %multiply_convert_fusion.q_ref.k_ref.v_ref, bf16[1024,1536]{1,0:T(8,128)(2,1)} %multiply_convert_fusion.q_ref.k_ref.v_ref, ...), custom_call_target="tpu_custom_call" | custom-call | tf_op jit(solution)/shard_map/pallas_call | solution.py:504
  454.6 0.9 fusion.47
  455.5 0.9 fusion.46
  456.4 3.7 convolution_convert_fusion.1.do_ref
  460.2 2.2 convolution_convert_fusion.2
  462.4 2.3 convolution_convert_fusion.3
  464.7 2.3 convolution_convert_fusion.4
  467.0 2.3 convolution_convert_fusion.5
  469.3 2.3 convolution_convert_fusion.6
  471.7 2.3 convolution_convert_fusion.7
  474.0 2.3 convolution_convert_fusion.8
  476.3 2.3 convolution_convert_fusion.10
  478.6 3.2 maximum_select_fusion.1.refs_0_
  481.8 16.9 %shard_map.241 = (bf16[1024,512]{1,0:T(8,128)(2,1)}, bf16[1024,512]{1,0:T(8,128)(2,1)}, bf16[1024,512]{1,0:T(8,128)(2,1)}, f32[1,512]{1,0:T(1,128)}, f32[1,512]{1,0:T(1,128)}) custom-call(bf16[1024,1536]{1,0:T(8,128)(2,1)} %multiply_convert_fusion.1.q_ref.k_ref.v_ref, bf16[1024,1536]{1,0:T(8,128)(2,1)} %multiply_convert_fusion.1.q_ref.k_ref.v_ref, ...), custom_call_target="tpu_custom_call" | custom-call | tf_op jit(solution)/shard_map/pallas_call | solution.py:504
  499.6 1.2 copy-done.5
  500.8 1.2 copy-done.6
  502.1 1.2 copy-done.7
  503.3 10.6 %shard_map.243 = bf16[1024,1024]{1,0:T(8,128)(2,1)S(1)} custom-call(bf16[1024,512]{1,0:T(8,128)(2,1)S(1)} %copy-done.5, bf16[1024,512]{1,0:T(8,128)(2,1)S(1)} %copy-done.2, bf16[1024,512]{1,0:T(8,128)(2,1)S(1)} %copy-done.6, bf16[1024,512]{1,0:T(8,128)(2,1)S(1)} %copy-done.3, bf16[1024,512]{1,0:T(8,128)(2,1)S(1)} %copy-done.7, ...), custom_call_target="tpu_custom_call" | custom-call | tf_op jit(solution)/shard_map/pallas_call | solution.py:1054
  513.9 1.3 copy-done.1
  515.4 3.2 maximum_select_fusion.2.refs_18_
  518.6 107.5 %shard_map.244 = (f32[64,4096]{1,0:T(8,128)}, f32[136,128]{1,0:T(8,128)}, bf16[2,512,1024]{2,1,0:T(8,128)(2,1)}) custom-call(bf16[4,2,2,64,512]{4,3,2,1,0:T(8,128)(2,1)} %bitcast.196, bf16[4,2,2,64,512]{4,3,2,1,0:T(8,128)(2,1)} %bitcast.195, bf16[4,2,2,64,512]{4,3,2,1,0:T(8,128)(2,1)} %bitcast.194, bf16[4,2,2,64,512]{4,3,2,1,0:T(8,128)(2,1)} %bitcast.193, ...), custom_call_target="tpu_custom_call" | custom-call | bytes 167772160 | tf_op jit(solution)/shard_map/pallas_call | solution.py:819
  626.1 2.7 shard_map.245
  628.8 3.1 copy.54
  (157 shorter events, 7.9 us)
Async XLA Ops:
  7.2 120.4 %copy-start.53 = (f32[1536]{0:T(1024)S(1)}, f32[1536]{0:T(1024)}, u32[]{:S(2)}) copy-start(f32[1536]{0:T(1024)} %constant.40.clone.1) | copy-start | bytes 18436
  7.2 115.5 %copy-start.36 = (bf16[64,2048]{1,0:T(8,128)(2,1)S(1)}, bf16[64,2048]{1,0:T(8,128)(2,1)}, u32[]{:S(2)}) copy-start(bf16[64,2048]{1,0:T(8,128)(2,1)} %param.20) | copy-start | bytes 786436
  7.2 115.5 %copy-start.35 = (bf16[2048,64]{0,1:T(8,128)(2,1)S(1)}, bf16[2048,64]{0,1:T(8,128)(2,1)}, u32[]{:S(2)}) copy-start(bf16[2048,64]{0,1:T(8,128)(2,1)} %param.21) | copy-start | bytes 786436
  7.2 116.4 %copy-start.41 = (bf16[4,512]{1,0:T(4,128)(2,1)S(1)}, bf16[4,512]{1,0:T(4,128)(2,1)}, u32[]{:S(2)}) copy-start(bf16[4,512]{1,0:T(4,128)(2,1)} %param.22) | copy-start | bytes 12292
  7.2 116.4 %copy-start.42 = (bf16[2048]{0:T(1024)(128)(2,1)S(1)}, bf16[2048]{0:T(1024)(128)(2,1)}, u32[]{:S(2)}) copy-start(bf16[2048]{0:T(1024)(128)(2,1)} %param.23) | copy-start | bytes 12292
  7.2 117.1 %copy-start.39 = (bf16[3,1024]{1,0:T(4,128)(2,1)S(1)}, bf16[3,1024]{1,0:T(4,128)(2,1)}, u32[]{:S(2)}) copy-start(bf16[3,1024]{1,0:T(4,128)(2,1)} %param.24) | copy-start | bytes 18436
  7.2 117.1 %copy-start.38 = (bf16[6,1024]{1,0:T(8,128)(2,1)S(1)}, bf16[6,1024]{1,0:T(8,128)(2,1)}, u32[]{:S(2)}) copy-start(bf16[6,1024]{1,0:T(8,128)(2,1)} %param.25) | copy-start | bytes 36868
  7.3 228.8 %all-gather.2.cloned.1.call-start = ((), (), s32[]{:S(2)}) async-start(), calls=%async_computation.1 | async-start | bytes 17301504 | tf_op jit(solution)/shard_map/all_gather | solution.py:1227
  123.5 502.6 %reduce-scatter.2.cloned.1.call-start = ((), (), s32[]{:S(2)}) async-start(), calls=%async_computation.2 | async-start | bytes 17301504 | tf_op jit(solution)/shard_map/reduce_scatter | solution.py:1294
  123.7 3.7 collective-permute-start
  135.3 9.7 %copy-start.20 = (bf16[2,512,1024]{2,1,0:T(8,128)(2,1)S(1)}, bf16[2,512,1024]{2,1,0:T(8,128)(2,1)}, u32[]{:S(2)}) copy-start(bf16[2,512,1024]{2,1,0:T(8,128)(2,1)} %get-tuple-element.75) | copy-start | bytes 6291460
  151.7 10.1 %copy-start.25 = (bf16[1024,512]{1,0:T(8,128)(2,1)S(1)}, bf16[1024,512]{1,0:T(8,128)(2,1)}, u32[]{:S(2)}) copy-start(bf16[1024,512]{1,0:T(8,128)(2,1)} %get-tuple-element.78.o_ref.refs_16_) | copy-start | bytes 3145732
  161.8 2.7 copy-start.18
  161.8 2.7 copy-start.21
  167.4 51.8 %copy-start.15 = (f32[1024,1024]{1,0:T(8,128)}, f32[1024,1024]{1,0:T(8,128)S(1)}, u32[]{:S(2)}) copy-start(f32[1024,1024]{1,0:T(8,128)S(1)} %get-tuple-element.182) | copy-start | bytes 12582916
  168.8 24.2 %copy-start.26 = (bf16[1024,1024]{1,0:T(8,128)(2,1)}, bf16[1024,1024]{1,0:T(8,128)(2,1)S(1)}, u32[]{:S(2)}) copy-start(bf16[1024,1024]{1,0:T(8,128)(2,1)S(1)} %fusion) | copy-start | bytes 6291460
  168.8 4.4 copy-start.47
  193.0 3.6 copy-start.48
  216.1 3.1 copy-start.30
  219.2 16.9 %copy-start.28 = (bf16[2,512,1024]{2,1,0:T(8,128)(2,1)S(1)}, bf16[2,512,1024]{2,1,0:T(8,128)(2,1)}, u32[]{:S(2)}) copy-start(bf16[2,512,1024]{2,1,0:T(8,128)(2,1)} %param.15) | copy-start | bytes 6291460
  236.1 2.2 copy-start.17
  236.3 35.1 %collective-permute-start.1 = (bf16[512,1024]{1,0:T(8,128)(2,1)S(1)}, bf16[512,1024]{1,0:T(8,128)(2,1)S(1)}, u32[]{:S(2)}, u32[]{:S(2)}) collective-permute-start(bf16[512,1024]{1,0:T(8,128)(2,1)S(1)} %get-tuple-element.151), channel_id=1, source_target_pairs={{0,1},{1,0},{2,3},{3,2},{4,5},{5,4},{6,7},{7,6},{8,9},{9,8},{10,11... | collective-permute-start | bytes 3145736 | tf_op jit(solution)/shard_map/ppermute | solution.py:1177
  357.2 24.3 %copy-start.50 = (bf16[1024,1024]{1,0:T(8,128)(2,1)S(1)}, bf16[1024,1024]{1,0:T(8,128)(2,1)}, u32[]{:S(2)}) copy-start(bf16[1024,1024]{1,0:T(8,128)(2,1)} %get-tuple-element.94) | copy-start | bytes 6291460
  385.0 26.9 %copy-start.33 = (bf16[1024,512]{1,0:T(8,128)(2,1)S(1)}, bf16[1024,512]{1,0:T(8,128)(2,1)}, u32[]{:S(2)}) copy-start(bf16[1024,512]{1,0:T(8,128)(2,1)} %get-tuple-element.98) | copy-start | bytes 3145732
  408.8 3.1 copy-start.16
  408.8 4.3 copy-start.24
  418.4 2.3 copy-start.29
  418.4 5.0 copy-start.8
  418.4 4.9 copy-start.9
  418.5 4.9 copy-start.11
  418.5 4.9 copy-start.13
  418.8 37.6 %copy-start.19 = (bf16[1024,1024]{1,0:T(8,128)(2,1)}, bf16[1024,1024]{1,0:T(8,128)(2,1)S(1)}, u32[]{:S(2)}) copy-start(bf16[1024,1024]{1,0:T(8,128)(2,1)S(1)} %convert_element_type.102.refs_9_) | copy-start | bytes 6291460
  422.3 56.3 %collective-permute-start.2 = (bf16[1,512,1024]{2,1,0:T(8,128)(2,1)}, bf16[1,512,1024]{2,1,0:T(8,128)(2,1)}, u32[]{:S(2)}, u32[]{:S(2)}) collective-permute-start(bf16[1,512,1024]{2,1,0:T(8,128)(2,1)} %get-tuple-element.149), channel_id=1, source_target_pairs={{0,1},{1,0},{2,3},{3,2},{4,5},{5,4},{6,7},{7,6},{8,9},{9,8},{10,11... | collective-permute-start | bytes 3145736 | tf_op jit(solution)/shard_map/ppermute | solution.py:1177
  430.8 6.1 copy-start
  432.5 82.9 %collective-permute-start.3 = (bf16[1,512,1024]{2,1,0:T(8,128)(2,1)}, bf16[1,512,1024]{2,1,0:T(8,128)(2,1)}, u32[]{:S(2)}, u32[]{:S(2)}) collective-permute-start(bf16[1,512,1024]{2,1,0:T(8,128)(2,1)} %get-tuple-element.147), channel_id=1, source_target_pairs={{0,1},{1,0},{2,3},{3,2},{4,5},{5,4},{6,7},{7,6},{8,9},{9,8},{10,11... | collective-permute-start | bytes 3145736 | tf_op jit(solution)/shard_map/ppermute | solution.py:1177
  437.0 16.9 %copy-start.45 = (f32[1,512]{1,0:T(1,128)S(1)}, f32[1,512]{1,0:T(1,128)}, u32[]{:S(2)}) copy-start(f32[1,512]{1,0:T(1,128)} %get-tuple-element.118) | copy-start | bytes 6148
  437.0 16.9 %copy-start.46 = (f32[1,512]{1,0:T(1,128)S(1)}, f32[1,512]{1,0:T(1,128)}, u32[]{:S(2)}) copy-start(f32[1,512]{1,0:T(1,128)} %get-tuple-element.119) | copy-start | bytes 6148
  456.4 3.8 copy-start.31
  456.4 3.7 copy-start.51
  460.2 2.3 copy-start.32
  462.4 2.3 copy-start.10
  462.4 2.3 copy-start.49
  464.7 2.3 copy-start.14
  469.3 2.3 copy-start.12
  471.6 2.3 copy-start.27
  471.6 2.3 copy-start.34
  474.0 2.4 copy-start.52
  476.3 2.3 copy-start.23
  481.8 16.9 %copy-start.43 = (f32[1,512]{1,0:T(1,128)S(1)}, f32[1,512]{1,0:T(1,128)}, u32[]{:S(2)}) copy-start(f32[1,512]{1,0:T(1,128)} %get-tuple-element.114) | copy-start | bytes 6148
  481.8 17.0 %copy-start.44 = (f32[1,512]{1,0:T(1,128)S(1)}, f32[1,512]{1,0:T(1,128)}, u32[]{:S(2)}) copy-start(f32[1,512]{1,0:T(1,128)} %get-tuple-element.115) | copy-start | bytes 6148
  481.8 17.7 %copy-start.40 = (f32[1,4096]{1,0:T(1,128)S(1)}, f32[1,4096]{1,0:T(1,128)}, u32[]{:S(2)}) copy-start(f32[1,4096]{1,0:T(1,128)} %get-tuple-element.120) | copy-start | bytes 49156
  481.8 17.7 %copy-start.2 = (bf16[1024,512]{1,0:T(8,128)(2,1)S(1)}, bf16[1024,512]{1,0:T(8,128)(2,1)}, u32[]{:S(2)}) copy-start(bf16[1024,512]{1,0:T(8,128)(2,1)} %get-tuple-element.107.refs_1_.refs_11_) | copy-start | bytes 3145732
  481.8 17.7 %copy-start.3 = (bf16[1024,512]{1,0:T(8,128)(2,1)S(1)}, bf16[1024,512]{1,0:T(8,128)(2,1)}, u32[]{:S(2)}) copy-start(bf16[1024,512]{1,0:T(8,128)(2,1)} %get-tuple-element.109.refs_3_.refs_13_) | copy-start | bytes 3145732
  481.8 17.7 %copy-start.4 = (bf16[1024,512]{1,0:T(8,128)(2,1)S(1)}, bf16[1024,512]{1,0:T(8,128)(2,1)}, u32[]{:S(2)}) copy-start(bf16[1024,512]{1,0:T(8,128)(2,1)} %get-tuple-element.111.refs_5_.refs_15_) | copy-start | bytes 3145732
  499.6 1.2 copy-start.5
  500.8 1.2 copy-start.6
  502.1 1.2 copy-start.7
  503.3 12.1 %copy-start.22 = (bf16[1,512,1024]{2,1,0:T(8,128)(2,1)S(1)}, bf16[1,512,1024]{2,1,0:T(8,128)(2,1)}, u32[]{:S(2)}) copy-start(bf16[1,512,1024]{2,1,0:T(8,128)(2,1)} %get-tuple-element.146) | copy-start | bytes 3145732
  513.9 1.3 copy-start.1
  515.3 3.3 copy-start.37
Sparse Core Ops, SparseCore 0:
  123.7 112.3 all-gather.1
  334.3 182.9 reduce-scatter.1
